TPU v7x, 32 devices: a whole 2x2x4 slice. The times are simulated.
32 devices in a mesh: groups: 2 (over x), space: 16 (over z, y, core).
Axes of the slice: x: 2, y: 2, z: 4, core: 2. Of those that a mesh axis runs over, the one named last changes fastest.
Arguments:
- slowness: float32 [512, 4096], P(('groups', 'space')), parts along dimension 0, may hold values from 0.25 to 1
- ocean: int32 [512, 4096], P(('groups', 'space')), parts along dimension 0, may hold values 0 or 1
- start_times: float32 [8, 256, 4096], P('groups', 'space'), parts along dimension 0, may hold values from 0 to 96
- source_cells: int32 [8], P('groups'), parts along dimension 0, may hold values from 0 to 1048575
- gauge_cells: int32 [4096], P(('groups', 'space')), parts along dimension 0, may hold values from 0 to 65535
- gauge_owner: int32 [4096, 1], P(('groups', 'space')), parts along dimension 0, may hold values from 0 to 15; in each aligned block of 128 rows (0 to 127, 128 to 255, ...) at most 16 rows name the same one
Outputs:
- arrival: float32 [512, 4096], P(('groups', 'space')), parts along dimension 0
- gauge_arrivals: float32 [32, 4, 256], P(('groups', 'space')), parts along dimension 0
There are 2 independent parts, one for each index of `groups`. A program takes and returns all parts, laid end to end along the dimension named above; each array names one. Nothing has to cross between parts.
Inputs may be any that keep to these rules, and one draw needn't show every extreme that they name: `gauge_owner`: among the 128 gauges of one device block, no owner is named more than 16 times, a bound that some block reaches.
All inputs are finite; a program needn't handle non-finite values. No bound on the sum of `ocean` on one device may be relied on, other than what follows from the above.
Results may differ from a plain program's by a relative error of at most 0.00016.
Values sent between devices are 32-bit elements; how exact they have to be, the bound alone decides.
No kernel may reach another device: no remote copies, remote signals or barrier semaphores. Data moves between devices by JAX's collectives and lax.ppermute only.
A program may use at most 128 MiB of HBM per device.

v0:
```python
import jax
import jax.numpy as jnp
from jax import lax
from jax.sharding import PartitionSpec as P

SWEEPS = 8
BLOCKS = 3


far_value = 1000000.0
land_cost = 10000.0
clip_value = 48.0
root_two = 1.41421356
root_five = 2.23606798


def padded_2(shard, sides, width):
    for axis, dim in sides:
        size, length = (lax.axis_size(axis), shard.shape[dim])
        up = [(i, (i + 1) % size) for i in range(size - 1)]
        down = [(j, i) for i, j in up]
        last = lax.slice_in_dim(shard, length - width, length, axis=dim)
        leading = lax.slice_in_dim(shard, 0, width, axis=dim)
        before = lax.ppermute(last, axis, up)
        after = lax.ppermute(leading, axis, down)
        shard = jnp.concatenate([before, shard, after], axis=dim)
    return shard


def relax(padded, cost):
    height = padded.shape[1] - 4
    width = padded.shape[2] - 4

    def shifted(drow, dcol):
        return padded[:, 2 + drow : 2 + drow + height, 2 + dcol : 2 + dcol + width]

    near = jnp.minimum(
        jnp.minimum(shifted(0, 1), shifted(0, -1)), jnp.minimum(shifted(1, 0), shifted(-1, 0))
    )
    diag = jnp.minimum(
        jnp.minimum(shifted(1, 1), shifted(1, -1)), jnp.minimum(shifted(-1, 1), shifted(-1, -1))
    )
    knight = jnp.minimum(
        jnp.minimum(shifted(1, 2), shifted(1, -2)), jnp.minimum(shifted(-1, 2), shifted(-1, -2))
    )
    knight = jnp.minimum(
        knight,
        jnp.minimum(
            jnp.minimum(shifted(2, 1), shifted(2, -1)), jnp.minimum(shifted(-2, 1), shifted(-2, -1))
        ),
    )
    best = jnp.minimum(near + cost, diag + root_two * cost)
    best = jnp.minimum(best, knight + root_five * cost)
    return jnp.minimum(shifted(0, 0), best)


def fence(field, first_row, total_rows):
    rows = first_row + jnp.arange(field.shape[1], dtype=jnp.int32)
    inside = (rows >= 0) & (rows < total_rows)
    return jnp.where(inside[None, :, None], field, jnp.float32(far_value))


def on_device(slowness, ocean, start_times, source_cells, gauge_cells, gauge_owner):
    index = lax.axis_index("space")
    count = lax.axis_size("space")
    rows_dev = slowness.shape[0]
    width = slowness.shape[1]
    sources = start_times.shape[0]
    total_rows = count * rows_dev
    first_row = index * rows_dev
    cost = jnp.where(ocean == 1, slowness, jnp.float32(land_cost))
    flat = first_row * width + jnp.arange(rows_dev * width, dtype=jnp.int32).reshape(
        rows_dev, width
    )
    times = jnp.where(flat[None] == source_cells[:, None, None], jnp.float32(0.0), start_times)

    def sweep(step, field):
        padded = padded_2(field, (("space", 1),), 2)
        padded = fence(padded, first_row - 2, total_rows)
        return relax(jnp.pad(padded, ((0, 0), (0, 0), (2, 2)), constant_values=far_value), cost)

    times = lax.fori_loop(0, BLOCKS * SWEEPS, sweep, times)
    each_arrival = jnp.minimum(times, jnp.float32(clip_value)) / clip_value
    arrival = jnp.min(each_arrival, axis=0)
    values = each_arrival.reshape(sources, -1)[:, gauge_cells]
    owners = gauge_owner[:, 0]
    capacity = max(2, 2 * gauge_cells.shape[0] // count)
    slots = jnp.arange(count * capacity, dtype=jnp.int32)
    onehot = (owners[:, None] == jnp.arange(count, dtype=jnp.int32)[None, :]).astype(jnp.int32)
    ranks = jnp.sum((jnp.cumsum(onehot, axis=0) - 1) * onehot, axis=1)
    target = owners * capacity + ranks
    placing = (target[:, None] == slots[None, :]).astype(jnp.float32)
    placed = jnp.dot(
        values, placing, precision=lax.Precision.HIGHEST, preferred_element_type=jnp.float32
    )
    received = lax.all_to_all(
        placed.reshape(sources, count, capacity), "space", split_axis=1, concat_axis=1, tiled=True
    )
    result = received.reshape(1, sources, count * capacity)
    return (arrival, result)


def solution(mesh):
    return jax.shard_map(
        on_device,
        mesh=mesh,
        in_specs=(
            P(("groups", "space"), None),
            P(("groups", "space"), None),
            P("groups", "space", None),
            P("groups"),
            P(("groups", "space")),
            P(("groups", "space"), None),
        ),
        out_specs=(P(("groups", "space"), None), P(("groups", "space"), None, None)),
        check_vma=False,
    )
```

profile of v0, /device:TPU:0, one launch (start us, length us, event | category | flops | bytes accessed | tf_op | source)
XLA Modules:
  0.0 370.7 jit_solution(18091390072638009376)
XLA Ops:
  2.8 320.2 %while.12 = (s32[]{:T(128)}, f32[4,16,4096]{2,1,0:T(8,128)S(1)}, s32[]{:T(128)}, f32[16,4096]{1,0:T(8,128)S(1)}, s32[]{:T(128)}) while((s32[]{:T(128)}, f32[4,16,4096]{2,1,0:T(8,128)S(1)}, s32[]{:T(128)}, f32[16,4096]{1,0:T(8,128)S(1)}, s32[]{:T(128)}) %tuple.36), condition=%wide.region_1.2_spmd, body=%wide.region_0.1_spmd.sunk | while | flops 6094930 | bytes 11534521 | solution.py:82
  8.6 4.0 %fusion.21 = f32[4,16,4096]{2,1,0:T(8,128)S(1)} fusion(f32[4,20,4096]{2,1,0:T(8,128)S(1)} %maximum_select_fusion.2, f32[16,4096]{1,0:T(8,128)S(1)} %get-tuple-element.99, f32[16,4096]{1,0:T(8,128)S(1)} %get-tuple-element.100, f32[16,4096]{1,0:T(8,128)S(1)} %get-tuple-element.114), kind=kLoop, calls=%fused_computation.7.clone.1 | loop fusion | flops 4980736 | bytes 6553600 | tf_op jit(solution)/shard_map/while/body/eval_jaxpr/min | solution.py:54
  13.9 6.5 %collective-permute-start.1 = (f32[4,2,4096]{2,1,0:T(2,128)S(1)}, f32[4,2,4096]{2,1,0:T(2,128)S(1)}, u32[]{:S(2)}, u32[]{:S(2)}) collective-permute-start(f32[4,2,4096]{2,1,0:T(2,128)S(1)} %get-tuple-element.98), channel_id=1, source_target_pairs={{0,1},{1,2},{2,3},{3,4},{4,5},{5,6},{6,7},{7,8},{8,9},{9,10},{10,1... | collective-permute-start | bytes 393224 | tf_op jit(solution)/shard_map/while/body/eval_jaxpr/ppermute | solution.py:24
  21.7 4.0 %fusion.21 = f32[4,16,4096]{2,1,0:T(8,128)S(1)} fusion(f32[4,20,4096]{2,1,0:T(8,128)S(1)} %maximum_select_fusion.2, f32[16,4096]{1,0:T(8,128)S(1)} %get-tuple-element.99, f32[16,4096]{1,0:T(8,128)S(1)} %get-tuple-element.100, f32[16,4096]{1,0:T(8,128)S(1)} %get-tuple-element.114), kind=kLoop, calls=%fused_computation.7.clone.1 | loop fusion | flops 4980736 | bytes 6553600 | tf_op jit(solution)/shard_map/while/body/eval_jaxpr/min | solution.py:54
  27.1 6.8 %collective-permute-start.1 = (f32[4,2,4096]{2,1,0:T(2,128)S(1)}, f32[4,2,4096]{2,1,0:T(2,128)S(1)}, u32[]{:S(2)}, u32[]{:S(2)}) collective-permute-start(f32[4,2,4096]{2,1,0:T(2,128)S(1)} %get-tuple-element.98), channel_id=1, source_target_pairs={{0,1},{1,2},{2,3},{3,4},{4,5},{5,6},{6,7},{7,8},{8,9},{9,10},{10,1... | collective-permute-start | bytes 393224 | tf_op jit(solution)/shard_map/while/body/eval_jaxpr/ppermute | solution.py:24
  35.2 4.0 %fusion.21 = f32[4,16,4096]{2,1,0:T(8,128)S(1)} fusion(f32[4,20,4096]{2,1,0:T(8,128)S(1)} %maximum_select_fusion.2, f32[16,4096]{1,0:T(8,128)S(1)} %get-tuple-element.99, f32[16,4096]{1,0:T(8,128)S(1)} %get-tuple-element.100, f32[16,4096]{1,0:T(8,128)S(1)} %get-tuple-element.114), kind=kLoop, calls=%fused_computation.7.clone.1 | loop fusion | flops 4980736 | bytes 6553600 | tf_op jit(solution)/shard_map/while/body/eval_jaxpr/min | solution.py:54
  40.6 6.8 %collective-permute-start.1 = (f32[4,2,4096]{2,1,0:T(2,128)S(1)}, f32[4,2,4096]{2,1,0:T(2,128)S(1)}, u32[]{:S(2)}, u32[]{:S(2)}) collective-permute-start(f32[4,2,4096]{2,1,0:T(2,128)S(1)} %get-tuple-element.98), channel_id=1, source_target_pairs={{0,1},{1,2},{2,3},{3,4},{4,5},{5,6},{6,7},{7,8},{8,9},{9,10},{10,1... | collective-permute-start | bytes 393224 | tf_op jit(solution)/shard_map/while/body/eval_jaxpr/ppermute | solution.py:24
  48.7 4.0 %fusion.21 = f32[4,16,4096]{2,1,0:T(8,128)S(1)} fusion(f32[4,20,4096]{2,1,0:T(8,128)S(1)} %maximum_select_fusion.2, f32[16,4096]{1,0:T(8,128)S(1)} %get-tuple-element.99, f32[16,4096]{1,0:T(8,128)S(1)} %get-tuple-element.100, f32[16,4096]{1,0:T(8,128)S(1)} %get-tuple-element.114), kind=kLoop, calls=%fused_computation.7.clone.1 | loop fusion | flops 4980736 | bytes 6553600 | tf_op jit(solution)/shard_map/while/body/eval_jaxpr/min | solution.py:54
  54.1 6.8 %collective-permute-start.1 = (f32[4,2,4096]{2,1,0:T(2,128)S(1)}, f32[4,2,4096]{2,1,0:T(2,128)S(1)}, u32[]{:S(2)}, u32[]{:S(2)}) collective-permute-start(f32[4,2,4096]{2,1,0:T(2,128)S(1)} %get-tuple-element.98), channel_id=1, source_target_pairs={{0,1},{1,2},{2,3},{3,4},{4,5},{5,6},{6,7},{7,8},{8,9},{9,10},{10,1... | collective-permute-start | bytes 393224 | tf_op jit(solution)/shard_map/while/body/eval_jaxpr/ppermute | solution.py:24
  62.2 4.0 %fusion.21 = f32[4,16,4096]{2,1,0:T(8,128)S(1)} fusion(f32[4,20,4096]{2,1,0:T(8,128)S(1)} %maximum_select_fusion.2, f32[16,4096]{1,0:T(8,128)S(1)} %get-tuple-element.99, f32[16,4096]{1,0:T(8,128)S(1)} %get-tuple-element.100, f32[16,4096]{1,0:T(8,128)S(1)} %get-tuple-element.114), kind=kLoop, calls=%fused_computation.7.clone.1 | loop fusion | flops 4980736 | bytes 6553600 | tf_op jit(solution)/shard_map/while/body/eval_jaxpr/min | solution.py:54
  67.6 6.8 %collective-permute-start.1 = (f32[4,2,4096]{2,1,0:T(2,128)S(1)}, f32[4,2,4096]{2,1,0:T(2,128)S(1)}, u32[]{:S(2)}, u32[]{:S(2)}) collective-permute-start(f32[4,2,4096]{2,1,0:T(2,128)S(1)} %get-tuple-element.98), channel_id=1, source_target_pairs={{0,1},{1,2},{2,3},{3,4},{4,5},{5,6},{6,7},{7,8},{8,9},{9,10},{10,1... | collective-permute-start | bytes 393224 | tf_op jit(solution)/shard_map/while/body/eval_jaxpr/ppermute | solution.py:24
  81.1 6.8 %collective-permute-start.1 = (f32[4,2,4096]{2,1,0:T(2,128)S(1)}, f32[4,2,4096]{2,1,0:T(2,128)S(1)}, u32[]{:S(2)}, u32[]{:S(2)}) collective-permute-start(f32[4,2,4096]{2,1,0:T(2,128)S(1)} %get-tuple-element.98), channel_id=1, source_target_pairs={{0,1},{1,2},{2,3},{3,4},{4,5},{5,6},{6,7},{7,8},{8,9},{9,10},{10,1... | collective-permute-start | bytes 393224 | tf_op jit(solution)/shard_map/while/body/eval_jaxpr/ppermute | solution.py:24
  94.6 6.8 %collective-permute-start.1 = (f32[4,2,4096]{2,1,0:T(2,128)S(1)}, f32[4,2,4096]{2,1,0:T(2,128)S(1)}, u32[]{:S(2)}, u32[]{:S(2)}) collective-permute-start(f32[4,2,4096]{2,1,0:T(2,128)S(1)} %get-tuple-element.98), channel_id=1, source_target_pairs={{0,1},{1,2},{2,3},{3,4},{4,5},{5,6},{6,7},{7,8},{8,9},{9,10},{10,1... | collective-permute-start | bytes 393224 | tf_op jit(solution)/shard_map/while/body/eval_jaxpr/ppermute | solution.py:24
  108.2 6.8 %collective-permute-start.1 = (f32[4,2,4096]{2,1,0:T(2,128)S(1)}, f32[4,2,4096]{2,1,0:T(2,128)S(1)}, u32[]{:S(2)}, u32[]{:S(2)}) collective-permute-start(f32[4,2,4096]{2,1,0:T(2,128)S(1)} %get-tuple-element.98), channel_id=1, source_target_pairs={{0,1},{1,2},{2,3},{3,4},{4,5},{5,6},{6,7},{7,8},{8,9},{9,10},{10,1... | collective-permute-start | bytes 393224 | tf_op jit(solution)/shard_map/while/body/eval_jaxpr/ppermute | solution.py:24
  121.7 6.8 %collective-permute-start.1 = (f32[4,2,4096]{2,1,0:T(2,128)S(1)}, f32[4,2,4096]{2,1,0:T(2,128)S(1)}, u32[]{:S(2)}, u32[]{:S(2)}) collective-permute-start(f32[4,2,4096]{2,1,0:T(2,128)S(1)} %get-tuple-element.98), channel_id=1, source_target_pairs={{0,1},{1,2},{2,3},{3,4},{4,5},{5,6},{6,7},{7,8},{8,9},{9,10},{10,1... | collective-permute-start | bytes 393224 | tf_op jit(solution)/shard_map/while/body/eval_jaxpr/ppermute | solution.py:24
  135.2 6.8 %collective-permute-start.1 = (f32[4,2,4096]{2,1,0:T(2,128)S(1)}, f32[4,2,4096]{2,1,0:T(2,128)S(1)}, u32[]{:S(2)}, u32[]{:S(2)}) collective-permute-start(f32[4,2,4096]{2,1,0:T(2,128)S(1)} %get-tuple-element.98), channel_id=1, source_target_pairs={{0,1},{1,2},{2,3},{3,4},{4,5},{5,6},{6,7},{7,8},{8,9},{9,10},{10,1... | collective-permute-start | bytes 393224 | tf_op jit(solution)/shard_map/while/body/eval_jaxpr/ppermute | solution.py:24
  148.7 6.8 %collective-permute-start.1 = (f32[4,2,4096]{2,1,0:T(2,128)S(1)}, f32[4,2,4096]{2,1,0:T(2,128)S(1)}, u32[]{:S(2)}, u32[]{:S(2)}) collective-permute-start(f32[4,2,4096]{2,1,0:T(2,128)S(1)} %get-tuple-element.98), channel_id=1, source_target_pairs={{0,1},{1,2},{2,3},{3,4},{4,5},{5,6},{6,7},{7,8},{8,9},{9,10},{10,1... | collective-permute-start | bytes 393224 | tf_op jit(solution)/shard_map/while/body/eval_jaxpr/ppermute | solution.py:24
  162.2 6.8 %collective-permute-start.1 = (f32[4,2,4096]{2,1,0:T(2,128)S(1)}, f32[4,2,4096]{2,1,0:T(2,128)S(1)}, u32[]{:S(2)}, u32[]{:S(2)}) collective-permute-start(f32[4,2,4096]{2,1,0:T(2,128)S(1)} %get-tuple-element.98), channel_id=1, source_target_pairs={{0,1},{1,2},{2,3},{3,4},{4,5},{5,6},{6,7},{7,8},{8,9},{9,10},{10,1... | collective-permute-start | bytes 393224 | tf_op jit(solution)/shard_map/while/body/eval_jaxpr/ppermute | solution.py:24
  175.7 6.8 %collective-permute-start.1 = (f32[4,2,4096]{2,1,0:T(2,128)S(1)}, f32[4,2,4096]{2,1,0:T(2,128)S(1)}, u32[]{:S(2)}, u32[]{:S(2)}) collective-permute-start(f32[4,2,4096]{2,1,0:T(2,128)S(1)} %get-tuple-element.98), channel_id=1, source_target_pairs={{0,1},{1,2},{2,3},{3,4},{4,5},{5,6},{6,7},{7,8},{8,9},{9,10},{10,1... | collective-permute-start | bytes 393224 | tf_op jit(solution)/shard_map/while/body/eval_jaxpr/ppermute | solution.py:24
  189.3 6.8 %collective-permute-start.1 = (f32[4,2,4096]{2,1,0:T(2,128)S(1)}, f32[4,2,4096]{2,1,0:T(2,128)S(1)}, u32[]{:S(2)}, u32[]{:S(2)}) collective-permute-start(f32[4,2,4096]{2,1,0:T(2,128)S(1)} %get-tuple-element.98), channel_id=1, source_target_pairs={{0,1},{1,2},{2,3},{3,4},{4,5},{5,6},{6,7},{7,8},{8,9},{9,10},{10,1... | collective-permute-start | bytes 393224 | tf_op jit(solution)/shard_map/while/body/eval_jaxpr/ppermute | solution.py:24
  202.8 6.8 %collective-permute-start.1 = (f32[4,2,4096]{2,1,0:T(2,128)S(1)}, f32[4,2,4096]{2,1,0:T(2,128)S(1)}, u32[]{:S(2)}, u32[]{:S(2)}) collective-permute-start(f32[4,2,4096]{2,1,0:T(2,128)S(1)} %get-tuple-element.98), channel_id=1, source_target_pairs={{0,1},{1,2},{2,3},{3,4},{4,5},{5,6},{6,7},{7,8},{8,9},{9,10},{10,1... | collective-permute-start | bytes 393224 | tf_op jit(solution)/shard_map/while/body/eval_jaxpr/ppermute | solution.py:24
  216.3 6.8 %collective-permute-start.1 = (f32[4,2,4096]{2,1,0:T(2,128)S(1)}, f32[4,2,4096]{2,1,0:T(2,128)S(1)}, u32[]{:S(2)}, u32[]{:S(2)}) collective-permute-start(f32[4,2,4096]{2,1,0:T(2,128)S(1)} %get-tuple-element.98), channel_id=1, source_target_pairs={{0,1},{1,2},{2,3},{3,4},{4,5},{5,6},{6,7},{7,8},{8,9},{9,10},{10,1... | collective-permute-start | bytes 393224 | tf_op jit(solution)/shard_map/while/body/eval_jaxpr/ppermute | solution.py:24
  229.8 6.8 %collective-permute-start.1 = (f32[4,2,4096]{2,1,0:T(2,128)S(1)}, f32[4,2,4096]{2,1,0:T(2,128)S(1)}, u32[]{:S(2)}, u32[]{:S(2)}) collective-permute-start(f32[4,2,4096]{2,1,0:T(2,128)S(1)} %get-tuple-element.98), channel_id=1, source_target_pairs={{0,1},{1,2},{2,3},{3,4},{4,5},{5,6},{6,7},{7,8},{8,9},{9,10},{10,1... | collective-permute-start | bytes 393224 | tf_op jit(solution)/shard_map/while/body/eval_jaxpr/ppermute | solution.py:24
  243.3 6.8 %collective-permute-start.1 = (f32[4,2,4096]{2,1,0:T(2,128)S(1)}, f32[4,2,4096]{2,1,0:T(2,128)S(1)}, u32[]{:S(2)}, u32[]{:S(2)}) collective-permute-start(f32[4,2,4096]{2,1,0:T(2,128)S(1)} %get-tuple-element.98), channel_id=1, source_target_pairs={{0,1},{1,2},{2,3},{3,4},{4,5},{5,6},{6,7},{7,8},{8,9},{9,10},{10,1... | collective-permute-start | bytes 393224 | tf_op jit(solution)/shard_map/while/body/eval_jaxpr/ppermute | solution.py:24
  256.8 6.8 %collective-permute-start.1 = (f32[4,2,4096]{2,1,0:T(2,128)S(1)}, f32[4,2,4096]{2,1,0:T(2,128)S(1)}, u32[]{:S(2)}, u32[]{:S(2)}) collective-permute-start(f32[4,2,4096]{2,1,0:T(2,128)S(1)} %get-tuple-element.98), channel_id=1, source_target_pairs={{0,1},{1,2},{2,3},{3,4},{4,5},{5,6},{6,7},{7,8},{8,9},{9,10},{10,1... | collective-permute-start | bytes 393224 | tf_op jit(solution)/shard_map/while/body/eval_jaxpr/ppermute | solution.py:24
  270.3 6.8 %collective-permute-start.1 = (f32[4,2,4096]{2,1,0:T(2,128)S(1)}, f32[4,2,4096]{2,1,0:T(2,128)S(1)}, u32[]{:S(2)}, u32[]{:S(2)}) collective-permute-start(f32[4,2,4096]{2,1,0:T(2,128)S(1)} %get-tuple-element.98), channel_id=1, source_target_pairs={{0,1},{1,2},{2,3},{3,4},{4,5},{5,6},{6,7},{7,8},{8,9},{9,10},{10,1... | collective-permute-start | bytes 393224 | tf_op jit(solution)/shard_map/while/body/eval_jaxpr/ppermute | solution.py:24
  283.9 6.8 %collective-permute-start.1 = (f32[4,2,4096]{2,1,0:T(2,128)S(1)}, f32[4,2,4096]{2,1,0:T(2,128)S(1)}, u32[]{:S(2)}, u32[]{:S(2)}) collective-permute-start(f32[4,2,4096]{2,1,0:T(2,128)S(1)} %get-tuple-element.98), channel_id=1, source_target_pairs={{0,1},{1,2},{2,3},{3,4},{4,5},{5,6},{6,7},{7,8},{8,9},{9,10},{10,1... | collective-permute-start | bytes 393224 | tf_op jit(solution)/shard_map/while/body/eval_jaxpr/ppermute | solution.py:24
  297.4 6.8 %collective-permute-start.1 = (f32[4,2,4096]{2,1,0:T(2,128)S(1)}, f32[4,2,4096]{2,1,0:T(2,128)S(1)}, u32[]{:S(2)}, u32[]{:S(2)}) collective-permute-start(f32[4,2,4096]{2,1,0:T(2,128)S(1)} %get-tuple-element.98), channel_id=1, source_target_pairs={{0,1},{1,2},{2,3},{3,4},{4,5},{5,6},{6,7},{7,8},{8,9},{9,10},{10,1... | collective-permute-start | bytes 393224 | tf_op jit(solution)/shard_map/while/body/eval_jaxpr/ppermute | solution.py:24
  310.9 6.8 %collective-permute-start.1 = (f32[4,2,4096]{2,1,0:T(2,128)S(1)}, f32[4,2,4096]{2,1,0:T(2,128)S(1)}, u32[]{:S(2)}, u32[]{:S(2)}) collective-permute-start(f32[4,2,4096]{2,1,0:T(2,128)S(1)} %get-tuple-element.98), channel_id=1, source_target_pairs={{0,1},{1,2},{2,3},{3,4},{4,5},{5,6},{6,7},{7,8},{8,9},{9,10},{10,1... | collective-permute-start | bytes 393224 | tf_op jit(solution)/shard_map/while/body/eval_jaxpr/ppermute | solution.py:24
  323.8 16.2 %copy.11 = f32[4,16,4096]{0,2,1:T(8,128)} copy(f32[4,16,4096]{2,1,0:T(8,128)S(1)} %get-tuple-element.66) | data formatting | bytes 2097152 | tf_op jit(solution)/shard_map/div | solution.py:83
  340.5 11.2 %gather_fusion = f32[128,4]{1,0:T(8,128)S(1)} fusion(f32[4,65536]{0,1:T(8,128)} %bitcast.9, s32[1024]{0:T(1024)S(1)} %pad_clamp_fusion), kind=kCustom, calls=%fused_computation | custom fusion | bytes 4608 | tf_op jit(solution)/shard_map/gather | solution.py:85
  352.1 17.9 %all_to_all.5 = f32[4,16,16]{2,0,1:T(4,128)S(1)} all-to-all(f32[4,16,16]{2,0,1:T(4,128)S(1)} %copy.12), channel_id=1, replica_groups=mesh['groups'=2,'space'=16] {'space'}, dimensions={1} | all-to-all | bytes 8192 | tf_op jit(solution)/shard_map/all_to_all | solution.py:96
  (209 shorter events, 146.0 us)
Async XLA Ops:
  12.6 7.8 %collective-permute-start = (f32[4,2,4096]{2,1,0:T(2,128)S(1)}, f32[4,2,4096]{2,1,0:T(2,128)S(1)}, u32[]{:S(2)}, u32[]{:S(2)}) collective-permute-start(f32[4,2,4096]{2,1,0:T(2,128)S(1)} %get-tuple-element.97), channel_id=1, source_target_pairs={{1,0},{2,1},{3,2},{4,3},{5,4},{6,5},{7,6},{8,7},{9,8},{10,9},{11,1... | collective-permute-start | bytes 393224 | tf_op jit(solution)/shard_map/while/body/eval_jaxpr/ppermute | solution.py:25
  25.8 8.2 %collective-permute-start = (f32[4,2,4096]{2,1,0:T(2,128)S(1)}, f32[4,2,4096]{2,1,0:T(2,128)S(1)}, u32[]{:S(2)}, u32[]{:S(2)}) collective-permute-start(f32[4,2,4096]{2,1,0:T(2,128)S(1)} %get-tuple-element.97), channel_id=1, source_target_pairs={{1,0},{2,1},{3,2},{4,3},{5,4},{6,5},{7,6},{8,7},{9,8},{10,9},{11,1... | collective-permute-start | bytes 393224 | tf_op jit(solution)/shard_map/while/body/eval_jaxpr/ppermute | solution.py:25
  27.1 7.8 %collective-permute-start.1 = (f32[4,2,4096]{2,1,0:T(2,128)S(1)}, f32[4,2,4096]{2,1,0:T(2,128)S(1)}, u32[]{:S(2)}, u32[]{:S(2)}) collective-permute-start(f32[4,2,4096]{2,1,0:T(2,128)S(1)} %get-tuple-element.98), channel_id=1, source_target_pairs={{0,1},{1,2},{2,3},{3,4},{4,5},{5,6},{6,7},{7,8},{8,9},{9,10},{10,1... | collective-permute-start | bytes 393224 | tf_op jit(solution)/shard_map/while/body/eval_jaxpr/ppermute | solution.py:24
  39.3 8.2 %collective-permute-start = (f32[4,2,4096]{2,1,0:T(2,128)S(1)}, f32[4,2,4096]{2,1,0:T(2,128)S(1)}, u32[]{:S(2)}, u32[]{:S(2)}) collective-permute-start(f32[4,2,4096]{2,1,0:T(2,128)S(1)} %get-tuple-element.97), channel_id=1, source_target_pairs={{1,0},{2,1},{3,2},{4,3},{5,4},{6,5},{7,6},{8,7},{9,8},{10,9},{11,1... | collective-permute-start | bytes 393224 | tf_op jit(solution)/shard_map/while/body/eval_jaxpr/ppermute | solution.py:25
  40.6 7.8 %collective-permute-start.1 = (f32[4,2,4096]{2,1,0:T(2,128)S(1)}, f32[4,2,4096]{2,1,0:T(2,128)S(1)}, u32[]{:S(2)}, u32[]{:S(2)}) collective-permute-start(f32[4,2,4096]{2,1,0:T(2,128)S(1)} %get-tuple-element.98), channel_id=1, source_target_pairs={{0,1},{1,2},{2,3},{3,4},{4,5},{5,6},{6,7},{7,8},{8,9},{9,10},{10,1... | collective-permute-start | bytes 393224 | tf_op jit(solution)/shard_map/while/body/eval_jaxpr/ppermute | solution.py:24
  52.8 8.2 %collective-permute-start = (f32[4,2,4096]{2,1,0:T(2,128)S(1)}, f32[4,2,4096]{2,1,0:T(2,128)S(1)}, u32[]{:S(2)}, u32[]{:S(2)}) collective-permute-start(f32[4,2,4096]{2,1,0:T(2,128)S(1)} %get-tuple-element.97), channel_id=1, source_target_pairs={{1,0},{2,1},{3,2},{4,3},{5,4},{6,5},{7,6},{8,7},{9,8},{10,9},{11,1... | collective-permute-start | bytes 393224 | tf_op jit(solution)/shard_map/while/body/eval_jaxpr/ppermute | solution.py:25
  66.3 8.2 %collective-permute-start = (f32[4,2,4096]{2,1,0:T(2,128)S(1)}, f32[4,2,4096]{2,1,0:T(2,128)S(1)}, u32[]{:S(2)}, u32[]{:S(2)}) collective-permute-start(f32[4,2,4096]{2,1,0:T(2,128)S(1)} %get-tuple-element.97), channel_id=1, source_target_pairs={{1,0},{2,1},{3,2},{4,3},{5,4},{6,5},{7,6},{8,7},{9,8},{10,9},{11,1... | collective-permute-start | bytes 393224 | tf_op jit(solution)/shard_map/while/body/eval_jaxpr/ppermute | solution.py:25
  67.6 7.8 %collective-permute-start.1 = (f32[4,2,4096]{2,1,0:T(2,128)S(1)}, f32[4,2,4096]{2,1,0:T(2,128)S(1)}, u32[]{:S(2)}, u32[]{:S(2)}) collective-permute-start(f32[4,2,4096]{2,1,0:T(2,128)S(1)} %get-tuple-element.98), channel_id=1, source_target_pairs={{0,1},{1,2},{2,3},{3,4},{4,5},{5,6},{6,7},{7,8},{8,9},{9,10},{10,1... | collective-permute-start | bytes 393224 | tf_op jit(solution)/shard_map/while/body/eval_jaxpr/ppermute | solution.py:24
  79.8 8.2 %collective-permute-start = (f32[4,2,4096]{2,1,0:T(2,128)S(1)}, f32[4,2,4096]{2,1,0:T(2,128)S(1)}, u32[]{:S(2)}, u32[]{:S(2)}) collective-permute-start(f32[4,2,4096]{2,1,0:T(2,128)S(1)} %get-tuple-element.97), channel_id=1, source_target_pairs={{1,0},{2,1},{3,2},{4,3},{5,4},{6,5},{7,6},{8,7},{9,8},{10,9},{11,1... | collective-permute-start | bytes 393224 | tf_op jit(solution)/shard_map/while/body/eval_jaxpr/ppermute | solution.py:25
  81.1 7.8 %collective-permute-start.1 = (f32[4,2,4096]{2,1,0:T(2,128)S(1)}, f32[4,2,4096]{2,1,0:T(2,128)S(1)}, u32[]{:S(2)}, u32[]{:S(2)}) collective-permute-start(f32[4,2,4096]{2,1,0:T(2,128)S(1)} %get-tuple-element.98), channel_id=1, source_target_pairs={{0,1},{1,2},{2,3},{3,4},{4,5},{5,6},{6,7},{7,8},{8,9},{9,10},{10,1... | collective-permute-start | bytes 393224 | tf_op jit(solution)/shard_map/while/body/eval_jaxpr/ppermute | solution.py:24
  93.3 8.2 %collective-permute-start = (f32[4,2,4096]{2,1,0:T(2,128)S(1)}, f32[4,2,4096]{2,1,0:T(2,128)S(1)}, u32[]{:S(2)}, u32[]{:S(2)}) collective-permute-start(f32[4,2,4096]{2,1,0:T(2,128)S(1)} %get-tuple-element.97), channel_id=1, source_target_pairs={{1,0},{2,1},{3,2},{4,3},{5,4},{6,5},{7,6},{8,7},{9,8},{10,9},{11,1... | collective-permute-start | bytes 393224 | tf_op jit(solution)/shard_map/while/body/eval_jaxpr/ppermute | solution.py:25
  94.6 7.8 %collective-permute-start.1 = (f32[4,2,4096]{2,1,0:T(2,128)S(1)}, f32[4,2,4096]{2,1,0:T(2,128)S(1)}, u32[]{:S(2)}, u32[]{:S(2)}) collective-permute-start(f32[4,2,4096]{2,1,0:T(2,128)S(1)} %get-tuple-element.98), channel_id=1, source_target_pairs={{0,1},{1,2},{2,3},{3,4},{4,5},{5,6},{6,7},{7,8},{8,9},{9,10},{10,1... | collective-permute-start | bytes 393224 | tf_op jit(solution)/shard_map/while/body/eval_jaxpr/ppermute | solution.py:24
  106.9 8.2 %collective-permute-start = (f32[4,2,4096]{2,1,0:T(2,128)S(1)}, f32[4,2,4096]{2,1,0:T(2,128)S(1)}, u32[]{:S(2)}, u32[]{:S(2)}) collective-permute-start(f32[4,2,4096]{2,1,0:T(2,128)S(1)} %get-tuple-element.97), channel_id=1, source_target_pairs={{1,0},{2,1},{3,2},{4,3},{5,4},{6,5},{7,6},{8,7},{9,8},{10,9},{11,1... | collective-permute-start | bytes 393224 | tf_op jit(solution)/shard_map/while/body/eval_jaxpr/ppermute | solution.py:25
  108.2 7.8 %collective-permute-start.1 = (f32[4,2,4096]{2,1,0:T(2,128)S(1)}, f32[4,2,4096]{2,1,0:T(2,128)S(1)}, u32[]{:S(2)}, u32[]{:S(2)}) collective-permute-start(f32[4,2,4096]{2,1,0:T(2,128)S(1)} %get-tuple-element.98), channel_id=1, source_target_pairs={{0,1},{1,2},{2,3},{3,4},{4,5},{5,6},{6,7},{7,8},{8,9},{9,10},{10,1... | collective-permute-start | bytes 393224 | tf_op jit(solution)/shard_map/while/body/eval_jaxpr/ppermute | solution.py:24
  120.4 8.2 %collective-permute-start = (f32[4,2,4096]{2,1,0:T(2,128)S(1)}, f32[4,2,4096]{2,1,0:T(2,128)S(1)}, u32[]{:S(2)}, u32[]{:S(2)}) collective-permute-start(f32[4,2,4096]{2,1,0:T(2,128)S(1)} %get-tuple-element.97), channel_id=1, source_target_pairs={{1,0},{2,1},{3,2},{4,3},{5,4},{6,5},{7,6},{8,7},{9,8},{10,9},{11,1... | collective-permute-start | bytes 393224 | tf_op jit(solution)/shard_map/while/body/eval_jaxpr/ppermute | solution.py:25
  121.7 7.8 %collective-permute-start.1 = (f32[4,2,4096]{2,1,0:T(2,128)S(1)}, f32[4,2,4096]{2,1,0:T(2,128)S(1)}, u32[]{:S(2)}, u32[]{:S(2)}) collective-permute-start(f32[4,2,4096]{2,1,0:T(2,128)S(1)} %get-tuple-element.98), channel_id=1, source_target_pairs={{0,1},{1,2},{2,3},{3,4},{4,5},{5,6},{6,7},{7,8},{8,9},{9,10},{10,1... | collective-permute-start | bytes 393224 | tf_op jit(solution)/shard_map/while/body/eval_jaxpr/ppermute | solution.py:24
  133.9 8.2 %collective-permute-start = (f32[4,2,4096]{2,1,0:T(2,128)S(1)}, f32[4,2,4096]{2,1,0:T(2,128)S(1)}, u32[]{:S(2)}, u32[]{:S(2)}) collective-permute-start(f32[4,2,4096]{2,1,0:T(2,128)S(1)} %get-tuple-element.97), channel_id=1, source_target_pairs={{1,0},{2,1},{3,2},{4,3},{5,4},{6,5},{7,6},{8,7},{9,8},{10,9},{11,1... | collective-permute-start | bytes 393224 | tf_op jit(solution)/shard_map/while/body/eval_jaxpr/ppermute | solution.py:25
  147.4 8.2 %collective-permute-start = (f32[4,2,4096]{2,1,0:T(2,128)S(1)}, f32[4,2,4096]{2,1,0:T(2,128)S(1)}, u32[]{:S(2)}, u32[]{:S(2)}) collective-permute-start(f32[4,2,4096]{2,1,0:T(2,128)S(1)} %get-tuple-element.97), channel_id=1, source_target_pairs={{1,0},{2,1},{3,2},{4,3},{5,4},{6,5},{7,6},{8,7},{9,8},{10,9},{11,1... | collective-permute-start | bytes 393224 | tf_op jit(solution)/shard_map/while/body/eval_jaxpr/ppermute | solution.py:25
  148.7 7.8 %collective-permute-start.1 = (f32[4,2,4096]{2,1,0:T(2,128)S(1)}, f32[4,2,4096]{2,1,0:T(2,128)S(1)}, u32[]{:S(2)}, u32[]{:S(2)}) collective-permute-start(f32[4,2,4096]{2,1,0:T(2,128)S(1)} %get-tuple-element.98), channel_id=1, source_target_pairs={{0,1},{1,2},{2,3},{3,4},{4,5},{5,6},{6,7},{7,8},{8,9},{9,10},{10,1... | collective-permute-start | bytes 393224 | tf_op jit(solution)/shard_map/while/body/eval_jaxpr/ppermute | solution.py:24
  160.9 8.2 %collective-permute-start = (f32[4,2,4096]{2,1,0:T(2,128)S(1)}, f32[4,2,4096]{2,1,0:T(2,128)S(1)}, u32[]{:S(2)}, u32[]{:S(2)}) collective-permute-start(f32[4,2,4096]{2,1,0:T(2,128)S(1)} %get-tuple-element.97), channel_id=1, source_target_pairs={{1,0},{2,1},{3,2},{4,3},{5,4},{6,5},{7,6},{8,7},{9,8},{10,9},{11,1... | collective-permute-start | bytes 393224 | tf_op jit(solution)/shard_map/while/body/eval_jaxpr/ppermute | solution.py:25
  162.2 7.8 %collective-permute-start.1 = (f32[4,2,4096]{2,1,0:T(2,128)S(1)}, f32[4,2,4096]{2,1,0:T(2,128)S(1)}, u32[]{:S(2)}, u32[]{:S(2)}) collective-permute-start(f32[4,2,4096]{2,1,0:T(2,128)S(1)} %get-tuple-element.98), channel_id=1, source_target_pairs={{0,1},{1,2},{2,3},{3,4},{4,5},{5,6},{6,7},{7,8},{8,9},{9,10},{10,1... | collective-permute-start | bytes 393224 | tf_op jit(solution)/shard_map/while/body/eval_jaxpr/ppermute | solution.py:24
  174.4 8.2 %collective-permute-start = (f32[4,2,4096]{2,1,0:T(2,128)S(1)}, f32[4,2,4096]{2,1,0:T(2,128)S(1)}, u32[]{:S(2)}, u32[]{:S(2)}) collective-permute-start(f32[4,2,4096]{2,1,0:T(2,128)S(1)} %get-tuple-element.97), channel_id=1, source_target_pairs={{1,0},{2,1},{3,2},{4,3},{5,4},{6,5},{7,6},{8,7},{9,8},{10,9},{11,1... | collective-permute-start | bytes 393224 | tf_op jit(solution)/shard_map/while/body/eval_jaxpr/ppermute | solution.py:25
  188.0 8.2 %collective-permute-start = (f32[4,2,4096]{2,1,0:T(2,128)S(1)}, f32[4,2,4096]{2,1,0:T(2,128)S(1)}, u32[]{:S(2)}, u32[]{:S(2)}) collective-permute-start(f32[4,2,4096]{2,1,0:T(2,128)S(1)} %get-tuple-element.97), channel_id=1, source_target_pairs={{1,0},{2,1},{3,2},{4,3},{5,4},{6,5},{7,6},{8,7},{9,8},{10,9},{11,1... | collective-permute-start | bytes 393224 | tf_op jit(solution)/shard_map/while/body/eval_jaxpr/ppermute | solution.py:25
  201.5 8.2 %collective-permute-start = (f32[4,2,4096]{2,1,0:T(2,128)S(1)}, f32[4,2,4096]{2,1,0:T(2,128)S(1)}, u32[]{:S(2)}, u32[]{:S(2)}) collective-permute-start(f32[4,2,4096]{2,1,0:T(2,128)S(1)} %get-tuple-element.97), channel_id=1, source_target_pairs={{1,0},{2,1},{3,2},{4,3},{5,4},{6,5},{7,6},{8,7},{9,8},{10,9},{11,1... | collective-permute-start | bytes 393224 | tf_op jit(solution)/shard_map/while/body/eval_jaxpr/ppermute | solution.py:25
  215.0 8.2 %collective-permute-start = (f32[4,2,4096]{2,1,0:T(2,128)S(1)}, f32[4,2,4096]{2,1,0:T(2,128)S(1)}, u32[]{:S(2)}, u32[]{:S(2)}) collective-permute-start(f32[4,2,4096]{2,1,0:T(2,128)S(1)} %get-tuple-element.97), channel_id=1, source_target_pairs={{1,0},{2,1},{3,2},{4,3},{5,4},{6,5},{7,6},{8,7},{9,8},{10,9},{11,1... | collective-permute-start | bytes 393224 | tf_op jit(solution)/shard_map/while/body/eval_jaxpr/ppermute | solution.py:25
  228.5 8.2 %collective-permute-start = (f32[4,2,4096]{2,1,0:T(2,128)S(1)}, f32[4,2,4096]{2,1,0:T(2,128)S(1)}, u32[]{:S(2)}, u32[]{:S(2)}) collective-permute-start(f32[4,2,4096]{2,1,0:T(2,128)S(1)} %get-tuple-element.97), channel_id=1, source_target_pairs={{1,0},{2,1},{3,2},{4,3},{5,4},{6,5},{7,6},{8,7},{9,8},{10,9},{11,1... | collective-permute-start | bytes 393224 | tf_op jit(solution)/shard_map/while/body/eval_jaxpr/ppermute | solution.py:25
  242.0 8.2 %collective-permute-start = (f32[4,2,4096]{2,1,0:T(2,128)S(1)}, f32[4,2,4096]{2,1,0:T(2,128)S(1)}, u32[]{:S(2)}, u32[]{:S(2)}) collective-permute-start(f32[4,2,4096]{2,1,0:T(2,128)S(1)} %get-tuple-element.97), channel_id=1, source_target_pairs={{1,0},{2,1},{3,2},{4,3},{5,4},{6,5},{7,6},{8,7},{9,8},{10,9},{11,1... | collective-permute-start | bytes 393224 | tf_op jit(solution)/shard_map/while/body/eval_jaxpr/ppermute | solution.py:25
  255.5 8.2 %collective-permute-start = (f32[4,2,4096]{2,1,0:T(2,128)S(1)}, f32[4,2,4096]{2,1,0:T(2,128)S(1)}, u32[]{:S(2)}, u32[]{:S(2)}) collective-permute-start(f32[4,2,4096]{2,1,0:T(2,128)S(1)} %get-tuple-element.97), channel_id=1, source_target_pairs={{1,0},{2,1},{3,2},{4,3},{5,4},{6,5},{7,6},{8,7},{9,8},{10,9},{11,1... | collective-permute-start | bytes 393224 | tf_op jit(solution)/shard_map/while/body/eval_jaxpr/ppermute | solution.py:25
  269.0 8.2 %collective-permute-start = (f32[4,2,4096]{2,1,0:T(2,128)S(1)}, f32[4,2,4096]{2,1,0:T(2,128)S(1)}, u32[]{:S(2)}, u32[]{:S(2)}) collective-permute-start(f32[4,2,4096]{2,1,0:T(2,128)S(1)} %get-tuple-element.97), channel_id=1, source_target_pairs={{1,0},{2,1},{3,2},{4,3},{5,4},{6,5},{7,6},{8,7},{9,8},{10,9},{11,1... | collective-permute-start | bytes 393224 | tf_op jit(solution)/shard_map/while/body/eval_jaxpr/ppermute | solution.py:25
  282.6 8.2 %collective-permute-start = (f32[4,2,4096]{2,1,0:T(2,128)S(1)}, f32[4,2,4096]{2,1,0:T(2,128)S(1)}, u32[]{:S(2)}, u32[]{:S(2)}) collective-permute-start(f32[4,2,4096]{2,1,0:T(2,128)S(1)} %get-tuple-element.97), channel_id=1, source_target_pairs={{1,0},{2,1},{3,2},{4,3},{5,4},{6,5},{7,6},{8,7},{9,8},{10,9},{11,1... | collective-permute-start | bytes 393224 | tf_op jit(solution)/shard_map/while/body/eval_jaxpr/ppermute | solution.py:25
  296.1 8.2 %collective-permute-start = (f32[4,2,4096]{2,1,0:T(2,128)S(1)}, f32[4,2,4096]{2,1,0:T(2,128)S(1)}, u32[]{:S(2)}, u32[]{:S(2)}) collective-permute-start(f32[4,2,4096]{2,1,0:T(2,128)S(1)} %get-tuple-element.97), channel_id=1, source_target_pairs={{1,0},{2,1},{3,2},{4,3},{5,4},{6,5},{7,6},{8,7},{9,8},{10,9},{11,1... | collective-permute-start | bytes 393224 | tf_op jit(solution)/shard_map/while/body/eval_jaxpr/ppermute | solution.py:25
  309.6 8.2 %collective-permute-start = (f32[4,2,4096]{2,1,0:T(2,128)S(1)}, f32[4,2,4096]{2,1,0:T(2,128)S(1)}, u32[]{:S(2)}, u32[]{:S(2)}) collective-permute-start(f32[4,2,4096]{2,1,0:T(2,128)S(1)} %get-tuple-element.97), channel_id=1, source_target_pairs={{1,0},{2,1},{3,2},{4,3},{5,4},{6,5},{7,6},{8,7},{9,8},{10,9},{11,1... | collective-permute-start | bytes 393224 | tf_op jit(solution)/shard_map/while/body/eval_jaxpr/ppermute | solution.py:25
  (19 other events, 151.3 us)
where the time goes:
time: 373 us; the launch traced here: 371 us
  starting transfers between devices  191 us (51%)
  other arithmetic  107 us (29%)
  local copies, waits for them, and re-layouts  30.6 us (8%)
  waiting for transfers between devices  21.3 us (6%)
  blocking collectives  17.9 us (5%)
    ppermute x24, starting transfers between devices, padded_2(): before = lax.ppermute(last, axis, up)  160 us
    min x24, other arithmetic, relax(): return jnp.minimum(shifted(0, 0), best)  95 us
    ppermute x24, starting transfers between devices, padded_2(): after = lax.ppermute(leading, axis, down)  31 us
    ppermute x24, waiting for transfers between devices, padded_2(): before = lax.ppermute(last, axis, up)  21.3 us
    all_to_all x1, blocking collectives, on_device(): lax.all_to_all(placed.reshape(sources, count, capacity), 'space', split_a...  17.9 us
    div x1, local copies, waits for them, and re-layouts, on_device(): each_arrival = jnp.minimum(times, jnp.float32(clip_value)) / clip_value  16.2 us
    gather x1, local copies, waits for them, and re-layouts, on_device(): values = each_arrival.reshape(sources, -1)[:, gauge_cells]  11.2 us
  transfers between devices with their start and end apart: 48, of which 24 were waited for; matrix products, arithmetic and copies ran while one was open for 0% of the time, Pallas kernels for 0%

commit v1 on v0

v1 whole, which is shorter than its diff:
```python
import functools
import jax
import jax.numpy as jnp
from jax import lax
from jax.experimental import pallas as pl
from jax.experimental.pallas import tpu as pltpu
from jax.sharding import PartitionSpec as P

SWEEPS = 8
BLOCKS = 3
ROUNDS = 2

far_value = 1000000.0
land_cost = 10000.0
clip_value = 48.0
root_two = 1.41421356
root_five = 2.23606798

PLANE = 4
LANES = 128
SIDE = 64
PAD = 8
ANY = pl.BlockSpec(memory_space=pl.ANY)
SMEM = pl.BlockSpec(memory_space=pltpu.SMEM)
VMEM = pl.BlockSpec(memory_space=pltpu.VMEM)


def run_copies(copies):
    for copy in copies:
        copy.start()
    for copy in copies:
        copy.wait()


def pack_kernel(groups, cap, place_ref, source_ref, slow_ref, ocean_ref, start_ref, gauge_ref, *rest):
    outs, (cut, sem) = rest[:-2], rest[-2:]
    rows, width = slow_ref.shape
    own = width // PLANE
    tiles = own // LANES
    member = place_ref[0]
    first_row = place_ref[2]
    lane = lax.broadcasted_iota(jnp.int32, (rows, LANES), 1)
    row = lax.broadcasted_iota(jnp.int32, (rows, LANES), 0)
    far = jnp.full((rows, LANES), far_value, jnp.float32)

    def window(field, base):
        for w in range(PLANE):
            for t in range(tiles):
                cut[w, base + t] = field(w * tiles + t)
            right = field((w + 1) * tiles) if w < PLANE - 1 else far
            left = field(w * tiles - 1) if w > 0 else far
            cut[w, base + tiles] = jnp.where(lane < SIDE, right, left)

    def cost(t):
        at = slice(t * LANES, (t + 1) * LANES)
        return jnp.where(ocean_ref[:, at] == 1, slow_ref[:, at], jnp.float32(land_cost))

    def times(s):
        def tile(t):
            flat = (first_row + row) * width + (t * LANES + lane)
            return jnp.where(flat == source_ref[s], 0.0, start_ref[s, :, t * LANES : (t + 1) * LANES])

        return tile

    base = 0
    for number, group in enumerate(groups):
        for s in group:
            window(times(s), base)
            base += tiles + 1
        if number == 0:
            window(cost, base)
            base += tiles + 1
            owner = gauge_ref[2:3, :].astype(jnp.float32)
            across = jnp.broadcast_to(owner, (LANES, LANES))
            down = jnp.transpose(across)
            earlier = lax.broadcasted_iota(jnp.int32, (LANES, LANES), 0) < lax.broadcasted_iota(
                jnp.int32, (LANES, LANES), 1
            )
            same = jnp.where(earlier & (across == down), 1.0, 0.0)
            slot = owner * cap + jnp.sum(same, axis=0, keepdims=True)
            spots = gauge_ref[...].astype(jnp.float32)
            head = lax.broadcasted_iota(jnp.int32, spots.shape, 0)
            meta = jnp.where(head == 2, slot, spots)
            for w in range(PLANE):
                cut[w, base, 0:8] = meta
                cut[w, base, 8:rows] = jnp.zeros((rows - 8, LANES), jnp.float32)
            base += 1
    copies = []
    start = 0
    for number in range(len(groups)):
        for j in range(PLANE):
            out = outs[number * PLANE + j]
            size = out.shape[0]
            copies.append(
                pltpu.make_async_copy(
                    cut.at[member ^ j, start : start + size], out, sem.at[number * PLANE + j]
                )
            )
        start += size
    run_copies(copies)


def edge_kernel(slabs, halo, place_ref, p0, p1, p2, p3, even_ref, odd_ref, full, sem):
    member, plane = place_ref[0], place_ref[1]
    rows = p0.shape[1]
    total = PLANE * rows
    run_copies(
        [
            pltpu.make_async_copy(
                p.at[0:slabs], full.at[:, pl.ds(pl.multiple_of((member ^ j) * rows, 8), rows)], sem.at[j]
            )
            for j, p in enumerate((p0, p1, p2, p3))
        ]
    )
    parity = lax.rem(plane, 2)
    low = pl.multiple_of((1 - parity) * (total - halo), 8)
    high = pl.multiple_of(parity * (total - halo), 8)
    run_copies(
        [
            pltpu.make_async_copy(full.at[:, pl.ds(low, halo)], even_ref, sem.at[0]),
            pltpu.make_async_copy(full.at[:, pl.ds(high, halo)], odd_ref, sem.at[1]),
        ]
    )


def relax_rows(src, dst, cost, count, tiles, start):
    lane = lax.broadcasted_iota(jnp.int32, (8, LANES), 1)
    first, last = lane == 0, lane == LANES - 1

    def from_left(field):
        turned = [pltpu.roll(v, 1, 1) for v in field]
        return [jnp.where(first, turned[t - 1], turned[t]) for t in range(tiles)]

    def from_right(field):
        turned = [pltpu.roll(v, LANES - 1, 1) for v in field]
        return [jnp.where(last, turned[(t + 1) % tiles], turned[t]) for t in range(tiles)]

    c1 = [cost[t, pl.ds(start, 8)] for t in range(tiles)]
    c2 = [root_two * v for v in c1]
    c5 = [root_five * v for v in c1]
    for s in range(count):
        here, one, two = [], [], []
        for t in range(tiles):
            at = s * tiles + t
            here.append(src[at, pl.ds(start, 8)])
            one.append(jnp.minimum(src[at, pl.ds(start - 1, 8)], src[at, pl.ds(start + 1, 8)]))
            two.append(jnp.minimum(src[at, pl.ds(start - 2, 8)], src[at, pl.ds(start + 2, 8)]))
        left, right = from_left(one), from_right(one)
        wide_left = from_left([jnp.minimum(a, b) for a, b in zip(left, two)])
        wide_right = from_right([jnp.minimum(a, b) for a, b in zip(right, two)])
        here_left, here_right = from_left(here), from_right(here)
        for t in range(tiles):
            m1 = jnp.minimum(one[t], jnp.minimum(here_left[t], here_right[t]))
            m2 = jnp.minimum(left[t], right[t])
            m5 = jnp.minimum(wide_left[t], wide_right[t])
            best = jnp.minimum(jnp.minimum(m1 + c1[t], m2 + c2[t]), m5 + c5[t])
            dst[s * tiles + t, pl.ds(start, 8)] = jnp.minimum(here[t], best)


def run_sweeps(first, second, cost, count, tiles, sweeps):
    groups = (first.shape[1] - 2 * PAD) // 8

    def sweep(src, dst, number):
        low = (2 * number) // 8

        def group(at, carry):
            relax_rows(src, dst, cost, count, tiles, pl.multiple_of(PAD + at * 8, 8))
            return carry

        lax.fori_loop(low, groups - low, group, 0)

    def pair(at, carry):
        sweep(first, second, 2 * at + 1)
        sweep(second, first, 2 * at + 2)
        return carry

    lax.fori_loop(0, sweeps // 2, pair, 0)


def halo_copies(plane, halo, total, even, odd, dst, sem, slabs):
    parity = lax.rem(plane, 2)
    above, below = PAD, PAD + halo + total
    even_at = pl.multiple_of(parity * above + (1 - parity) * below, 8)
    odd_at = pl.multiple_of((1 - parity) * above + parity * below, 8)
    copies = [
        pltpu.make_async_copy(even.at[slabs], dst.at[:, pl.ds(even_at, halo)], sem.at[0]),
        pltpu.make_async_copy(odd.at[slabs], dst.at[:, pl.ds(odd_at, halo)], sem.at[1]),
    ]
    return copies, odd_at


def fence(plane, planes, odd_at, halo, field):
    @pl.when((plane == 0) | (plane == planes - 1))
    def _():
        for t in range(field.shape[0]):
            field[t, pl.ds(odd_at, halo)] = jnp.full((halo, LANES), far_value, jnp.float32)


def first_kernel(count, sweeps, has_cost, planes, place_ref, p0, p1, p2, p3, even, odd, *rest):
    if has_cost:
        state, low_ref, high_ref, cost_out, one, two, cost, sem = rest
    else:
        cost_in, state, low_ref, high_ref, one, two, cost, sem = rest
    member, plane = place_ref[0], place_ref[1]
    rows, halo = p0.shape[1], even.shape[1]
    total = PLANE * rows
    tiles = cost.shape[0]
    size = count * tiles
    copies = [
        pltpu.make_async_copy(
            p.at[0:size],
            one.at[:, pl.ds(pl.multiple_of(PAD + halo + (member ^ j) * rows, 8), rows)],
            sem.at[4 + j],
        )
        for j, p in enumerate((p0, p1, p2, p3))
    ]
    halos, odd_at = halo_copies(plane, halo, total, even, odd, one, sem, slice(0, size))
    copies += halos
    if has_cost:
        more, _ = halo_copies(
            plane, halo, total, even, odd, cost, sem.at[pl.ds(2, 2)], slice(size, size + tiles)
        )
        copies += more
        copies += [
            pltpu.make_async_copy(
                p.at[size : size + tiles],
                cost.at[:, pl.ds(pl.multiple_of(PAD + halo + (member ^ j) * rows, 8), rows)],
                sem.at[8 + j],
            )
            for j, p in enumerate((p0, p1, p2, p3))
        ]
    else:
        copies.append(pltpu.make_async_copy(cost_in, cost, sem.at[8]))
    run_copies(copies)
    fence(plane, planes, odd_at, halo, one)
    if has_cost:
        fence(plane, planes, odd_at, halo, cost)
    run_sweeps(one, two, cost, count, tiles, sweeps)
    parity = lax.rem(plane, 2)
    top, bottom = PAD + halo, PAD + halo + total - halo
    low = pl.multiple_of(parity * top + (1 - parity) * bottom, 8)
    high = pl.multiple_of((1 - parity) * top + parity * bottom, 8)
    copies = [
        pltpu.make_async_copy(one.at[:, pl.ds(low, halo)], low_ref, sem.at[0]),
        pltpu.make_async_copy(one.at[:, pl.ds(high, halo)], high_ref, sem.at[1]),
        pltpu.make_async_copy(one.at[:, PAD + halo : PAD + halo + total], state, sem.at[2]),
    ]
    if has_cost:
        copies.append(pltpu.make_async_copy(cost, cost_out, sem.at[3]))
    run_copies(copies)


def last_kernel(count, sweeps, is_last, planes, place_ref, state, even, odd, cost_in, m0, m1, m2, m3, *rest):
    if is_last:
        partial_ref, placed_ref, r0, r1, r2, r3, one, two, cost, meta, best, sem = rest
    else:
        placed_ref, best, one, two, cost, meta, sem = rest
    member, plane = place_ref[0], place_ref[1]
    total, halo = state.shape[1], even.shape[1]
    rows = total // PLANE
    tiles = cost.shape[0]
    own = tiles - 1
    copies = [
        pltpu.make_async_copy(state, one.at[:, PAD + halo : PAD + halo + total], sem.at[2]),
        pltpu.make_async_copy(cost_in, cost, sem.at[3]),
    ]
    copies += [
        pltpu.make_async_copy(m.at[m.shape[0] - 1], meta.at[member ^ j], sem.at[4 + j])
        for j, m in enumerate((m0, m1, m2, m3))
    ]
    halos, odd_at = halo_copies(plane, halo, total, even, odd, one, sem, slice(0, count * tiles))
    run_copies(copies + halos)
    fence(plane, planes, odd_at, halo, one)
    run_sweeps(one, two, cost, count, tiles, sweeps)

    for t in range(own):
        low = None
        for s in range(count):
            at = (s * tiles + t, slice(PAD + halo, PAD + halo + total))
            each = jnp.minimum(one[at], jnp.float32(clip_value)) / clip_value
            one[at] = each
            low = each if low is None else jnp.minimum(low, each)
        best[t] = jnp.minimum(low, partial_ref[t]) if is_last else low
    copies = []
    if is_last:
        copies = [
            pltpu.make_async_copy(
                best.at[:, pl.ds(pl.multiple_of((member ^ j) * rows, 8), rows)], r, sem.at[j]
            )
            for j, r in enumerate((r0, r1, r2, r3))
        ]
        for copy in copies:
            copy.start()

    slots = placed_ref.shape[1]
    lane = lax.broadcasted_iota(jnp.int32, (LANES, LANES), 1).astype(jnp.float32)
    spot = lax.broadcasted_iota(jnp.int32, (LANES, slots), 1).astype(jnp.float32)
    filler = jnp.zeros((LANES - meta.shape[1], LANES), jnp.float32)
    offset = (member * (own * rows)).astype(jnp.float32)
    for q in range(PLANE):
        turned = jnp.transpose(jnp.concatenate([meta[q], filler], axis=0))
        pick = jnp.where(turned[:, 0:1] - offset == lane, 1.0, 0.0).astype(jnp.bfloat16)
        at_lane = turned[:, 1:2] == lane
        at_slot = turned[:, 2:3] == spot
        for s in range(count):
            block = one[s * tiles : s * tiles + own, PAD + halo + q * rows : PAD + halo + (q + 1) * rows]
            rest_of = block.reshape(own * rows, LANES)
            found = jnp.zeros((LANES, LANES), jnp.float32)
            for _ in range(3):
                part = rest_of.astype(jnp.bfloat16)
                rest_of = rest_of - part.astype(jnp.float32)
                found = found + jnp.dot(pick, part, preferred_element_type=jnp.float32)
            value = jnp.sum(jnp.where(at_lane, found, 0.0), axis=1, keepdims=True)
            placed_ref[s * PLANE + q : s * PLANE + q + 1] = jnp.sum(
                jnp.where(at_slot, value, 0.0), axis=0, keepdims=True
            )
    for copy in copies:
        copy.wait()


def join_kernel(place_ref, r0, r1, r2, r3, out_ref):
    member = place_ref[0]
    tiles, rows, _ = r0.shape
    for j, r in enumerate((r0, r1, r2, r3)):
        base = (member ^ j) * (tiles * LANES)
        for t in range(tiles):
            out_ref[:, pl.ds(pl.multiple_of(base + t * LANES, LANES), LANES)] = r[t]


def shape_of(*dims):
    return jax.ShapeDtypeStruct(dims, jnp.float32)


def on_device(slowness, ocean, start_times, source_cells, gauge_cells, gauge_owner):
    axis = "space"
    index = lax.axis_index(axis)
    n = lax.axis_size(axis)
    rows, width = slowness.shape
    sources = start_times.shape[0]
    gauges = gauge_cells.shape[0]
    planes = n // PLANE
    assert n % (2 * PLANE) == 0 and width % (PLANE * LANES) == 0
    assert gauges == LANES and rows * (width // PLANE) == LANES * LANES and sources % 2 == 0
    sweeps = SWEEPS * BLOCKS // ROUNDS
    halo = 2 * sweeps
    total = rows * PLANE
    tiles = width // PLANE // LANES + 1
    assert 2 * SWEEPS * BLOCKS <= SIDE and halo <= total and sweeps % 2 == 0 and halo % 8 == 0
    cap = max(2, 2 * gauges // n)
    half = sources // 2
    groups = (tuple(range(half)), tuple(range(half, sources)))
    plane = index // PLANE
    place = jnp.stack([index % PLANE, plane, index * rows]).astype(jnp.int32)
    column, line = gauge_cells % width, gauge_cells // width
    spots = jnp.stack(
        [(column // LANES) * rows + line, column % LANES, gauge_owner[:, 0]]
        + [jnp.zeros_like(gauge_cells)] * 5
    )

    sizes = [half * tiles + tiles + 1, half * tiles]
    packed = pl.pallas_call(
        functools.partial(pack_kernel, groups, cap),
        out_shape=[shape_of(size, rows, LANES) for size in sizes for _ in range(PLANE)],
        in_specs=[SMEM, SMEM, VMEM, VMEM, VMEM, VMEM],
        out_specs=[ANY] * (2 * PLANE),
        scratch_shapes=[
            pltpu.VMEM((PLANE, sum(sizes), rows, LANES), jnp.float32),
            pltpu.SemaphoreType.DMA((2 * PLANE,)),
        ],
        name="pack",
    )(place, source_cells, slowness, ocean, start_times, spots)

    def swap(x, j):
        return lax.ppermute(x, axis, [(d, d ^ j) for d in range(n)])

    def swap_planes(even, odd):
        pairs_even = [(d, (d // PLANE ^ 1) * PLANE + d % PLANE) for d in range(n)]
        pairs_odd = [
            (d, (((d // PLANE + 1) ^ 1) - 1) * PLANE + d % PLANE)
            for d in range(PLANE, n - PLANE)
        ]
        return lax.ppermute(even, axis, pairs_even), lax.ppermute(odd, axis, pairs_odd)

    pieces = [
        [packed[k * PLANE]] + [swap(packed[k * PLANE + j], j) for j in range(1, PLANE)]
        for k in range(2)
    ]
    halos = []
    for k in range(2):
        slabs = half * tiles + (tiles if k == 0 else 0)
        even, odd = pl.pallas_call(
            functools.partial(edge_kernel, slabs, halo),
            out_shape=[shape_of(slabs, halo, LANES)] * 2,
            in_specs=[SMEM] + [ANY] * 4,
            out_specs=[ANY] * 2,
            scratch_shapes=[
                pltpu.VMEM((slabs, total, LANES), jnp.float32),
                pltpu.SemaphoreType.DMA((PLANE,)),
            ],
            name=f"edge{k}",
        )(place, *pieces[k])
        halos.append(swap_planes(even, odd))

    deep = total + 2 * halo + 2 * PAD
    size = half * tiles
    scratch = [
        pltpu.VMEM((size, deep, LANES), jnp.float32),
        pltpu.VMEM((size, deep, LANES), jnp.float32),
        pltpu.VMEM((tiles, deep, LANES), jnp.float32),
    ]
    states, later = [], []
    cost = None
    for k in range(2):
        outs = pl.pallas_call(
            functools.partial(first_kernel, half, sweeps, k == 0, planes),
            out_shape=[shape_of(size, total, LANES)]
            + [shape_of(size, halo, LANES)] * 2
            + ([shape_of(tiles, deep, LANES)] if k == 0 else []),
            in_specs=[SMEM] + [ANY] * (6 if k == 0 else 7),
            out_specs=[ANY] * (4 if k == 0 else 3),
            scratch_shapes=scratch + [pltpu.SemaphoreType.DMA((12,))],
            name=f"first{k}",
        )(place, *pieces[k], *halos[k], *([] if k == 0 else [cost]))
        if k == 0:
            cost = outs[3]
        states.append(outs[0])
        later.append(swap_planes(outs[1], outs[2]))

    own = tiles - 1
    slots = n * cap
    placed = []
    partial = None
    for k in range(2):
        is_last = k == 1
        out_shape = [shape_of(half * PLANE, slots)]
        out_specs = [VMEM]
        more = [pltpu.VMEM((PLANE, rows, LANES), jnp.float32)]
        if is_last:
            out_shape += [shape_of(own, rows, LANES)] * PLANE
            out_specs += [ANY] * PLANE
            more.append(pltpu.VMEM((own, total, LANES), jnp.float32))
        else:
            out_shape.append(shape_of(own, total, LANES))
            out_specs.append(VMEM)
        outs = pl.pallas_call(
            functools.partial(last_kernel, half, sweeps, is_last, planes),
            out_shape=out_shape,
            in_specs=[SMEM] + [ANY] * 8 + ([VMEM] if is_last else []),
            out_specs=out_specs,
            scratch_shapes=scratch + more + [pltpu.SemaphoreType.DMA((8,))],
            name=f"last{k}",
        )(place, states[k], *later[k], cost, *pieces[0], *([partial] if is_last else []))
        placed.append(outs[0])
        if is_last:
            returned = outs[1:]
        else:
            partial = outs[1]

    arrival = pl.pallas_call(
        join_kernel,
        out_shape=shape_of(rows, width),
        in_specs=[SMEM] + [VMEM] * PLANE,
        out_specs=VMEM,
        name="join",
    )(place, returned[0], *[swap(returned[j], j) for j in range(1, PLANE)])

    sent = jnp.concatenate(placed, axis=0).reshape(sources * PLANE, n, cap).transpose(1, 0, 2)
    received = lax.all_to_all(sent, axis, split_axis=0, concat_axis=0, tiled=True)
    joined = jnp.sum(received.reshape(planes, PLANE, sources, PLANE, cap), axis=1)
    result = joined.transpose(1, 0, 2, 3).reshape(1, sources, n * cap)
    return (arrival, result)


def solution(mesh):
    return jax.shard_map(
        on_device,
        mesh=mesh,
        in_specs=(
            P(("groups", "space"), None),
            P(("groups", "space"), None),
            P("groups", "space", None),
            P("groups"),
            P(("groups", "space")),
            P(("groups", "space"), None),
        ),
        out_specs=(P(("groups", "space"), None), P(("groups", "space"), None, None)),
        check_vma=False,
    )
```

time: 373 us -> 198 us (0.53)
  starting transfers between devices: 191 us -> 23.1 us
  Pallas kernels: 0 us -> 141 us
  other arithmetic: 107 us -> 2.06 us
  local copies, waits for them, and re-layouts: 30.6 us -> 9.17 us
  waiting for transfers between devices: 21.3 us -> 9.37 us
  blocking collectives: 17.9 us -> 11.1 us
    ppermute x48 -> x17, starting transfers between devices: 191 us -> 23.1 us  [the longest x4 13.3 us: swap_planes(): lax.ppermute(even, axis, pairs_even)]
    pallas_call x0 -> x8, Pallas kernels: none -> 141 us  [the longest x2 66.3 us: on_device(): pl.pallas_call(functools.partial(last_kernel, half, sweeps, is_last, plan...]
    min x24 -> x0, other arithmetic: 95 us -> none  [relax(): return jnp.minimum(shifted(0, 0), best)]
    div x1 -> x0, local copies, waits for them, and re-layouts: 16.2 us -> none  [on_device(): each_arrival = jnp.minimum(times, jnp.float32(clip_value)) / clip_value]
    ppermute x48 -> x17, waiting for transfers between devices: 21.3 us -> 9.37 us  [the longest x9 9.35 us: swap(): return lax.ppermute(x, axis, [(d, d ^ j) for d in range(n)])]
    gather x1 -> x0, local copies, waits for them, and re-layouts: 11.2 us -> none  [on_device(): values = each_arrival.reshape(sources, -1)[:, gauge_cells]]
    select_n x27 -> x0, other arithmetic: 9.4 us -> none  [the longest x24 7.45 us: fence(): return jnp.where(inside[None, :, None], field, jnp.float32(far_value))]
    unnamed x6 -> x42, local copies, waits for them, and re-layouts: 0.19 us -> 7.21 us
  transfers between devices with their start and end apart: 48 -> 17, of which waited for: 24 -> 3; matrix products, arithmetic and copies ran while one was open for 0% -> 2% of each run, Pallas kernels for 0% -> 52%
where the time goes in v1:
time: 198 us; the launch traced here: 197 us
  Pallas kernels  141 us (71%)
  starting transfers between devices  23.1 us (12%)
  blocking collectives  11.1 us (6%)
  waiting for transfers between devices  9.37 us (5%)
  local copies, waits for them, and re-layouts  9.17 us (5%)
  other arithmetic  2.06 us (1%)
    pallas_call x2, Pallas kernels, on_device(): pl.pallas_call(functools.partial(last_kernel, half, sweeps, is_last, plan...  66.3 us
    pallas_call x2, Pallas kernels, on_device(): pl.pallas_call(functools.partial(first_kernel, half, sweeps, k == 0, plan...  65 us
    ppermute x4, starting transfers between devices, swap_planes(): lax.ppermute(even, axis, pairs_even)  13.3 us
    all_to_all x1, blocking collectives, on_device(): lax.all_to_all(sent, axis, split_axis=0, concat_axis=0, tiled=True)  11.1 us
    ppermute x9, waiting for transfers between devices, swap(): return lax.ppermute(x, axis, [(d, d ^ j) for d in range(n)])  9.35 us
    unnamed x42, local copies, waits for them, and re-layouts  7.21 us
    ppermute x9, starting transfers between devices, swap(): return lax.ppermute(x, axis, [(d, d ^ j) for d in range(n)])  7.2 us
    pallas_call x2, Pallas kernels, on_device(): pl.pallas_call(functools.partial(edge_kernel, slabs, halo), out_shape=[sh...  5.38 us
  transfers between devices with their start and end apart: 17, of which 3 were waited for; matrix products, arithmetic and copies ran while one was open for 2% of the time, Pallas kernels for 52%

profile of v1, /device:TPU:0, one launch (start us, length us, event | category | flops | bytes accessed | tf_op | source)
XLA Modules:
  0.0 197.0 jit_solution(12604176602945835470)
XLA Ops:
  2.0 0.7 copy-done.18
  3.2 2.8 %pack.1 = (f32[28,16,128]{2,1,0:T(8,128)}, f32[28,16,128]{2,1,0:T(8,128)}, f32[28,16,128]{2,1,0:T(8,128)}, f32[28,16,128]{2,1,0:T(8,128)}, f32[18,16,128]{2,1,0:...) custom-call(s32[3]{0:T(128)} %pad_add_fusion.place_ref, s32[4]{0:T(128)} %source_ref.1, ...), custom_call_target="tpu_custom_call" | custom-call | tf_op jit(solution)/shard_map/pack/pallas_call | solution.py:361
  6.5 2.6 %collective-permute-start.6 = (f32[28,16,128]{2,1,0:T(8,128)}, f32[28,16,128]{2,1,0:T(8,128)S(1)}, u32[]{:S(2)}, u32[]{:S(2)}) collective-permute-start(f32[28,16,128]{2,1,0:T(8,128)} %get-tuple-element.36), channel_id=1, source_target_pairs={{0,2},{1,3},{2,0},{3,1},{4,6},{5,7},{6,4},{7,5},{8,10},{9,11},{10,... | collective-permute-start | bytes 688136 | tf_op jit(solution)/shard_map/ppermute | solution.py:374
  9.3 1.9 collective-permute-start.1
  11.3 4.5 %collective-permute-done.6.p2.m2 = f32[28,16,128]{2,1,0:T(8,128)S(1)} collective-permute-done((f32[28,16,128]{2,1,0:T(8,128)}, f32[28,16,128]{2,1,0:T(8,128)S(1)}, u32[]{:S(2)}, u32[]{:S(2)}) %collective-permute-start.6) | collective-permute-done | bytes 229408 | tf_op jit(solution)/shard_map/ppermute | solution.py:374
  15.8 4.6 %collective-permute-done.7.p3.m3 = f32[28,16,128]{2,1,0:T(8,128)S(1)} collective-permute-done((f32[28,16,128]{2,1,0:T(8,128)}, f32[28,16,128]{2,1,0:T(8,128)S(1)}, u32[]{:S(2)}, u32[]{:S(2)}) %collective-permute-start.7) | collective-permute-done | bytes 229408 | tf_op jit(solution)/shard_map/ppermute | solution.py:374
  20.4 0.7 copy-done.2
  21.1 2.8 %edge0.1 = (f32[27,24,128]{2,1,0:T(8,128)}, f32[27,24,128]{2,1,0:T(8,128)}) custom-call(s32[3]{0:T(128)} %pad_add_fusion.place_ref, f32[28,16,128]{2,1,0:T(8,128)} %get-tuple-element.34.p0.m0, f32[28,16,128]{2,1,0:T(8,128)} %copy-done, f32[28,16,128]{2,1,0:T(8,128)} %copy-done.1, f32[28,16,128]{2,1,0:T(8,128)} %copy-done.2), custom_call_target="tpu_custom_call" | custom-call | tf_op jit(solution)/shard_map/edge0/pallas_call | solution.py:391
  23.9 1.6 collective-permute-start.8
  25.5 0.7 collective-permute-start.9
  27.2 2.6 %edge1.1 = (f32[18,24,128]{2,1,0:T(8,128)}, f32[18,24,128]{2,1,0:T(8,128)}) custom-call(s32[3]{0:T(128)} %pad_add_fusion.place_ref, f32[18,16,128]{2,1,0:T(8,128)} %get-tuple-element.28.p0, f32[18,16,128]{2,1,0:T(8,128)} %copy-done.3, f32[18,16,128]{2,1,0:T(8,128)} %copy-done.4, f32[18,16,128]{2,1,0:T(8,128)} %copy-done.5), custom_call_target="tpu_custom_call" | custom-call | tf_op jit(solution)/shard_map/edge1/pallas_call | solution.py:391
  29.7 4.3 %collective-permute-start.3 = (f32[18,24,128]{2,1,0:T(8,128)}, f32[18,24,128]{2,1,0:T(8,128)S(1)}, u32[]{:S(2)}, u32[]{:S(2)}) collective-permute-start(f32[18,24,128]{2,1,0:T(8,128)} %get-tuple-element.32), channel_id=1, source_target_pairs={{0,4},{1,5},{2,6},{3,7},{4,0},{5,1},{6,2},{7,3},{8,12},{9,13},{10,... | collective-permute-start | bytes 663560 | tf_op jit(solution)/shard_map/ppermute | solution.py:382
  34.0 0.7 collective-permute-start.4
  34.7 0.7 copy-done.6
  35.4 0.7 copy-done.7
  36.2 32.6 %first0.1 = (f32[18,64,128]{2,1,0:T(8,128)}, f32[18,24,128]{2,1,0:T(8,128)}, f32[18,24,128]{2,1,0:T(8,128)}, f32[9,128,128]{2,1,0:T(8,128)}) custom-call(s32[3]{0:T(128)} %pad_add_fusion.place_ref, f32[28,16,128]{2,1,0:T(8,128)} %get-tuple-element.34.p0.m0, f32[28,16,128]{2,1,0:T(8,128)} %copy-done, f32[28,16,128]{2,1,0:T(8,128)} %copy-done.1, ...), custom_call_target="tpu_custom_call" | custom-call | tf_op jit(solution)/shard_map/first0/pallas_call | solution.py:414
  68.8 4.0 %collective-permute-start.12 = (f32[18,24,128]{2,1,0:T(8,128)}, f32[18,24,128]{2,1,0:T(8,128)S(1)}, u32[]{:S(2)}, u32[]{:S(2)}) collective-permute-start(f32[18,24,128]{2,1,0:T(8,128)} %get-tuple-element.45), channel_id=1, source_target_pairs={{0,4},{1,5},{2,6},{3,7},{4,0},{5,1},{6,2},{7,3},{8,12},{9,13},{10,... | collective-permute-start | bytes 663560 | tf_op jit(solution)/shard_map/ppermute | solution.py:382
  72.8 0.7 collective-permute-start.13
  73.5 0.7 copy-done.10
  74.2 32.4 %first1.1 = (f32[18,64,128]{2,1,0:T(8,128)}, f32[18,24,128]{2,1,0:T(8,128)}, f32[18,24,128]{2,1,0:T(8,128)}) custom-call(s32[3]{0:T(128)} %pad_add_fusion.place_ref, f32[18,16,128]{2,1,0:T(8,128)} %get-tuple-element.28.p0, f32[18,16,128]{2,1,0:T(8,128)} %copy-done.3, f32[18,16,128]{2,1,0:T(8,128)} %copy-done.4, f32[18,16,128]{2,1,0:T(8,128)} %copy-done.5, ...), custom_call_target="tpu_custom_call" | custom-call | tf_op jit(solution)/shard_map/first1/pallas_call | solution.py:414
  106.7 3.3 %collective-permute-start.10 = (f32[18,24,128]{2,1,0:T(8,128)}, f32[18,24,128]{2,1,0:T(8,128)S(1)}, u32[]{:S(2)}, u32[]{:S(2)}) collective-permute-start(f32[18,24,128]{2,1,0:T(8,128)} %get-tuple-element.42), channel_id=1, source_target_pairs={{0,4},{1,5},{2,6},{3,7},{4,0},{5,1},{6,2},{7,3},{8,12},{9,13},{10,... | collective-permute-start | bytes 663560 | tf_op jit(solution)/shard_map/ppermute | solution.py:382
  110.0 0.7 collective-permute-start.11
  110.7 0.7 copy-done.11
  111.4 32.9 %last0.1 = (f32[8,256]{1,0:T(8,128)}, f32[8,64,128]{2,1,0:T(8,128)}) custom-call(s32[3]{0:T(128)} %pad_add_fusion.place_ref, f32[18,64,128]{2,1,0:T(8,128)} %get-tuple-element.44.state, f32[18,24,128]{2,1,0:T(8,128)} %copy-done.11, f32[18,24,128]{2,1,0:T(8,128)} %copy-done.13, f32[9,128,128]{2,1,0:T(8,128)} %get-tuple-element.40.rest_0_.cost_in, ...), custom_call_target="tpu_custom_call" | custom-call | tf_op jit(solution)/shard_map/last0/pallas_call | solution.py:445
  144.4 0.7 copy-done.8
  145.1 33.4 %last1.1 = (f32[8,256]{1,0:T(8,128)}, f32[8,16,128]{2,1,0:T(8,128)}, f32[8,16,128]{2,1,0:T(8,128)}, f32[8,16,128]{2,1,0:T(8,128)}, f32[8,16,128]{2,1,0:T(8,128)}) custom-call(s32[3]{0:T(128)} %pad_add_fusion.place_ref, f32[18,64,128]{2,1,0:T(8,128)} %get-tuple-element.41.state, f32[18,24,128]{2,1,0:T(8,128)} %copy-done.8, f32[18,24,128]{2,1,0:T(8,128)} %copy-done.9, ...), custom_call_target="tpu_custom_call" | custom-call | tf_op jit(solution)/shard_map/last1/pallas_call | solution.py:445
  178.6 1.4 collective-permute-start.15
  180.5 0.7 pad_maximum_fusion
  181.5 11.1 %all_to_all.5 = f32[16,1,256]{2,1,0:T(1,128)S(1)} all-to-all(f32[16,1,256]{2,1,0:T(1,128)S(1)} %reshape.16), channel_id=1, replica_groups=mesh['groups'=2,'space'=16] {'space'}, dimensions={0} | all-to-all | bytes 32768 | tf_op jit(solution)/shard_map/all_to_all | solution.py:468
  193.1 0.7 reduce
  193.9 0.7 reshape.15
  195.3 1.7 join.1
  (67 shorter events, 6.0 us)
Async XLA Ops:
  6.0 5.3 %collective-permute-start.5 = (f32[28,16,128]{2,1,0:T(8,128)}, f32[28,16,128]{2,1,0:T(8,128)S(1)}, u32[]{:S(2)}, u32[]{:S(2)}) collective-permute-start(f32[28,16,128]{2,1,0:T(8,128)} %get-tuple-element.35), channel_id=1, source_target_pairs={{0,1},{1,0},{2,3},{3,2},{4,5},{5,4},{6,7},{7,6},{8,9},{9,8},{10,11... | collective-permute-start | bytes 688136 | tf_op jit(solution)/shard_map/ppermute | solution.py:374
  6.5 9.2 %collective-permute-start.6 = (f32[28,16,128]{2,1,0:T(8,128)}, f32[28,16,128]{2,1,0:T(8,128)S(1)}, u32[]{:S(2)}, u32[]{:S(2)}) collective-permute-start(f32[28,16,128]{2,1,0:T(8,128)} %get-tuple-element.36), channel_id=1, source_target_pairs={{0,2},{1,3},{2,0},{3,1},{4,6},{5,7},{6,4},{7,5},{8,10},{9,11},{10,... | collective-permute-start | bytes 688136 | tf_op jit(solution)/shard_map/ppermute | solution.py:374
  9.1 11.2 %collective-permute-start.7 = (f32[28,16,128]{2,1,0:T(8,128)}, f32[28,16,128]{2,1,0:T(8,128)S(1)}, u32[]{:S(2)}, u32[]{:S(2)}) collective-permute-start(f32[28,16,128]{2,1,0:T(8,128)} %get-tuple-element.37), channel_id=1, source_target_pairs={{0,3},{1,2},{2,1},{3,0},{4,7},{5,6},{6,5},{7,4},{8,11},{9,10},{10,... | collective-permute-start | bytes 688136 | tf_op jit(solution)/shard_map/ppermute | solution.py:374
  9.2 17.0 %collective-permute-start = (f32[18,16,128]{2,1,0:T(8,128)}, f32[18,16,128]{2,1,0:T(8,128)S(1)}, u32[]{:S(2)}, u32[]{:S(2)}) collective-permute-start(f32[18,16,128]{2,1,0:T(8,128)} %get-tuple-element.29), channel_id=1, source_target_pairs={{0,1},{1,0},{2,3},{3,2},{4,5},{5,4},{6,7},{7,6},{8,9},{9,8},{10,11... | collective-permute-start | bytes 442376 | tf_op jit(solution)/shard_map/ppermute | solution.py:374
  9.3 16.9 %collective-permute-start.1 = (f32[18,16,128]{2,1,0:T(8,128)}, f32[18,16,128]{2,1,0:T(8,128)S(1)}, u32[]{:S(2)}, u32[]{:S(2)}) collective-permute-start(f32[18,16,128]{2,1,0:T(8,128)} %get-tuple-element.30), channel_id=1, source_target_pairs={{0,2},{1,3},{2,0},{3,1},{4,6},{5,7},{6,4},{7,5},{8,10},{9,11},{10,... | collective-permute-start | bytes 442376 | tf_op jit(solution)/shard_map/ppermute | solution.py:374
  11.3 9.1 %copy-start = (f32[28,16,128]{2,1,0:T(8,128)}, f32[28,16,128]{2,1,0:T(8,128)S(1)}, u32[]{:S(2)}) copy-start(f32[28,16,128]{2,1,0:T(8,128)S(1)} %collective-permute-done.5.p1.m1) | copy-start | bytes 688132
  11.3 15.2 %collective-permute-start.2 = (f32[18,16,128]{2,1,0:T(8,128)}, f32[18,16,128]{2,1,0:T(8,128)S(1)}, u32[]{:S(2)}, u32[]{:S(2)}) collective-permute-start(f32[18,16,128]{2,1,0:T(8,128)} %get-tuple-element.31), channel_id=1, source_target_pairs={{0,3},{1,2},{2,1},{3,0},{4,7},{5,6},{6,5},{7,4},{8,11},{9,10},{10,... | collective-permute-start | bytes 442376 | tf_op jit(solution)/shard_map/ppermute | solution.py:374
  15.8 4.6 %copy-start.1 = (f32[28,16,128]{2,1,0:T(8,128)}, f32[28,16,128]{2,1,0:T(8,128)S(1)}, u32[]{:S(2)}) copy-start(f32[28,16,128]{2,1,0:T(8,128)S(1)} %collective-permute-done.6.p2.m2) | copy-start | bytes 688132
  20.4 0.7 copy-start.2
  23.9 10.8 %collective-permute-start.8 = (f32[27,24,128]{2,1,0:T(8,128)}, f32[27,24,128]{2,1,0:T(8,128)S(1)}, u32[]{:S(2)}, u32[]{:S(2)}) collective-permute-start(f32[27,24,128]{2,1,0:T(8,128)} %get-tuple-element.38), channel_id=1, source_target_pairs={{0,4},{1,5},{2,6},{3,7},{4,0},{5,1},{6,2},{7,3},{8,12},{9,13},{10,... | collective-permute-start | bytes 995336 | tf_op jit(solution)/shard_map/ppermute | solution.py:382
  25.5 9.2 %collective-permute-start.9 = (f32[27,24,128]{2,1,0:T(8,128)}, f32[27,24,128]{2,1,0:T(8,128)S(1)}, u32[]{:S(2)}, u32[]{:S(2)}) collective-permute-start(f32[27,24,128]{2,1,0:T(8,128)} %get-tuple-element.39), channel_id=1, source_target_pairs={{4,8},{5,9},{6,10},{7,11},{8,4},{9,5},{10,6},{11,7},{20,24},{21,25... | collective-permute-start | bytes 995336 | tf_op jit(solution)/shard_map/ppermute | solution.py:382
  26.2 0.7 copy-start.3
  26.2 0.7 copy-start.4
  26.5 0.7 copy-start.5
  29.7 43.7 %collective-permute-start.3 = (f32[18,24,128]{2,1,0:T(8,128)}, f32[18,24,128]{2,1,0:T(8,128)S(1)}, u32[]{:S(2)}, u32[]{:S(2)}) collective-permute-start(f32[18,24,128]{2,1,0:T(8,128)} %get-tuple-element.32), channel_id=1, source_target_pairs={{0,4},{1,5},{2,6},{3,7},{4,0},{5,1},{6,2},{7,3},{8,12},{9,13},{10,... | collective-permute-start | bytes 663560 | tf_op jit(solution)/shard_map/ppermute | solution.py:382
  34.0 39.5 %collective-permute-start.4 = (f32[18,24,128]{2,1,0:T(8,128)}, f32[18,24,128]{2,1,0:T(8,128)S(1)}, u32[]{:S(2)}, u32[]{:S(2)}) collective-permute-start(f32[18,24,128]{2,1,0:T(8,128)} %get-tuple-element.33), channel_id=1, source_target_pairs={{4,8},{5,9},{6,10},{7,11},{8,4},{9,5},{10,6},{11,7},{20,24},{21,25... | collective-permute-start | bytes 663560 | tf_op jit(solution)/shard_map/ppermute | solution.py:382
  34.7 0.7 copy-start.6
  35.4 0.7 copy-start.7
  68.8 41.9 %collective-permute-start.12 = (f32[18,24,128]{2,1,0:T(8,128)}, f32[18,24,128]{2,1,0:T(8,128)S(1)}, u32[]{:S(2)}, u32[]{:S(2)}) collective-permute-start(f32[18,24,128]{2,1,0:T(8,128)} %get-tuple-element.45), channel_id=1, source_target_pairs={{0,4},{1,5},{2,6},{3,7},{4,0},{5,1},{6,2},{7,3},{8,12},{9,13},{10,... | collective-permute-start | bytes 663560 | tf_op jit(solution)/shard_map/ppermute | solution.py:382
  72.8 37.9 %collective-permute-start.13 = (f32[18,24,128]{2,1,0:T(8,128)}, f32[18,24,128]{2,1,0:T(8,128)S(1)}, u32[]{:S(2)}, u32[]{:S(2)}) collective-permute-start(f32[18,24,128]{2,1,0:T(8,128)} %get-tuple-element.46), channel_id=1, source_target_pairs={{4,8},{5,9},{6,10},{7,11},{8,4},{9,5},{10,6},{11,7},{20,24},{21,25... | collective-permute-start | bytes 663560 | tf_op jit(solution)/shard_map/ppermute | solution.py:382
  73.5 0.7 copy-start.10
  73.5 0.8 copy-start.12
  106.7 37.7 %collective-permute-start.10 = (f32[18,24,128]{2,1,0:T(8,128)}, f32[18,24,128]{2,1,0:T(8,128)S(1)}, u32[]{:S(2)}, u32[]{:S(2)}) collective-permute-start(f32[18,24,128]{2,1,0:T(8,128)} %get-tuple-element.42), channel_id=1, source_target_pairs={{0,4},{1,5},{2,6},{3,7},{4,0},{5,1},{6,2},{7,3},{8,12},{9,13},{10,... | collective-permute-start | bytes 663560 | tf_op jit(solution)/shard_map/ppermute | solution.py:382
  110.0 34.4 %collective-permute-start.11 = (f32[18,24,128]{2,1,0:T(8,128)}, f32[18,24,128]{2,1,0:T(8,128)S(1)}, u32[]{:S(2)}, u32[]{:S(2)}) collective-permute-start(f32[18,24,128]{2,1,0:T(8,128)} %get-tuple-element.43), channel_id=1, source_target_pairs={{4,8},{5,9},{6,10},{7,11},{8,4},{9,5},{10,6},{11,7},{20,24},{21,25... | collective-permute-start | bytes 663560 | tf_op jit(solution)/shard_map/ppermute | solution.py:382
  110.7 0.7 copy-start.11
  110.7 0.8 copy-start.13
  144.3 0.7 copy-start.8
  144.4 0.7 copy-start.9
  178.5 1.9 copy-start.17
  178.6 16.0 %collective-permute-start.14 = (f32[8,16,128]{2,1,0:T(8,128)}, f32[8,16,128]{2,1,0:T(8,128)S(1)}, u32[]{:S(2)}, u32[]{:S(2)}) collective-permute-start(f32[8,16,128]{2,1,0:T(8,128)} %get-tuple-element.49), channel_id=1, source_target_pairs={{0,1},{1,0},{2,3},{3,2},{4,5},{5,4},{6,7},{7,6},{8,9},{9,8},{10,11... | collective-permute-start | bytes 196616 | tf_op jit(solution)/shard_map/ppermute | solution.py:374
  178.6 16.0 %collective-permute-start.15 = (f32[8,16,128]{2,1,0:T(8,128)}, f32[8,16,128]{2,1,0:T(8,128)S(1)}, u32[]{:S(2)}, u32[]{:S(2)}) collective-permute-start(f32[8,16,128]{2,1,0:T(8,128)} %get-tuple-element.50), channel_id=1, source_target_pairs={{0,2},{1,3},{2,0},{3,1},{4,6},{5,7},{6,4},{7,5},{8,10},{9,11},{10,... | collective-permute-start | bytes 196616 | tf_op jit(solution)/shard_map/ppermute | solution.py:374
  180.0 14.6 %collective-permute-start.16 = (f32[8,16,128]{2,1,0:T(8,128)}, f32[8,16,128]{2,1,0:T(8,128)S(1)}, u32[]{:S(2)}, u32[]{:S(2)}) collective-permute-start(f32[8,16,128]{2,1,0:T(8,128)} %get-tuple-element.51), channel_id=1, source_target_pairs={{0,3},{1,2},{2,1},{3,0},{4,7},{5,6},{6,5},{7,4},{8,11},{9,10},{10,... | collective-permute-start | bytes 196616 | tf_op jit(solution)/shard_map/ppermute | solution.py:374
  (5 other events, 3.2 us)

commit v2 on v1

v2 whole, which is shorter than its diff:
```python
import functools
import jax
import jax.numpy as jnp
from jax import lax
from jax.experimental import pallas as pl
from jax.experimental.pallas import tpu as pltpu
from jax.sharding import PartitionSpec as P

SWEEPS = 8
BLOCKS = 3
ROUNDS = 2

far_value = 1000000.0
land_cost = 10000.0
clip_value = 48.0
root_two = 1.41421356
root_five = 2.23606798

PLANE = 4
LANES = 128
SIDE = 64
PAD = 8
VMEM_BYTES = 24 * 1024 * 1024
ANY = pl.BlockSpec(memory_space=pl.ANY)
SMEM = pl.BlockSpec(memory_space=pltpu.SMEM)
VMEM = pl.BlockSpec(memory_space=pltpu.VMEM)


def run_copies(copies):
    for copy in copies:
        copy.start()
    for copy in copies:
        copy.wait()


def inverse(number):
    return pow(number, -1, LANES)


def spread(tiles):
    shape = (8, LANES)
    lane = lax.broadcasted_iota(jnp.int32, shape, 1)
    for j in range(tiles):
        chunk = ((lane + (LANES - j)) * inverse(tiles)) & (LANES - 1)
        tile_of = (chunk * tiles + j) >> 7
        masks = [tile_of == t for t in range(1, tiles)]
        order = (lane * tiles + j) & (LANES - 1)
        yield j, masks, order


def gather_lanes(x, order):
    return jnp.take_along_axis(x, order, axis=1, mode="promise_in_bounds")


def here():
    index = lax.axis_index("space")
    return lax.rem(index, PLANE), lax.div(index, PLANE), index


def pack_kernel(groups, cap, source_ref, slow_ref, ocean_ref, start_ref, cell_ref, owner_ref, *rest):
    outs, (plain, cut, sem) = rest[:-3], rest[-3:]
    rows, width = slow_ref.shape
    own = width // PLANE
    tiles = own // LANES
    chunk = tiles + 1
    member, _, index = here()
    first_row = index * rows
    lane = lax.broadcasted_iota(jnp.int32, (rows, LANES), 1)
    row = lax.broadcasted_iota(jnp.int32, (rows, LANES), 0)
    far = jnp.full((rows, LANES), far_value, jnp.float32)

    def window(field, at):
        for w in range(PLANE):
            for t in range(tiles):
                plain[w, at, t] = field(w * tiles + t)
            right = field((w + 1) * tiles) if w < PLANE - 1 else far
            left = field(w * tiles - 1) if w > 0 else far
            plain[w, at, tiles] = jnp.where(lane < SIDE, right, left)

    def cost(t):
        at = slice(t * LANES, (t + 1) * LANES)
        return jnp.where(ocean_ref[:, at] == 1, slow_ref[:, at], jnp.float32(land_cost))

    def times(s):
        def tile(t):
            flat = (first_row + row) * width + (t * LANES + lane)
            return jnp.where(flat == source_ref[s], 0.0, start_ref[s, :, t * LANES : (t + 1) * LANES])

        return tile

    fields = []
    for number, group in enumerate(groups):
        fields += [times(s) for s in group]
        if number == 0:
            fields.append(cost)
    for at, field in enumerate(fields):
        window(field, at)
    bases, base = [], 0
    for number, group in enumerate(groups):
        for _ in range(len(group) + (number == 0)):
            bases.append(base)
            base += chunk
        if number == 0:
            meta_at = base
            base += 1

    for j, masks, order in spread(chunk):
        for at in range(len(fields)):
            def convert(w, carry, at=at):
                for half in range(0, rows, 8):
                    mixed = plain[w, at, 0, half : half + 8]
                    for t, mask in enumerate(masks):
                        mixed = jnp.where(mask, plain[w, at, t + 1, half : half + 8], mixed)
                    cut[w, bases[at] + j, half : half + 8] = gather_lanes(mixed, order)
                return carry

            lax.fori_loop(0, PLANE, convert, 0)

    owner = owner_ref[...].astype(jnp.float32)
    across = jnp.broadcast_to(owner, (LANES, LANES))
    down = jnp.transpose(across)
    earlier = lax.broadcasted_iota(jnp.int32, (LANES, LANES), 0) < lax.broadcasted_iota(
        jnp.int32, (LANES, LANES), 1
    )
    rank = jnp.sum(jnp.where(earlier & (across == down), 1.0, 0.0), axis=0, keepdims=True)
    cell = cell_ref[...].astype(jnp.float32)
    line = jnp.floor(cell / width)
    column = cell - line * width
    part = jnp.floor(column / own)
    column = column - part * own
    spot = jnp.floor((column + 0.5) / chunk)
    place = (part * chunk + (column - spot * chunk)) * rows + line
    filler = jnp.zeros((rows - 4, LANES), jnp.float32)
    meta = jnp.concatenate([place, spot, owner, rank, filler], axis=0)
    for w in range(PLANE):
        cut[w, meta_at] = meta

    copies = []
    start = 0
    for number in range(len(groups)):
        for j in range(PLANE):
            out = outs[number * PLANE + j]
            size = out.shape[0]
            copies.append(
                pltpu.make_async_copy(
                    cut.at[member ^ j, start : start + size], out, sem.at[number * PLANE + j]
                )
            )
        start += size
    run_copies(copies)


def edge_kernel(slabs, halo, p0, p1, p2, p3, even_ref, odd_ref, full, sem):
    member, plane, _ = here()
    rows = p0.shape[1]
    total = PLANE * rows
    run_copies(
        [
            pltpu.make_async_copy(
                p.at[0:slabs], full.at[:, pl.ds(pl.multiple_of((member ^ j) * rows, 8), rows)], sem.at[j]
            )
            for j, p in enumerate((p0, p1, p2, p3))
        ]
    )
    parity = lax.rem(plane, 2)
    low = pl.multiple_of((1 - parity) * (total - halo), 8)
    high = pl.multiple_of(parity * (total - halo), 8)
    run_copies(
        [
            pltpu.make_async_copy(full.at[:, pl.ds(low, halo)], even_ref, sem.at[0]),
            pltpu.make_async_copy(full.at[:, pl.ds(high, halo)], odd_ref, sem.at[1]),
        ]
    )


def relax_rows(src, dst, cost, count, tiles, start):
    def ends(field, reach):
        before = [pltpu.roll(field[tiles - k], 1, 1) for k in range(reach, 0, -1)]
        after = [pltpu.roll(field[k], LANES - 1, 1) for k in range(reach)]
        return before + field + after

    for s in range(count):
        near, one, two = [], [], []
        for t in range(tiles):
            at = s * tiles + t
            near.append(src[at, pl.ds(start, 8)])
            one.append(jnp.minimum(src[at, pl.ds(start - 1, 8)], src[at, pl.ds(start + 1, 8)]))
            two.append(jnp.minimum(src[at, pl.ds(start - 2, 8)], src[at, pl.ds(start + 2, 8)]))
        near, one, two = ends(near, 1), ends(one, 2), ends(two, 1)
        for t in range(tiles):
            m1 = jnp.minimum(one[t + 2], jnp.minimum(near[t], near[t + 2]))
            m2 = jnp.minimum(one[t + 1], one[t + 3])
            m5 = jnp.minimum(jnp.minimum(one[t], one[t + 4]), jnp.minimum(two[t], two[t + 2]))
            best = jnp.minimum(m1 + cost[0, t, pl.ds(start, 8)], m2 + cost[1, t, pl.ds(start, 8)])
            best = jnp.minimum(best, m5 + cost[2, t, pl.ds(start, 8)])
            dst[s * tiles + t, pl.ds(start, 8)] = jnp.minimum(near[t + 1], best)


def scale_cost(cost):
    def group(at, carry):
        spot = pl.ds(pl.multiple_of(at * 8, 8), 8)
        for t in range(cost.shape[1]):
            value = cost[0, t, spot]
            cost[1, t, spot] = root_two * value
            cost[2, t, spot] = root_five * value
        return carry

    lax.fori_loop(0, cost.shape[2] // 8, group, 0)


def run_sweeps(first, second, cost, count, tiles, sweeps):
    groups = (first.shape[1] - 2 * PAD) // 8

    def sweep(src, dst, number):
        low = (2 * number) // 8

        def group(at, carry):
            relax_rows(src, dst, cost, count, tiles, pl.multiple_of(PAD + at * 8, 8))
            return carry

        lax.fori_loop(low, groups - low, group, 0)

    def pair(at, carry):
        sweep(first, second, 2 * at + 1)
        sweep(second, first, 2 * at + 2)
        return carry

    lax.fori_loop(0, sweeps // 2, pair, 0)


def halo_copies(plane, halo, total, even, odd, dst, sem, slabs):
    parity = lax.rem(plane, 2)
    above, below = PAD, PAD + halo + total
    even_at = pl.multiple_of(parity * above + (1 - parity) * below, 8)
    odd_at = pl.multiple_of((1 - parity) * above + parity * below, 8)
    copies = [
        pltpu.make_async_copy(even.at[slabs], dst.at[:, pl.ds(even_at, halo)], sem.at[0]),
        pltpu.make_async_copy(odd.at[slabs], dst.at[:, pl.ds(odd_at, halo)], sem.at[1]),
    ]
    return copies, odd_at


def fence(plane, planes, odd_at, halo, field):
    @pl.when((plane == 0) | (plane == planes - 1))
    def _():
        for t in range(field.shape[0]):
            field[t, pl.ds(odd_at, halo)] = jnp.full((halo, LANES), far_value, jnp.float32)


def first_kernel(count, sweeps, has_cost, planes, p0, p1, p2, p3, even, odd, *rest):
    if has_cost:
        state, low_ref, high_ref, cost_out, one, two, cost, sem = rest
    else:
        cost_in, state, low_ref, high_ref, one, two, cost, sem = rest
    member, plane, _ = here()
    rows, halo = p0.shape[1], even.shape[1]
    total = PLANE * rows
    tiles = cost.shape[1]
    size = count * tiles
    base = cost.at[0]
    copies = [
        pltpu.make_async_copy(
            p.at[0:size],
            one.at[:, pl.ds(pl.multiple_of(PAD + halo + (member ^ j) * rows, 8), rows)],
            sem.at[4 + j],
        )
        for j, p in enumerate((p0, p1, p2, p3))
    ]
    halos, odd_at = halo_copies(plane, halo, total, even, odd, one, sem, slice(0, size))
    copies += halos
    if has_cost:
        more, _ = halo_copies(
            plane, halo, total, even, odd, base, sem.at[pl.ds(2, 2)], slice(size, size + tiles)
        )
        copies += more
        copies += [
            pltpu.make_async_copy(
                p.at[size : size + tiles],
                base.at[:, pl.ds(pl.multiple_of(PAD + halo + (member ^ j) * rows, 8), rows)],
                sem.at[8 + j],
            )
            for j, p in enumerate((p0, p1, p2, p3))
        ]
    else:
        copies.append(pltpu.make_async_copy(cost_in, cost, sem.at[8]))
    run_copies(copies)
    fence(plane, planes, odd_at, halo, one)
    if has_cost:
        fence(plane, planes, odd_at, halo, base)
        scale_cost(cost)
    run_sweeps(one, two, cost, count, tiles, sweeps)
    parity = lax.rem(plane, 2)
    top, bottom = PAD + halo, PAD + halo + total - halo
    low = pl.multiple_of(parity * top + (1 - parity) * bottom, 8)
    high = pl.multiple_of((1 - parity) * top + parity * bottom, 8)
    copies = [
        pltpu.make_async_copy(one.at[:, pl.ds(low, halo)], low_ref, sem.at[0]),
        pltpu.make_async_copy(one.at[:, pl.ds(high, halo)], high_ref, sem.at[1]),
        pltpu.make_async_copy(one.at[:, PAD + halo : PAD + halo + total], state, sem.at[2]),
    ]
    if has_cost:
        copies.append(pltpu.make_async_copy(cost, cost_out, sem.at[3]))
    run_copies(copies)


def last_kernel(count, sweeps, is_last, planes, cap, state, even, odd, cost_in, m0, m1, m2, m3, *rest):
    if is_last:
        partial_ref, earlier_ref, placed_ref, r0, r1, r2, r3, one, two, cost, meta, best, plain, sem = rest
    else:
        placed_ref, best, one, two, cost, meta, sem = rest
    member, plane, _ = here()
    total, halo = state.shape[1], even.shape[1]
    rows = total // PLANE
    tiles = cost.shape[1]
    own = tiles - 1
    copies = [
        pltpu.make_async_copy(state, one.at[:, PAD + halo : PAD + halo + total], sem.at[2]),
        pltpu.make_async_copy(cost_in, cost, sem.at[3]),
    ]
    copies += [
        pltpu.make_async_copy(m.at[m.shape[0] - 1], meta.at[member ^ j], sem.at[4 + j])
        for j, m in enumerate((m0, m1, m2, m3))
    ]
    halos, odd_at = halo_copies(plane, halo, total, even, odd, one, sem, slice(0, count * tiles))
    run_copies(copies + halos)
    fence(plane, planes, odd_at, halo, one)
    run_sweeps(one, two, cost, count, tiles, sweeps)

    for t in range(tiles):
        low = None
        for s in range(count):
            at = (s * tiles + t, slice(PAD + halo, PAD + halo + total))
            each = jnp.minimum(one[at], jnp.float32(clip_value)) / clip_value
            one[at] = each
            low = each if low is None else jnp.minimum(low, each)
        best[t] = jnp.minimum(low, partial_ref[t]) if is_last else low
    copies = []
    if is_last:
        lane = lax.broadcasted_iota(jnp.int32, (8, LANES), 1)
        orders = [((lane + (LANES - j)) * inverse(tiles)) & (LANES - 1) for j in range(tiles)]
        chosen = [lax.rem(lane + t * LANES, tiles) for t in range(own)]

        def back(at, carry):
            spot = pl.ds(pl.multiple_of(at * 8, 8), 8)
            turned = [gather_lanes(best[j, spot], orders[j]) for j in range(tiles)]
            for t in range(own):
                value = turned[0]
                for j in range(1, tiles):
                    value = jnp.where(chosen[t] == j, turned[j], value)
                plain[t, spot] = value
            return carry

        lax.fori_loop(0, total // 8, back, 0)
        copies = [
            pltpu.make_async_copy(
                plain.at[:, pl.ds(pl.multiple_of((member ^ j) * rows, 8), rows)], r, sem.at[j]
            )
            for j, r in enumerate((r0, r1, r2, r3))
        ]
        for copy in copies:
            copy.start()

    def exact(pick, value):
        found = None
        for _ in range(3):
            part = value.astype(jnp.bfloat16)
            value = value - part.astype(jnp.float32)
            term = jnp.dot(pick, part, preferred_element_type=jnp.float32)
            found = term if found is None else found + term
        return found

    n, _, slots = placed_ref.shape
    height = tiles * rows
    lane = lax.broadcasted_iota(jnp.int32, (LANES, LANES), 1).astype(jnp.float32)
    place = lax.broadcasted_iota(jnp.int32, (LANES, height), 1).astype(jnp.float32)
    spot = lax.broadcasted_iota(jnp.int32, (LANES, slots), 1).astype(jnp.float32)
    device = lax.broadcasted_iota(jnp.int32, (n, LANES), 0).astype(jnp.float32)
    filler = jnp.zeros((LANES - meta.shape[1], LANES), jnp.float32)
    offset = (member * height).astype(jnp.float32)
    totals = [None] * count
    for q in range(PLANE):
        turned = jnp.transpose(jnp.concatenate([meta[q], filler], axis=0))
        pick = jnp.where(turned[:, 0:1] - offset == place, 1.0, 0.0).astype(jnp.bfloat16)
        at_lane = turned[:, 1:2] == lane
        base = ((plane * PLANE + q) * cap).astype(jnp.float32)
        at_slot = turned[:, 3:4] + base == spot
        to_owner = jnp.where(meta[q, 2:3] == device, 1.0, 0.0).astype(jnp.bfloat16)
        for s in range(count):
            block = one[s * tiles : (s + 1) * tiles, PAD + halo + q * rows : PAD + halo + (q + 1) * rows]
            found = exact(pick, block.reshape(height, LANES))
            value = jnp.sum(jnp.where(at_lane, found, 0.0), axis=1, keepdims=True)
            term = exact(to_owner, jnp.where(at_slot, value, 0.0))
            totals[s] = term if totals[s] is None else totals[s] + term
    if is_last:
        placed_ref[:, 0:count] = earlier_ref[...]
        for s in range(count):
            placed_ref[:, count + s] = totals[s]
    else:
        for s in range(count):
            placed_ref[:, s] = totals[s]
    for copy in copies:
        copy.wait()


def join_kernel(r0, r1, r2, r3, gauge_ref, out_ref, result_ref):
    member, _, _ = here()
    tiles, rows, _ = r0.shape
    for j, r in enumerate((r0, r1, r2, r3)):
        base = (member ^ j) * (tiles * LANES)
        for t in range(tiles):
            out_ref[:, pl.ds(pl.multiple_of(base + t * LANES, LANES), LANES)] = r[t]
    result_ref[0] = jnp.sum(gauge_ref[...], axis=0)


def shape_of(*dims):
    return jax.ShapeDtypeStruct(dims, jnp.float32)


def on_device(slowness, ocean, start_times, source_cells, gauge_cells, gauge_owner):
    axis = "space"
    index = lax.axis_index(axis)
    n = lax.axis_size(axis)
    rows, width = slowness.shape
    sources = start_times.shape[0]
    gauges = gauge_cells.shape[0]
    planes = n // PLANE
    assert n % (2 * PLANE) == 0 and width % (PLANE * LANES) == 0
    assert gauges == LANES and rows * (width // PLANE) == LANES * LANES and sources % 2 == 0
    sweeps = SWEEPS * BLOCKS // ROUNDS
    halo = 2 * sweeps
    total = rows * PLANE
    tiles = width // PLANE // LANES + 1
    assert 2 * SWEEPS * BLOCKS <= SIDE and halo <= total and sweeps % 2 == 0 and halo % 8 == 0
    cap = max(2, 2 * gauges // n)
    half = sources // 2
    groups = (tuple(range(half)), tuple(range(half, sources)))
    limit = pltpu.CompilerParams(vmem_limit_bytes=VMEM_BYTES)

    sizes = [half * tiles + tiles + 1, half * tiles]
    packed = pl.pallas_call(
        functools.partial(pack_kernel, groups, cap),
        out_shape=[shape_of(size, rows, LANES) for size in sizes for _ in range(PLANE)],
        in_specs=[SMEM, VMEM, VMEM, VMEM, VMEM, VMEM],
        out_specs=[ANY] * (2 * PLANE),
        scratch_shapes=[
            pltpu.VMEM((PLANE, sources + 1, tiles, rows, LANES), jnp.float32),
            pltpu.VMEM((PLANE, sum(sizes), rows, LANES), jnp.float32),
            pltpu.SemaphoreType.DMA((2 * PLANE,)),
        ],
        name="pack",
        compiler_params=limit,
    )(
        source_cells,
        slowness,
        ocean,
        start_times,
        gauge_cells.reshape(1, gauges),
        gauge_owner.reshape(1, gauges),
    )

    def swap(x, j):
        return lax.ppermute(x, axis, [(d, d ^ j) for d in range(n)])

    def swap_planes(even, odd):
        pairs_even = [(d, (d // PLANE ^ 1) * PLANE + d % PLANE) for d in range(n)]
        pairs_odd = [
            (d, (((d // PLANE + 1) ^ 1) - 1) * PLANE + d % PLANE)
            for d in range(PLANE, n - PLANE)
        ]
        return lax.ppermute(even, axis, pairs_even), lax.ppermute(odd, axis, pairs_odd)

    pieces = [
        [packed[k * PLANE]] + [swap(packed[k * PLANE + j], j) for j in range(1, PLANE)]
        for k in range(2)
    ]
    halos = []
    for k in range(2):
        slabs = half * tiles + (tiles if k == 0 else 0)
        even, odd = pl.pallas_call(
            functools.partial(edge_kernel, slabs, halo),
            out_shape=[shape_of(slabs, halo, LANES)] * 2,
            in_specs=[ANY] * 4,
            out_specs=[ANY] * 2,
            compiler_params=limit,
            scratch_shapes=[
                pltpu.VMEM((slabs, total, LANES), jnp.float32),
                pltpu.SemaphoreType.DMA((PLANE,)),
            ],
            name=f"edge{k}",
        )(*pieces[k])
        halos.append(swap_planes(even, odd))

    deep = total + 2 * halo + 2 * PAD
    size = half * tiles
    scratch = [
        pltpu.VMEM((size, deep, LANES), jnp.float32),
        pltpu.VMEM((size, deep, LANES), jnp.float32),
        pltpu.VMEM((3, tiles, deep, LANES), jnp.float32),
    ]
    states, later = [], []
    cost = None
    for k in range(2):
        outs = pl.pallas_call(
            functools.partial(first_kernel, half, sweeps, k == 0, planes),
            out_shape=[shape_of(size, total, LANES)]
            + [shape_of(size, halo, LANES)] * 2
            + ([shape_of(3, tiles, deep, LANES)] if k == 0 else []),
            in_specs=[ANY] * (6 if k == 0 else 7),
            compiler_params=limit,
            out_specs=[ANY] * (4 if k == 0 else 3),
            scratch_shapes=scratch + [pltpu.SemaphoreType.DMA((12,))],
            name=f"first{k}",
        )(*pieces[k], *halos[k], *([] if k == 0 else [cost]))
        if k == 0:
            cost = outs[3]
        states.append(outs[0])
        later.append(swap_planes(outs[1], outs[2]))

    slots = n * cap
    partial, placed = None, None
    for k in range(2):
        is_last = k == 1
        out_shape = [shape_of(n, half * (k + 1), slots)]
        out_specs = [VMEM]
        more = [pltpu.VMEM((PLANE, rows, LANES), jnp.float32)]
        if is_last:
            out_shape += [shape_of(tiles - 1, rows, LANES)] * PLANE
            out_specs += [ANY] * PLANE
            more.append(pltpu.VMEM((tiles, total, LANES), jnp.float32))
            more.append(pltpu.VMEM((tiles - 1, total, LANES), jnp.float32))
        else:
            out_shape.append(shape_of(tiles, total, LANES))
            out_specs.append(VMEM)
        outs = pl.pallas_call(
            functools.partial(last_kernel, half, sweeps, is_last, planes, cap),
            out_shape=out_shape,
            in_specs=[ANY] * 8 + ([VMEM, VMEM] if is_last else []),
            out_specs=out_specs,
            scratch_shapes=scratch + more + [pltpu.SemaphoreType.DMA((8,))],
            compiler_params=limit,
            name=f"last{k}",
        )(states[k], *later[k], cost, *pieces[0], *([partial, placed] if is_last else []))
        placed = outs[0]
        if is_last:
            returned = outs[1:]
        else:
            partial = outs[1]

    back = [returned[0]] + [swap(returned[j], j) for j in range(1, PLANE)]
    received = lax.all_to_all(placed, axis, split_axis=0, concat_axis=0, tiled=True)
    return pl.pallas_call(
        join_kernel,
        out_shape=(shape_of(rows, width), shape_of(1, sources, slots)),
        in_specs=[VMEM] * (PLANE + 1),
        out_specs=(VMEM, VMEM),
        compiler_params=limit,
        name="join",
    )(*back, received)


def solution(mesh):
    return jax.shard_map(
        on_device,
        mesh=mesh,
        in_specs=(
            P(("groups", "space"), None),
            P(("groups", "space"), None),
            P("groups", "space", None),
            P("groups"),
            P(("groups", "space")),
            P(("groups", "space"), None),
        ),
        out_specs=(P(("groups", "space"), None), P(("groups", "space"), None, None)),
        check_vma=False,
    )
```

time: 198 us -> 135 us (0.68)
  Pallas kernels: 141 us -> 82.6 us
  blocking collectives: 11.1 us -> 0 us
  waiting for transfers between devices: 9.37 us -> 19.6 us
  local copies, waits for them, and re-layouts: 9.17 us -> 5.08 us
  starting transfers between devices: 23.1 us -> 26.1 us
  other arithmetic: 2.06 us -> 0 us
    pallas_call x2, Pallas kernels: 65 us -> 29.7 us  [on_device(): pl.pallas_call(functools.partial(first_kernel, half, sweeps, k == 0, plan...]
    pallas_call x2, Pallas kernels: 66.3 us -> 35.3 us  [on_device(): pl.pallas_call(functools.partial(last_kernel, half, sweeps, is_last, plan...]
    pallas_call x1, Pallas kernels: 2.76 us -> 16.4 us  [on_device(): pl.pallas_call(functools.partial(pack_kernel, groups, cap), out_shape=[sh...]
    all_to_all x1 -> x0, blocking collectives: 11.1 us -> none  [on_device(): lax.all_to_all(sent, axis, split_axis=0, concat_axis=0, tiled=True)]
    ppermute x9, waiting for transfers between devices: 9.35 us -> 16.8 us  [swap(): return lax.ppermute(x, axis, [(d, d ^ j) for d in range(n)])]
    pallas_call x2, Pallas kernels: 5.38 us -> 0.39 us  [on_device(): pl.pallas_call(functools.partial(edge_kernel, slabs, halo), out_shape=[sh...]
    all_to_all x0 -> x1, starting transfers between devices: none -> 4.92 us  [on_device(): lax.all_to_all(placed, axis, split_axis=0, concat_axis=0, tiled=True)]
    ppermute x4, waiting for transfers between devices: 0.01 us -> 2.26 us  [swap_planes(): lax.ppermute(even, axis, pairs_even)]
  transfers between devices with their start and end apart: 17 -> 18, of which waited for: 3 -> 8; matrix products, arithmetic and copies ran while one was open for 2% -> 0% of each run, Pallas kernels for 52% -> 35%
where the time goes in v2:
time: 135 us; the launch traced here: 134 us
  Pallas kernels  82.6 us (61%)
  starting transfers between devices  26.1 us (19%)
  waiting for transfers between devices  19.6 us (15%)
  local copies, waits for them, and re-layouts  5.08 us (4%)
    pallas_call x2, Pallas kernels, on_device(): pl.pallas_call(functools.partial(last_kernel, half, sweeps, is_last, plan...  35.3 us
    pallas_call x2, Pallas kernels, on_device(): pl.pallas_call(functools.partial(first_kernel, half, sweeps, k == 0, plan...  29.7 us
    ppermute x9, waiting for transfers between devices, swap(): return lax.ppermute(x, axis, [(d, d ^ j) for d in range(n)])  16.8 us
    pallas_call x1, Pallas kernels, on_device(): pl.pallas_call(functools.partial(pack_kernel, groups, cap), out_shape=[sh...  16.4 us
    ppermute x4, starting transfers between devices, swap_planes(): lax.ppermute(even, axis, pairs_even)  11.2 us
    ppermute x9, starting transfers between devices, swap(): return lax.ppermute(x, axis, [(d, d ^ j) for d in range(n)])  7.33 us
    unnamed x12, local copies, waits for them, and re-layouts  5.08 us
    all_to_all x1, starting transfers between devices, on_device(): lax.all_to_all(placed, axis, split_axis=0, concat_axis=0, tiled=True)  4.92 us
  transfers between devices with their start and end apart: 18, of which 8 were waited for; matrix products, arithmetic and copies ran while one was open for 0% of the time, Pallas kernels for 35%

profile of v2, /device:TPU:0, one launch (start us, length us, event | category | flops | bytes accessed | tf_op | source)
XLA Modules:
  0.0 134.2 jit_solution(14393882502865464597)
XLA Ops:
  0.6 1.2 copy-done
  1.9 0.9 copy-done.1
  2.8 0.9 copy-done.2
  3.8 0.7 copy-done.3
  4.4 0.7 copy-done.4
  5.1 0.7 copy-done.5
  5.7 16.4 %pack.1 = (f32[28,16,128]{2,1,0:T(8,128)S(1)}, f32[28,16,128]{2,1,0:T(8,128)S(1)}, f32[28,16,128]{2,1,0:T(8,128)S(1)}, f32[28,16,128]{2,1,0:T(8,128)S(1)}, f32[1...) custom-call(s32[4]{0:T(128)S(1)} %copy-done.3, ...), custom_call_target="tpu_custom_call" | custom-call | tf_op jit(solution)/shard_map/pack/pallas_call | solution.py:440
  22.1 0.6 collective-permute-start.5
  22.7 2.6 %collective-permute-start.6 = (f32[28,16,128]{2,1,0:T(8,128)S(1)}, f32[28,16,128]{2,1,0:T(8,128)S(1)}, u32[]{:S(2)}, u32[]{:S(2)}) collective-permute-start(f32[28,16,128]{2,1,0:T(8,128)S(1)} %get-tuple-element.36), channel_id=1, source_target_pairs={{0,2},{1,3},{2,0},{3,1},{4,6},{5,7},{6,4},{7,5},{8,10},{9,11},{10,... | collective-permute-start | bytes 688136 | tf_op jit(solution)/shard_map/ppermute | solution.py:462
  25.4 1.9 %collective-permute-start.1 = (f32[18,16,128]{2,1,0:T(8,128)S(1)}, f32[18,16,128]{2,1,0:T(8,128)S(1)}, u32[]{:S(2)}, u32[]{:S(2)}) collective-permute-start(f32[18,16,128]{2,1,0:T(8,128)S(1)} %get-tuple-element.30), channel_id=1, source_target_pairs={{0,2},{1,3},{2,0},{3,1},{4,6},{5,7},{6,4},{7,5},{8,10},{9,11},{10,... | collective-permute-start | bytes 442376 | tf_op jit(solution)/shard_map/ppermute | solution.py:462
  27.4 4.3 %collective-permute-done.6.p2.m2 = f32[28,16,128]{2,1,0:T(8,128)S(1)} collective-permute-done((f32[28,16,128]{2,1,0:T(8,128)S(1)}, f32[28,16,128]{2,1,0:T(8,128)S(1)}, u32[]{:S(2)}, u32[]{:S(2)}) %collective-permute-start.6) | collective-permute-done | bytes 229408 | tf_op jit(solution)/shard_map/ppermute | solution.py:462
  31.7 4.5 %collective-permute-done.7.p3.m3 = f32[28,16,128]{2,1,0:T(8,128)S(1)} collective-permute-done((f32[28,16,128]{2,1,0:T(8,128)S(1)}, f32[28,16,128]{2,1,0:T(8,128)S(1)}, u32[]{:S(2)}, u32[]{:S(2)}) %collective-permute-start.7) | collective-permute-done | bytes 229408 | tf_op jit(solution)/shard_map/ppermute | solution.py:462
  36.4 1.6 %collective-permute-start.8 = (f32[27,24,128]{2,1,0:T(8,128)S(1)}, f32[27,24,128]{2,1,0:T(8,128)S(1)}, u32[]{:S(2)}, u32[]{:S(2)}) collective-permute-start(f32[27,24,128]{2,1,0:T(8,128)S(1)} %get-tuple-element.38), channel_id=1, source_target_pairs={{0,4},{1,5},{2,6},{3,7},{4,0},{5,1},{6,2},{7,3},{8,12},{9,13},{10,... | collective-permute-start | bytes 995336 | tf_op jit(solution)/shard_map/ppermute | solution.py:470
  38.0 0.7 collective-permute-start.9
  38.7 1.1 collective-permute-done.1.p2
  39.8 2.6 %collective-permute-done.2.p3 = f32[18,16,128]{2,1,0:T(8,128)S(1)} collective-permute-done((f32[18,16,128]{2,1,0:T(8,128)S(1)}, f32[18,16,128]{2,1,0:T(8,128)S(1)}, u32[]{:S(2)}, u32[]{:S(2)}) %collective-permute-start.2) | collective-permute-done | bytes 147488 | tf_op jit(solution)/shard_map/ppermute | solution.py:462
  42.6 1.6 %collective-permute-start.3 = (f32[18,24,128]{2,1,0:T(8,128)S(1)}, f32[18,24,128]{2,1,0:T(8,128)S(1)}, u32[]{:S(2)}, u32[]{:S(2)}) collective-permute-start(f32[18,24,128]{2,1,0:T(8,128)S(1)} %get-tuple-element.32), channel_id=1, source_target_pairs={{0,4},{1,5},{2,6},{3,7},{4,0},{5,1},{6,2},{7,3},{8,12},{9,13},{10,... | collective-permute-start | bytes 663560 | tf_op jit(solution)/shard_map/ppermute | solution.py:470
  44.2 0.7 collective-permute-start.4
  44.9 2.3 %collective-permute-done.8.even = f32[27,24,128]{2,1,0:T(8,128)S(1)} collective-permute-done((f32[27,24,128]{2,1,0:T(8,128)S(1)}, f32[27,24,128]{2,1,0:T(8,128)S(1)}, u32[]{:S(2)}, u32[]{:S(2)}) %collective-permute-start.8) | collective-permute-done | bytes 331808 | tf_op jit(solution)/shard_map/ppermute | solution.py:470
  47.1 15.0 %first0.1 = (f32[18,64,128]{2,1,0:T(8,128)S(1)}, f32[18,24,128]{2,1,0:T(8,128)S(1)}, f32[18,24,128]{2,1,0:T(8,128)S(1)}, f32[3,9,128,128]{3,2,1,0:T(8,128)S(1)}) custom-call(f32[28,16,128]{2,1,0:T(8,128)S(1)} %get-tuple-element.34.p0.m0, f32[28,16,128]{2,1,0:T(8,128)S(1)} %collective-permute-done.5.p1.m1, f32[28,16,128]{2,1,0:T(8,128)S(1)} %collective-permute-done.6.p2.m2, ...), custom_call_target="tpu_custom_call" | custom-call | tf_op jit(solution)/shard_map/first0/pallas_call | solution.py:503
  62.1 4.6 %collective-permute-start.12 = (f32[18,24,128]{2,1,0:T(8,128)S(1)}, f32[18,24,128]{2,1,0:T(8,128)S(1)}, u32[]{:S(2)}, u32[]{:S(2)}) collective-permute-start(f32[18,24,128]{2,1,0:T(8,128)S(1)} %get-tuple-element.45), channel_id=1, source_target_pairs={{0,4},{1,5},{2,6},{3,7},{4,0},{5,1},{6,2},{7,3},{8,12},{9,13},{10,... | collective-permute-start | bytes 663560 | tf_op jit(solution)/shard_map/ppermute | solution.py:470
  66.8 0.7 collective-permute-start.13
  67.5 14.7 %first1.1 = (f32[18,64,128]{2,1,0:T(8,128)S(1)}, f32[18,24,128]{2,1,0:T(8,128)S(1)}, f32[18,24,128]{2,1,0:T(8,128)S(1)}) custom-call(f32[18,16,128]{2,1,0:T(8,128)S(1)} %get-tuple-element.28.p0, f32[18,16,128]{2,1,0:T(8,128)S(1)} %collective-permute-done.p1, f32[18,16,128]{2,1,0:T(8,128)S(1)} %collective-permute-done.1.p2, ...), custom_call_target="tpu_custom_call" | custom-call | tf_op jit(solution)/shard_map/first1/pallas_call | solution.py:503
  82.2 3.3 %collective-permute-start.10 = (f32[18,24,128]{2,1,0:T(8,128)S(1)}, f32[18,24,128]{2,1,0:T(8,128)S(1)}, u32[]{:S(2)}, u32[]{:S(2)}) collective-permute-start(f32[18,24,128]{2,1,0:T(8,128)S(1)} %get-tuple-element.42), channel_id=1, source_target_pairs={{0,4},{1,5},{2,6},{3,7},{4,0},{5,1},{6,2},{7,3},{8,12},{9,13},{10,... | collective-permute-start | bytes 663560 | tf_op jit(solution)/shard_map/ppermute | solution.py:470
  85.5 0.7 collective-permute-start.11
  86.2 16.9 %last0.1 = (f32[16,2,256]{2,1,0:T(2,128)S(1)}, f32[9,64,128]{2,1,0:T(8,128)S(1)}) custom-call(f32[18,64,128]{2,1,0:T(8,128)S(1)} %get-tuple-element.44.state, f32[18,24,128]{2,1,0:T(8,128)S(1)} %collective-permute-done.12.even, f32[18,24,128]{2,1,0:T(8,128)S(1)} %collective-permute-done.13.odd, f32[3,9,128,128]{3,2,1,0:T(8,128)S(1)} %get-tuple-element.40.rest_0_.cost_in, ...), custom_call_target="tpu_custom_call" | custom-call | tf_op jit(solution)/shard_map/last0/pallas_call | solution.py:534
  103.2 18.4 %last1.1 = (f32[16,4,256]{2,1,0:T(4,128)}, f32[8,16,128]{2,1,0:T(8,128)S(1)}, f32[8,16,128]{2,1,0:T(8,128)S(1)}, f32[8,16,128]{2,1,0:T(8,128)S(1)}, f32[8,16,128]{2,1,0:T(8,128)S(1)}) custom-call(f32[18,64,128]{2,1,0:T(8,128)S(1)} %get-tuple-element.41.state, f32[18,24,128]{2,1,0:T(8,128)S(1)} %collective-permute-done.10.even, ...), custom_call_target="tpu_custom_call" | custom-call | tf_op jit(solution)/shard_map/last1/pallas_call | solution.py:534
  121.6 4.9 %all-to-all-start = ((f32[16,4,256]{2,1,0:T(4,128)}), f32[16,4,256]{2,1,0:T(4,128)S(1)}, u32[]{:S(2)}, u32[]{:S(2)}) async-start(f32[16,4,256]{2,1,0:T(4,128)} %get-tuple-element.53), calls=%async_computation | async-start | bytes 131072 | tf_op jit(solution)/shard_map/all_to_all | solution.py:550
  126.9 1.6 %collective-permute-start.15 = (f32[8,16,128]{2,1,0:T(8,128)S(1)}, f32[8,16,128]{2,1,0:T(8,128)S(1)}, u32[]{:S(2)}, u32[]{:S(2)}) collective-permute-start(f32[8,16,128]{2,1,0:T(8,128)S(1)} %get-tuple-element.51), channel_id=1, source_target_pairs={{0,2},{1,3},{2,0},{3,1},{4,6},{5,7},{6,4},{7,5},{8,10},{9,11},{10,... | collective-permute-start | bytes 196616 | tf_op jit(solution)/shard_map/ppermute | solution.py:462
  128.6 2.9 %collective-permute-done.15.r2 = f32[8,16,128]{2,1,0:T(8,128)S(1)} collective-permute-done((f32[8,16,128]{2,1,0:T(8,128)S(1)}, f32[8,16,128]{2,1,0:T(8,128)S(1)}, u32[]{:S(2)}, u32[]{:S(2)}) %collective-permute-start.15) | collective-permute-done | bytes 65568 | tf_op jit(solution)/shard_map/ppermute | solution.py:462
  131.5 1.4 %collective-permute-done.16.r3 = f32[8,16,128]{2,1,0:T(8,128)S(1)} collective-permute-done((f32[8,16,128]{2,1,0:T(8,128)S(1)}, f32[8,16,128]{2,1,0:T(8,128)S(1)}, u32[]{:S(2)}, u32[]{:S(2)}) %collective-permute-start.16) | collective-permute-done | bytes 65568 | tf_op jit(solution)/shard_map/ppermute | solution.py:462
  133.4 0.7 join.1
  (24 shorter events, 1.5 us)
Async XLA Ops:
  0.6 1.2 copy-start
  1.9 0.9 copy-start.1
  2.8 0.9 copy-start.2
  3.8 0.7 copy-start.3
  4.4 0.7 copy-start.4
  5.1 0.7 copy-start.5
  22.1 5.3 %collective-permute-start.5 = (f32[28,16,128]{2,1,0:T(8,128)S(1)}, f32[28,16,128]{2,1,0:T(8,128)S(1)}, u32[]{:S(2)}, u32[]{:S(2)}) collective-permute-start(f32[28,16,128]{2,1,0:T(8,128)S(1)} %get-tuple-element.35), channel_id=1, source_target_pairs={{0,1},{1,0},{2,3},{3,2},{4,5},{5,4},{6,7},{7,6},{8,9},{9,8},{10,11... | collective-permute-start | bytes 688136 | tf_op jit(solution)/shard_map/ppermute | solution.py:462
  22.7 9.0 %collective-permute-start.6 = (f32[28,16,128]{2,1,0:T(8,128)S(1)}, f32[28,16,128]{2,1,0:T(8,128)S(1)}, u32[]{:S(2)}, u32[]{:S(2)}) collective-permute-start(f32[28,16,128]{2,1,0:T(8,128)S(1)} %get-tuple-element.36), channel_id=1, source_target_pairs={{0,2},{1,3},{2,0},{3,1},{4,6},{5,7},{6,4},{7,5},{8,10},{9,11},{10,... | collective-permute-start | bytes 688136 | tf_op jit(solution)/shard_map/ppermute | solution.py:462
  25.2 10.9 %collective-permute-start.7 = (f32[28,16,128]{2,1,0:T(8,128)S(1)}, f32[28,16,128]{2,1,0:T(8,128)S(1)}, u32[]{:S(2)}, u32[]{:S(2)}) collective-permute-start(f32[28,16,128]{2,1,0:T(8,128)S(1)} %get-tuple-element.37), channel_id=1, source_target_pairs={{0,3},{1,2},{2,1},{3,0},{4,7},{5,6},{6,5},{7,4},{8,11},{9,10},{10,... | collective-permute-start | bytes 688136 | tf_op jit(solution)/shard_map/ppermute | solution.py:462
  25.3 13.4 %collective-permute-start = (f32[18,16,128]{2,1,0:T(8,128)S(1)}, f32[18,16,128]{2,1,0:T(8,128)S(1)}, u32[]{:S(2)}, u32[]{:S(2)}) collective-permute-start(f32[18,16,128]{2,1,0:T(8,128)S(1)} %get-tuple-element.29), channel_id=1, source_target_pairs={{0,1},{1,0},{2,3},{3,2},{4,5},{5,4},{6,7},{7,6},{8,9},{9,8},{10,11... | collective-permute-start | bytes 442376 | tf_op jit(solution)/shard_map/ppermute | solution.py:462
  25.4 14.3 %collective-permute-start.1 = (f32[18,16,128]{2,1,0:T(8,128)S(1)}, f32[18,16,128]{2,1,0:T(8,128)S(1)}, u32[]{:S(2)}, u32[]{:S(2)}) collective-permute-start(f32[18,16,128]{2,1,0:T(8,128)S(1)} %get-tuple-element.30), channel_id=1, source_target_pairs={{0,2},{1,3},{2,0},{3,1},{4,6},{5,7},{6,4},{7,5},{8,10},{9,11},{10,... | collective-permute-start | bytes 442376 | tf_op jit(solution)/shard_map/ppermute | solution.py:462
  27.4 15.0 %collective-permute-start.2 = (f32[18,16,128]{2,1,0:T(8,128)S(1)}, f32[18,16,128]{2,1,0:T(8,128)S(1)}, u32[]{:S(2)}, u32[]{:S(2)}) collective-permute-start(f32[18,16,128]{2,1,0:T(8,128)S(1)} %get-tuple-element.31), channel_id=1, source_target_pairs={{0,3},{1,2},{2,1},{3,0},{4,7},{5,6},{6,5},{7,4},{8,11},{9,10},{10,... | collective-permute-start | bytes 442376 | tf_op jit(solution)/shard_map/ppermute | solution.py:462
  36.4 10.7 %collective-permute-start.8 = (f32[27,24,128]{2,1,0:T(8,128)S(1)}, f32[27,24,128]{2,1,0:T(8,128)S(1)}, u32[]{:S(2)}, u32[]{:S(2)}) collective-permute-start(f32[27,24,128]{2,1,0:T(8,128)S(1)} %get-tuple-element.38), channel_id=1, source_target_pairs={{0,4},{1,5},{2,6},{3,7},{4,0},{5,1},{6,2},{7,3},{8,12},{9,13},{10,... | collective-permute-start | bytes 995336 | tf_op jit(solution)/shard_map/ppermute | solution.py:470
  38.0 9.1 %collective-permute-start.9 = (f32[27,24,128]{2,1,0:T(8,128)S(1)}, f32[27,24,128]{2,1,0:T(8,128)S(1)}, u32[]{:S(2)}, u32[]{:S(2)}) collective-permute-start(f32[27,24,128]{2,1,0:T(8,128)S(1)} %get-tuple-element.39), channel_id=1, source_target_pairs={{4,8},{5,9},{6,10},{7,11},{8,4},{9,5},{10,6},{11,7},{20,24},{21,25... | collective-permute-start | bytes 995336 | tf_op jit(solution)/shard_map/ppermute | solution.py:470
  42.6 24.8 %collective-permute-start.3 = (f32[18,24,128]{2,1,0:T(8,128)S(1)}, f32[18,24,128]{2,1,0:T(8,128)S(1)}, u32[]{:S(2)}, u32[]{:S(2)}) collective-permute-start(f32[18,24,128]{2,1,0:T(8,128)S(1)} %get-tuple-element.32), channel_id=1, source_target_pairs={{0,4},{1,5},{2,6},{3,7},{4,0},{5,1},{6,2},{7,3},{8,12},{9,13},{10,... | collective-permute-start | bytes 663560 | tf_op jit(solution)/shard_map/ppermute | solution.py:470
  44.2 23.3 %collective-permute-start.4 = (f32[18,24,128]{2,1,0:T(8,128)S(1)}, f32[18,24,128]{2,1,0:T(8,128)S(1)}, u32[]{:S(2)}, u32[]{:S(2)}) collective-permute-start(f32[18,24,128]{2,1,0:T(8,128)S(1)} %get-tuple-element.33), channel_id=1, source_target_pairs={{4,8},{5,9},{6,10},{7,11},{8,4},{9,5},{10,6},{11,7},{20,24},{21,25... | collective-permute-start | bytes 663560 | tf_op jit(solution)/shard_map/ppermute | solution.py:470
  62.1 24.1 %collective-permute-start.12 = (f32[18,24,128]{2,1,0:T(8,128)S(1)}, f32[18,24,128]{2,1,0:T(8,128)S(1)}, u32[]{:S(2)}, u32[]{:S(2)}) collective-permute-start(f32[18,24,128]{2,1,0:T(8,128)S(1)} %get-tuple-element.45), channel_id=1, source_target_pairs={{0,4},{1,5},{2,6},{3,7},{4,0},{5,1},{6,2},{7,3},{8,12},{9,13},{10,... | collective-permute-start | bytes 663560 | tf_op jit(solution)/shard_map/ppermute | solution.py:470
  66.8 19.4 %collective-permute-start.13 = (f32[18,24,128]{2,1,0:T(8,128)S(1)}, f32[18,24,128]{2,1,0:T(8,128)S(1)}, u32[]{:S(2)}, u32[]{:S(2)}) collective-permute-start(f32[18,24,128]{2,1,0:T(8,128)S(1)} %get-tuple-element.46), channel_id=1, source_target_pairs={{4,8},{5,9},{6,10},{7,11},{8,4},{9,5},{10,6},{11,7},{20,24},{21,25... | collective-permute-start | bytes 663560 | tf_op jit(solution)/shard_map/ppermute | solution.py:470
  82.2 21.0 %collective-permute-start.10 = (f32[18,24,128]{2,1,0:T(8,128)S(1)}, f32[18,24,128]{2,1,0:T(8,128)S(1)}, u32[]{:S(2)}, u32[]{:S(2)}) collective-permute-start(f32[18,24,128]{2,1,0:T(8,128)S(1)} %get-tuple-element.42), channel_id=1, source_target_pairs={{0,4},{1,5},{2,6},{3,7},{4,0},{5,1},{6,2},{7,3},{8,12},{9,13},{10,... | collective-permute-start | bytes 663560 | tf_op jit(solution)/shard_map/ppermute | solution.py:470
  85.5 17.6 %collective-permute-start.11 = (f32[18,24,128]{2,1,0:T(8,128)S(1)}, f32[18,24,128]{2,1,0:T(8,128)S(1)}, u32[]{:S(2)}, u32[]{:S(2)}) collective-permute-start(f32[18,24,128]{2,1,0:T(8,128)S(1)} %get-tuple-element.43), channel_id=1, source_target_pairs={{4,8},{5,9},{6,10},{7,11},{8,4},{9,5},{10,6},{11,7},{20,24},{21,25... | collective-permute-start | bytes 663560 | tf_op jit(solution)/shard_map/ppermute | solution.py:470
  121.6 11.8 %all-to-all-start = ((f32[16,4,256]{2,1,0:T(4,128)}), f32[16,4,256]{2,1,0:T(4,128)S(1)}, u32[]{:S(2)}, u32[]{:S(2)}) async-start(f32[16,4,256]{2,1,0:T(4,128)} %get-tuple-element.53), calls=%async_computation | async-start | bytes 131072 | tf_op jit(solution)/shard_map/all_to_all | solution.py:550
  126.5 2.0 %collective-permute-start.14 = (f32[8,16,128]{2,1,0:T(8,128)S(1)}, f32[8,16,128]{2,1,0:T(8,128)S(1)}, u32[]{:S(2)}, u32[]{:S(2)}) collective-permute-start(f32[8,16,128]{2,1,0:T(8,128)S(1)} %get-tuple-element.50), channel_id=1, source_target_pairs={{0,1},{1,0},{2,3},{3,2},{4,5},{5,4},{6,7},{7,6},{8,9},{9,8},{10,11... | collective-permute-start | bytes 196616 | tf_op jit(solution)/shard_map/ppermute | solution.py:462
  126.9 4.6 %collective-permute-start.15 = (f32[8,16,128]{2,1,0:T(8,128)S(1)}, f32[8,16,128]{2,1,0:T(8,128)S(1)}, u32[]{:S(2)}, u32[]{:S(2)}) collective-permute-start(f32[8,16,128]{2,1,0:T(8,128)S(1)} %get-tuple-element.51), channel_id=1, source_target_pairs={{0,2},{1,3},{2,0},{3,1},{4,6},{5,7},{6,4},{7,5},{8,10},{9,11},{10,... | collective-permute-start | bytes 196616 | tf_op jit(solution)/shard_map/ppermute | solution.py:462
  128.6 4.4 %collective-permute-start.16 = (f32[8,16,128]{2,1,0:T(8,128)S(1)}, f32[8,16,128]{2,1,0:T(8,128)S(1)}, u32[]{:S(2)}, u32[]{:S(2)}) collective-permute-start(f32[8,16,128]{2,1,0:T(8,128)S(1)} %get-tuple-element.52), channel_id=1, source_target_pairs={{0,3},{1,2},{2,1},{3,0},{4,7},{5,6},{6,5},{7,4},{8,11},{9,10},{10,... | collective-permute-start | bytes 196616 | tf_op jit(solution)/shard_map/ppermute | solution.py:462

commit v3 on v2

--- a/solution.py
+++ b/solution.py
@@ -20,6 +20,7 @@
 LANES = 128
 SIDE = 64
 PAD = 8
+REACH = 2
 VMEM_BYTES = 24 * 1024 * 1024
 ANY = pl.BlockSpec(memory_space=pl.ANY)
 SMEM = pl.BlockSpec(memory_space=pltpu.SMEM)
@@ -35,17 +36,6 @@
 
 def inverse(number):
     return pow(number, -1, LANES)
-
-
-def spread(tiles):
-    shape = (8, LANES)
-    lane = lax.broadcasted_iota(jnp.int32, shape, 1)
-    for j in range(tiles):
-        chunk = ((lane + (LANES - j)) * inverse(tiles)) & (LANES - 1)
-        tile_of = (chunk * tiles + j) >> 7
-        masks = [tile_of == t for t in range(1, tiles)]
-        order = (lane * tiles + j) & (LANES - 1)
-        yield j, masks, order
 
 
 def gather_lanes(x, order):
@@ -72,10 +62,10 @@
     def window(field, at):
         for w in range(PLANE):
             for t in range(tiles):
-                plain[w, at, t] = field(w * tiles + t)
+                plain[w, at, t, 0:rows] = field(w * tiles + t)
             right = field((w + 1) * tiles) if w < PLANE - 1 else far
             left = field(w * tiles - 1) if w > 0 else far
-            plain[w, at, tiles] = jnp.where(lane < SIDE, right, left)
+            plain[w, at, tiles, 0:rows] = jnp.where(lane < SIDE, right, left)
 
     def cost(t):
         at = slice(t * LANES, (t + 1) * LANES)
@@ -104,17 +94,22 @@
             meta_at = base
             base += 1
 
-    for j, masks, order in spread(chunk):
+    lane = lax.broadcasted_iota(jnp.int32, (8, LANES), 1)
+
+    def convert(j, carry):
+        column = (((lane + (LANES - j)) * inverse(chunk)) & (LANES - 1)) * chunk + j
+        masks = [column >= t * LANES for t in range(1, chunk)]
+        order = (lane * chunk + j) & (LANES - 1)
         for at in range(len(fields)):
-            def convert(w, carry, at=at):
+            for w in range(PLANE):
                 for half in range(0, rows, 8):
                     mixed = plain[w, at, 0, half : half + 8]
                     for t, mask in enumerate(masks):
                         mixed = jnp.where(mask, plain[w, at, t + 1, half : half + 8], mixed)
                     cut[w, bases[at] + j, half : half + 8] = gather_lanes(mixed, order)
-                return carry
-
-            lax.fori_loop(0, PLANE, convert, 0)
+        return carry
+
+    lax.fori_loop(0, chunk, convert, 0)
 
     owner = owner_ref[...].astype(jnp.float32)
     across = jnp.broadcast_to(owner, (LANES, LANES))
@@ -173,27 +168,50 @@
     )
 
 
+def keep_ends(dst, s, t, spot, value, tiles):
+    if t < REACH:
+        dst[s, tiles + REACH + t, spot] = pltpu.roll(value, LANES - 1, 1)
+    if t >= tiles - REACH:
+        dst[s, t - (tiles - REACH), spot] = pltpu.roll(value, 1, 1)
+
+
 def relax_rows(src, dst, cost, count, tiles, start):
-    def ends(field, reach):
-        before = [pltpu.roll(field[tiles - k], 1, 1) for k in range(reach, 0, -1)]
-        after = [pltpu.roll(field[k], LANES - 1, 1) for k in range(reach)]
-        return before + field + after
-
+    spot = pl.ds(start, 8)
+    order = sorted(range(tiles), key=lambda t: REACH <= t < tiles - REACH)
     for s in range(count):
-        near, one, two = [], [], []
-        for t in range(tiles):
-            at = s * tiles + t
-            near.append(src[at, pl.ds(start, 8)])
-            one.append(jnp.minimum(src[at, pl.ds(start - 1, 8)], src[at, pl.ds(start + 1, 8)]))
-            two.append(jnp.minimum(src[at, pl.ds(start - 2, 8)], src[at, pl.ds(start + 2, 8)]))
-        near, one, two = ends(near, 1), ends(one, 2), ends(two, 1)
-        for t in range(tiles):
-            m1 = jnp.minimum(one[t + 2], jnp.minimum(near[t], near[t + 2]))
-            m2 = jnp.minimum(one[t + 1], one[t + 3])
-            m5 = jnp.minimum(jnp.minimum(one[t], one[t + 4]), jnp.minimum(two[t], two[t + 2]))
-            best = jnp.minimum(m1 + cost[0, t, pl.ds(start, 8)], m2 + cost[1, t, pl.ds(start, 8)])
-            best = jnp.minimum(best, m5 + cost[2, t, pl.ds(start, 8)])
-            dst[s * tiles + t, pl.ds(start, 8)] = jnp.minimum(near[t + 1], best)
+
+        def load(t, shift):
+            return src[s, t + REACH, pl.ds(start + shift, 8)]
+
+        near = {t: load(t, 0) for t in range(-1, tiles + 1)}
+        one = {t: jnp.minimum(load(t, -1), load(t, 1)) for t in range(-2, tiles + 2)}
+        two = {t: jnp.minimum(load(t, -2), load(t, 2)) for t in range(-1, tiles + 1)}
+        for t in order:
+            m1 = jnp.minimum(one[t], jnp.minimum(near[t - 1], near[t + 1]))
+            m2 = jnp.minimum(one[t - 1], one[t + 1])
+            m5 = jnp.minimum(
+                jnp.minimum(one[t - 2], one[t + 2]), jnp.minimum(two[t - 1], two[t + 1])
+            )
+            best = jnp.minimum(m1 + cost[0, t, spot], m2 + cost[1, t, spot])
+            best = jnp.minimum(best, m5 + cost[2, t, spot])
+            value = jnp.minimum(near[t], best)
+            dst[s, t + REACH, spot] = value
+
+
+def fill_rows(field, tiles, start):
+    spot = pl.ds(start, 8)
+    for s in range(field.shape[0]):
+        for t in list(range(REACH)) + list(range(tiles - REACH, tiles)):
+            keep_ends(field, s, t, spot, field[s, t + REACH, spot], tiles)
+
+
+def fill_ends(field, tiles):
+    def group(at, carry):
+        for k in range(2):
+            fill_rows(field, tiles, pl.multiple_of(PAD + at * 16 + k * 8, 8))
+        return carry
+
+    lax.fori_loop(0, (field.shape[2] - 3 * PAD) // 16, group, 0)
 
 
 def scale_cost(cost):
@@ -209,23 +227,33 @@
 
 
 def run_sweeps(first, second, cost, count, tiles, sweeps):
-    groups = (first.shape[1] - 2 * PAD) // 8
+    groups = (first.shape[2] - 3 * PAD) // 8
 
     def sweep(src, dst, number):
         low = (2 * number) // 8
 
         def group(at, carry):
-            relax_rows(src, dst, cost, count, tiles, pl.multiple_of(PAD + at * 8, 8))
+            start = pl.multiple_of(PAD + (low + 2 * at) * 8, 8)
+            fill_rows(dst, tiles, pl.multiple_of(start - 8, 8))
+            relax_rows(src, dst, cost, count, tiles, start)
+            fill_rows(dst, tiles, start)
+            relax_rows(src, dst, cost, count, tiles, pl.multiple_of(start + 8, 8))
             return carry
 
-        lax.fori_loop(low, groups - low, group, 0)
+        lax.fori_loop(0, groups // 2 - low, group, 0)
+        fill_rows(dst, tiles, pl.multiple_of(PAD + (groups - low - 1) * 8, 8))
 
     def pair(at, carry):
         sweep(first, second, 2 * at + 1)
         sweep(second, first, 2 * at + 2)
         return carry
 
+    fill_ends(first, tiles)
     lax.fori_loop(0, sweeps // 2, pair, 0)
+
+
+def core(field, s, tiles):
+    return field.at[s, REACH : REACH + tiles]
 
 
 def halo_copies(plane, halo, total, even, odd, dst, sem, slabs):
@@ -258,16 +286,22 @@
     tiles = cost.shape[1]
     size = count * tiles
     base = cost.at[0]
-    copies = [
-        pltpu.make_async_copy(
-            p.at[0:size],
-            one.at[:, pl.ds(pl.multiple_of(PAD + halo + (member ^ j) * rows, 8), rows)],
-            sem.at[4 + j],
+    copies, sems = [], 16
+    for s in range(count):
+        slabs = slice(s * tiles, (s + 1) * tiles)
+        for j, p in enumerate((p0, p1, p2, p3)):
+            at = pl.multiple_of(PAD + halo + (member ^ j) * rows, 8)
+            copies.append(
+                pltpu.make_async_copy(
+                    p.at[slabs], core(one, s, tiles).at[:, pl.ds(at, rows)], sem.at[sems]
+                )
+            )
+            sems += 1
+        halos, odd_at = halo_copies(
+            plane, halo, total, even, odd, core(one, s, tiles), sem.at[pl.ds(sems, 2)], slabs
         )
-        for j, p in enumerate((p0, p1, p2, p3))
-    ]
-    halos, odd_at = halo_copies(plane, halo, total, even, odd, one, sem, slice(0, size))
-    copies += halos
+        copies += halos
+        sems += 2
     if has_cost:
         more, _ = halo_copies(
             plane, halo, total, even, odd, base, sem.at[pl.ds(2, 2)], slice(size, size + tiles)
@@ -284,7 +318,8 @@
     else:
         copies.append(pltpu.make_async_copy(cost_in, cost, sem.at[8]))
     run_copies(copies)
-    fence(plane, planes, odd_at, halo, one)
+    for s in range(count):
+        fence(plane, planes, odd_at, halo, core(one, s, tiles))
     if has_cost:
         fence(plane, planes, odd_at, halo, base)
         scale_cost(cost)
@@ -293,11 +328,19 @@
     top, bottom = PAD + halo, PAD + halo + total - halo
     low = pl.multiple_of(parity * top + (1 - parity) * bottom, 8)
     high = pl.multiple_of((1 - parity) * top + parity * bottom, 8)
-    copies = [
-        pltpu.make_async_copy(one.at[:, pl.ds(low, halo)], low_ref, sem.at[0]),
-        pltpu.make_async_copy(one.at[:, pl.ds(high, halo)], high_ref, sem.at[1]),
-        pltpu.make_async_copy(one.at[:, PAD + halo : PAD + halo + total], state, sem.at[2]),
-    ]
+    copies = []
+    for s in range(count):
+        slabs = slice(s * tiles, (s + 1) * tiles)
+        for k, (at, size_at, out) in enumerate(
+            ((low, halo, low_ref), (high, halo, high_ref), (PAD + halo, total, state))
+        ):
+            copies.append(
+                pltpu.make_async_copy(
+                    core(one, s, tiles).at[:, pl.ds(at, size_at)],
+                    out.at[slabs],
+                    sem.at[16 + 3 * s + k],
+                )
+            )
     if has_cost:
         copies.append(pltpu.make_async_copy(cost, cost_out, sem.at[3]))
     run_copies(copies)
@@ -313,23 +356,32 @@
     rows = total // PLANE
     tiles = cost.shape[1]
     own = tiles - 1
-    copies = [
-        pltpu.make_async_copy(state, one.at[:, PAD + halo : PAD + halo + total], sem.at[2]),
-        pltpu.make_async_copy(cost_in, cost, sem.at[3]),
-    ]
+    copies = [pltpu.make_async_copy(cost_in, cost, sem.at[3])]
+    for s in range(count):
+        slabs = slice(s * tiles, (s + 1) * tiles)
+        inner = core(one, s, tiles)
+        copies.append(
+            pltpu.make_async_copy(
+                state.at[slabs], inner.at[:, PAD + halo : PAD + halo + total], sem.at[8 + 3 * s]
+            )
+        )
+        halos, odd_at = halo_copies(
+            plane, halo, total, even, odd, inner, sem.at[pl.ds(9 + 3 * s, 2)], slabs
+        )
+        copies += halos
     copies += [
         pltpu.make_async_copy(m.at[m.shape[0] - 1], meta.at[member ^ j], sem.at[4 + j])
         for j, m in enumerate((m0, m1, m2, m3))
     ]
-    halos, odd_at = halo_copies(plane, halo, total, even, odd, one, sem, slice(0, count * tiles))
-    run_copies(copies + halos)
-    fence(plane, planes, odd_at, halo, one)
+    run_copies(copies)
+    for s in range(count):
+        fence(plane, planes, odd_at, halo, core(one, s, tiles))
     run_sweeps(one, two, cost, count, tiles, sweeps)
 
     for t in range(tiles):
         low = None
         for s in range(count):
-            at = (s * tiles + t, slice(PAD + halo, PAD + halo + total))
+            at = (s, REACH + t, slice(PAD + halo, PAD + halo + total))
             each = jnp.minimum(one[at], jnp.float32(clip_value)) / clip_value
             one[at] = each
             low = each if low is None else jnp.minimum(low, each)
@@ -386,7 +438,7 @@
         at_slot = turned[:, 3:4] + base == spot
         to_owner = jnp.where(meta[q, 2:3] == device, 1.0, 0.0).astype(jnp.bfloat16)
         for s in range(count):
-            block = one[s * tiles : (s + 1) * tiles, PAD + halo + q * rows : PAD + halo + (q + 1) * rows]
+            block = one[s, REACH : REACH + tiles, PAD + halo + q * rows : PAD + halo + (q + 1) * rows]
             found = exact(pick, block.reshape(height, LANES))
             value = jnp.sum(jnp.where(at_lane, found, 0.0), axis=1, keepdims=True)
             term = exact(to_owner, jnp.where(at_slot, value, 0.0))
@@ -443,7 +495,7 @@
         in_specs=[SMEM, VMEM, VMEM, VMEM, VMEM, VMEM],
         out_specs=[ANY] * (2 * PLANE),
         scratch_shapes=[
-            pltpu.VMEM((PLANE, sources + 1, tiles, rows, LANES), jnp.float32),
+            pltpu.VMEM((PLANE, sources + 1, tiles, rows + 8, LANES), jnp.float32),
             pltpu.VMEM((PLANE, sum(sizes), rows, LANES), jnp.float32),
             pltpu.SemaphoreType.DMA((2 * PLANE,)),
         ],
@@ -490,11 +542,11 @@
         )(*pieces[k])
         halos.append(swap_planes(even, odd))
 
-    deep = total + 2 * halo + 2 * PAD
+    deep = total + 2 * halo + 3 * PAD
     size = half * tiles
     scratch = [
-        pltpu.VMEM((size, deep, LANES), jnp.float32),
-        pltpu.VMEM((size, deep, LANES), jnp.float32),
+        pltpu.VMEM((half, tiles + 2 * REACH, deep, LANES), jnp.float32),
+        pltpu.VMEM((half, tiles + 2 * REACH, deep, LANES), jnp.float32),
         pltpu.VMEM((3, tiles, deep, LANES), jnp.float32),
     ]
     states, later = [], []
@@ -508,7 +560,7 @@
             in_specs=[ANY] * (6 if k == 0 else 7),
             compiler_params=limit,
             out_specs=[ANY] * (4 if k == 0 else 3),
-            scratch_shapes=scratch + [pltpu.SemaphoreType.DMA((12,))],
+            scratch_shapes=scratch + [pltpu.SemaphoreType.DMA((16 + 6 * half,))],
             name=f"first{k}",
         )(*pieces[k], *halos[k], *([] if k == 0 else [cost]))
         if k == 0:
@@ -536,7 +588,7 @@
             out_shape=out_shape,
             in_specs=[ANY] * 8 + ([VMEM, VMEM] if is_last else []),
             out_specs=out_specs,
-            scratch_shapes=scratch + more + [pltpu.SemaphoreType.DMA((8,))],
+            scratch_shapes=scratch + more + [pltpu.SemaphoreType.DMA((8 + 3 * half,))],
             compiler_params=limit,
             name=f"last{k}",
         )(states[k], *later[k], cost, *pieces[0], *([partial, placed] if is_last else []))

time: 135 us -> 105 us (0.78)
  Pallas kernels: 82.6 us -> 52.7 us
    pallas_call x1, Pallas kernels: 16.4 us -> 3.97 us  [on_device(): pl.pallas_call(functools.partial(pack_kernel, groups, cap), out_shape=[sh...]
    pallas_call x2, Pallas kernels: 35.3 us -> 26.5 us  [on_device(): pl.pallas_call(functools.partial(last_kernel, half, sweeps, is_last, plan...]
    pallas_call x2, Pallas kernels: 29.7 us -> 21.1 us  [on_device(): pl.pallas_call(functools.partial(first_kernel, half, sweeps, k == 0, plan...]
  transfers between devices with their start and end apart: 18 -> 18, of which waited for: 8 -> 8; matrix products, arithmetic and copies ran while one was open for 0% -> 0% of each run, Pallas kernels for 35% -> 33%
where the time goes in v3:
time: 105 us; the launch traced here: 104 us
  Pallas kernels  52.7 us (50%)
  starting transfers between devices  26.1 us (25%)
  waiting for transfers between devices  19.6 us (19%)
  local copies, waits for them, and re-layouts  5.08 us (5%)
    pallas_call x2, Pallas kernels, on_device(): pl.pallas_call(functools.partial(last_kernel, half, sweeps, is_last, plan...  26.5 us
    pallas_call x2, Pallas kernels, on_device(): pl.pallas_call(functools.partial(first_kernel, half, sweeps, k == 0, plan...  21.1 us
    ppermute x9, waiting for transfers between devices, swap(): return lax.ppermute(x, axis, [(d, d ^ j) for d in range(n)])  16.8 us
    ppermute x4, starting transfers between devices, swap_planes(): lax.ppermute(even, axis, pairs_even)  11.2 us
    ppermute x9, starting transfers between devices, swap(): return lax.ppermute(x, axis, [(d, d ^ j) for d in range(n)])  7.33 us
    unnamed x12, local copies, waits for them, and re-layouts  5.08 us
    all_to_all x1, starting transfers between devices, on_device(): lax.all_to_all(placed, axis, split_axis=0, concat_axis=0, tiled=True)  4.9 us
    pallas_call x1, Pallas kernels, on_device(): pl.pallas_call(functools.partial(pack_kernel, groups, cap), out_shape=[sh...  3.97 us
  transfers between devices with their start and end apart: 18, of which 8 were waited for; matrix products, arithmetic and copies ran while one was open for 0% of the time, Pallas kernels for 33%

profile of v3, /device:TPU:0, one launch (start us, length us, event | category | flops | bytes accessed | tf_op | source)
XLA Modules:
  0.0 104.3 jit_solution(6972995001192748226)
XLA Ops:
  0.6 1.2 %copy-done = f32[4,16,4096]{2,1,0:T(8,128)S(1)} copy-done((f32[4,16,4096]{2,1,0:T(8,128)S(1)}, f32[4,16,4096]{2,1,0:T(8,128)}, u32[]{:S(2)}) %copy-start) | copy-done | bytes 1048600
  1.9 0.9 copy-done.1
  2.8 0.9 copy-done.2
  3.8 0.7 copy-done.3
  4.4 0.7 copy-done.4
  5.1 0.7 copy-done.5
  5.7 4.0 %pack.1 = (f32[28,16,128]{2,1,0:T(8,128)S(1)}, f32[28,16,128]{2,1,0:T(8,128)S(1)}, f32[28,16,128]{2,1,0:T(8,128)S(1)}, f32[28,16,128]{2,1,0:T(8,128)S(1)}, f32[1...) custom-call(s32[4]{0:T(128)S(1)} %copy-done.3, ...), custom_call_target="tpu_custom_call" | custom-call | tf_op jit(solution)/shard_map/pack/pallas_call | solution.py:492
  9.7 0.6 collective-permute-start.5
  10.3 2.6 %collective-permute-start.6 = (f32[28,16,128]{2,1,0:T(8,128)S(1)}, f32[28,16,128]{2,1,0:T(8,128)S(1)}, u32[]{:S(2)}, u32[]{:S(2)}) collective-permute-start(f32[28,16,128]{2,1,0:T(8,128)S(1)} %get-tuple-element.36), channel_id=1, source_target_pairs={{0,2},{1,3},{2,0},{3,1},{4,6},{5,7},{6,4},{7,5},{8,10},{9,11},{10,... | collective-permute-start | bytes 688136 | tf_op jit(solution)/shard_map/ppermute | solution.py:514
  13.0 1.9 %collective-permute-start.1 = (f32[18,16,128]{2,1,0:T(8,128)S(1)}, f32[18,16,128]{2,1,0:T(8,128)S(1)}, u32[]{:S(2)}, u32[]{:S(2)}) collective-permute-start(f32[18,16,128]{2,1,0:T(8,128)S(1)} %get-tuple-element.30), channel_id=1, source_target_pairs={{0,2},{1,3},{2,0},{3,1},{4,6},{5,7},{6,4},{7,5},{8,10},{9,11},{10,... | collective-permute-start | bytes 442376 | tf_op jit(solution)/shard_map/ppermute | solution.py:514
  15.0 4.3 %collective-permute-done.6.p2.m2 = f32[28,16,128]{2,1,0:T(8,128)S(1)} collective-permute-done((f32[28,16,128]{2,1,0:T(8,128)S(1)}, f32[28,16,128]{2,1,0:T(8,128)S(1)}, u32[]{:S(2)}, u32[]{:S(2)}) %collective-permute-start.6) | collective-permute-done | bytes 229408 | tf_op jit(solution)/shard_map/ppermute | solution.py:514
  19.3 4.5 %collective-permute-done.7.p3.m3 = f32[28,16,128]{2,1,0:T(8,128)S(1)} collective-permute-done((f32[28,16,128]{2,1,0:T(8,128)S(1)}, f32[28,16,128]{2,1,0:T(8,128)S(1)}, u32[]{:S(2)}, u32[]{:S(2)}) %collective-permute-start.7) | collective-permute-done | bytes 229408 | tf_op jit(solution)/shard_map/ppermute | solution.py:514
  24.0 1.6 %collective-permute-start.8 = (f32[27,24,128]{2,1,0:T(8,128)S(1)}, f32[27,24,128]{2,1,0:T(8,128)S(1)}, u32[]{:S(2)}, u32[]{:S(2)}) collective-permute-start(f32[27,24,128]{2,1,0:T(8,128)S(1)} %get-tuple-element.38), channel_id=1, source_target_pairs={{0,4},{1,5},{2,6},{3,7},{4,0},{5,1},{6,2},{7,3},{8,12},{9,13},{10,... | collective-permute-start | bytes 995336 | tf_op jit(solution)/shard_map/ppermute | solution.py:522
  25.6 0.7 collective-permute-start.9
  26.3 1.1 %collective-permute-done.1.p2 = f32[18,16,128]{2,1,0:T(8,128)S(1)} collective-permute-done((f32[18,16,128]{2,1,0:T(8,128)S(1)}, f32[18,16,128]{2,1,0:T(8,128)S(1)}, u32[]{:S(2)}, u32[]{:S(2)}) %collective-permute-start.1) | collective-permute-done | bytes 147488 | tf_op jit(solution)/shard_map/ppermute | solution.py:514
  27.4 2.6 %collective-permute-done.2.p3 = f32[18,16,128]{2,1,0:T(8,128)S(1)} collective-permute-done((f32[18,16,128]{2,1,0:T(8,128)S(1)}, f32[18,16,128]{2,1,0:T(8,128)S(1)}, u32[]{:S(2)}, u32[]{:S(2)}) %collective-permute-start.2) | collective-permute-done | bytes 147488 | tf_op jit(solution)/shard_map/ppermute | solution.py:514
  30.2 1.6 %collective-permute-start.3 = (f32[18,24,128]{2,1,0:T(8,128)S(1)}, f32[18,24,128]{2,1,0:T(8,128)S(1)}, u32[]{:S(2)}, u32[]{:S(2)}) collective-permute-start(f32[18,24,128]{2,1,0:T(8,128)S(1)} %get-tuple-element.32), channel_id=1, source_target_pairs={{0,4},{1,5},{2,6},{3,7},{4,0},{5,1},{6,2},{7,3},{8,12},{9,13},{10,... | collective-permute-start | bytes 663560 | tf_op jit(solution)/shard_map/ppermute | solution.py:522
  31.8 0.7 collective-permute-start.4
  32.5 2.3 %collective-permute-done.8.even = f32[27,24,128]{2,1,0:T(8,128)S(1)} collective-permute-done((f32[27,24,128]{2,1,0:T(8,128)S(1)}, f32[27,24,128]{2,1,0:T(8,128)S(1)}, u32[]{:S(2)}, u32[]{:S(2)}) %collective-permute-start.8) | collective-permute-done | bytes 331808 | tf_op jit(solution)/shard_map/ppermute | solution.py:522
  34.7 10.7 %first0.1 = (f32[18,64,128]{2,1,0:T(8,128)S(1)}, f32[18,24,128]{2,1,0:T(8,128)S(1)}, f32[18,24,128]{2,1,0:T(8,128)S(1)}, f32[3,9,136,128]{3,2,1,0:T(8,128)S(1)}) custom-call(f32[28,16,128]{2,1,0:T(8,128)S(1)} %get-tuple-element.34.p0.m0, f32[28,16,128]{2,1,0:T(8,128)S(1)} %collective-permute-done.5.p1.m1, f32[28,16,128]{2,1,0:T(8,128)S(1)} %collective-permute-done.6.p2.m2, ...), custom_call_target="tpu_custom_call" | custom-call | tf_op jit(solution)/shard_map/first0/pallas_call | solution.py:555
  45.4 4.6 %collective-permute-start.12 = (f32[18,24,128]{2,1,0:T(8,128)S(1)}, f32[18,24,128]{2,1,0:T(8,128)S(1)}, u32[]{:S(2)}, u32[]{:S(2)}) collective-permute-start(f32[18,24,128]{2,1,0:T(8,128)S(1)} %get-tuple-element.45), channel_id=1, source_target_pairs={{0,4},{1,5},{2,6},{3,7},{4,0},{5,1},{6,2},{7,3},{8,12},{9,13},{10,... | collective-permute-start | bytes 663560 | tf_op jit(solution)/shard_map/ppermute | solution.py:522
  50.1 0.7 collective-permute-start.13
  50.8 10.4 %first1.1 = (f32[18,64,128]{2,1,0:T(8,128)S(1)}, f32[18,24,128]{2,1,0:T(8,128)S(1)}, f32[18,24,128]{2,1,0:T(8,128)S(1)}) custom-call(f32[18,16,128]{2,1,0:T(8,128)S(1)} %get-tuple-element.28.p0, f32[18,16,128]{2,1,0:T(8,128)S(1)} %collective-permute-done.p1, f32[18,16,128]{2,1,0:T(8,128)S(1)} %collective-permute-done.1.p2, ...), custom_call_target="tpu_custom_call" | custom-call | tf_op jit(solution)/shard_map/first1/pallas_call | solution.py:555
  61.2 3.3 %collective-permute-start.10 = (f32[18,24,128]{2,1,0:T(8,128)S(1)}, f32[18,24,128]{2,1,0:T(8,128)S(1)}, u32[]{:S(2)}, u32[]{:S(2)}) collective-permute-start(f32[18,24,128]{2,1,0:T(8,128)S(1)} %get-tuple-element.42), channel_id=1, source_target_pairs={{0,4},{1,5},{2,6},{3,7},{4,0},{5,1},{6,2},{7,3},{8,12},{9,13},{10,... | collective-permute-start | bytes 663560 | tf_op jit(solution)/shard_map/ppermute | solution.py:522
  64.5 0.7 collective-permute-start.11
  65.2 12.5 %last0.1 = (f32[16,2,256]{2,1,0:T(2,128)S(1)}, f32[9,64,128]{2,1,0:T(8,128)S(1)}) custom-call(f32[18,64,128]{2,1,0:T(8,128)S(1)} %get-tuple-element.44.state, f32[18,24,128]{2,1,0:T(8,128)S(1)} %collective-permute-done.12.even, f32[18,24,128]{2,1,0:T(8,128)S(1)} %collective-permute-done.13.odd, f32[3,9,136,128]{3,2,1,0:T(8,128)S(1)} %get-tuple-element.40.rest_0_.cost_in, ...), custom_call_target="tpu_custom_call" | custom-call | tf_op jit(solution)/shard_map/last0/pallas_call | solution.py:586
  77.7 14.0 %last1.1 = (f32[16,4,256]{2,1,0:T(4,128)}, f32[8,16,128]{2,1,0:T(8,128)S(1)}, f32[8,16,128]{2,1,0:T(8,128)S(1)}, f32[8,16,128]{2,1,0:T(8,128)S(1)}, f32[8,16,128]{2,1,0:T(8,128)S(1)}) custom-call(f32[18,64,128]{2,1,0:T(8,128)S(1)} %get-tuple-element.41.state, f32[18,24,128]{2,1,0:T(8,128)S(1)} %collective-permute-done.10.even, ...), custom_call_target="tpu_custom_call" | custom-call | tf_op jit(solution)/shard_map/last1/pallas_call | solution.py:586
  91.7 4.9 %all-to-all-start = ((f32[16,4,256]{2,1,0:T(4,128)}), f32[16,4,256]{2,1,0:T(4,128)S(1)}, u32[]{:S(2)}, u32[]{:S(2)}) async-start(f32[16,4,256]{2,1,0:T(4,128)} %get-tuple-element.53), calls=%async_computation | async-start | bytes 131072 | tf_op jit(solution)/shard_map/all_to_all | solution.py:602
  97.0 1.6 %collective-permute-start.15 = (f32[8,16,128]{2,1,0:T(8,128)S(1)}, f32[8,16,128]{2,1,0:T(8,128)S(1)}, u32[]{:S(2)}, u32[]{:S(2)}) collective-permute-start(f32[8,16,128]{2,1,0:T(8,128)S(1)} %get-tuple-element.51), channel_id=1, source_target_pairs={{0,2},{1,3},{2,0},{3,1},{4,6},{5,7},{6,4},{7,5},{8,10},{9,11},{10,... | collective-permute-start | bytes 196616 | tf_op jit(solution)/shard_map/ppermute | solution.py:514
  98.7 2.9 %collective-permute-done.15.r2 = f32[8,16,128]{2,1,0:T(8,128)S(1)} collective-permute-done((f32[8,16,128]{2,1,0:T(8,128)S(1)}, f32[8,16,128]{2,1,0:T(8,128)S(1)}, u32[]{:S(2)}, u32[]{:S(2)}) %collective-permute-start.15) | collective-permute-done | bytes 65568 | tf_op jit(solution)/shard_map/ppermute | solution.py:514
  101.6 1.4 %collective-permute-done.16.r3 = f32[8,16,128]{2,1,0:T(8,128)S(1)} collective-permute-done((f32[8,16,128]{2,1,0:T(8,128)S(1)}, f32[8,16,128]{2,1,0:T(8,128)S(1)}, u32[]{:S(2)}, u32[]{:S(2)}) %collective-permute-start.16) | collective-permute-done | bytes 65568 | tf_op jit(solution)/shard_map/ppermute | solution.py:514
  103.5 0.7 join.1
  (24 shorter events, 1.5 us)
Async XLA Ops:
  0.6 1.2 %copy-start = (f32[4,16,4096]{2,1,0:T(8,128)S(1)}, f32[4,16,4096]{2,1,0:T(8,128)}, u32[]{:S(2)}) copy-start(f32[4,16,4096]{2,1,0:T(8,128)} %start_ref.1) | copy-start | bytes 3145732
  1.9 0.9 copy-start.1
  2.8 0.9 copy-start.2
  3.8 0.7 copy-start.3
  4.4 0.7 copy-start.4
  5.1 0.7 copy-start.5
  9.7 5.3 %collective-permute-start.5 = (f32[28,16,128]{2,1,0:T(8,128)S(1)}, f32[28,16,128]{2,1,0:T(8,128)S(1)}, u32[]{:S(2)}, u32[]{:S(2)}) collective-permute-start(f32[28,16,128]{2,1,0:T(8,128)S(1)} %get-tuple-element.35), channel_id=1, source_target_pairs={{0,1},{1,0},{2,3},{3,2},{4,5},{5,4},{6,7},{7,6},{8,9},{9,8},{10,11... | collective-permute-start | bytes 688136 | tf_op jit(solution)/shard_map/ppermute | solution.py:514
  10.3 9.0 %collective-permute-start.6 = (f32[28,16,128]{2,1,0:T(8,128)S(1)}, f32[28,16,128]{2,1,0:T(8,128)S(1)}, u32[]{:S(2)}, u32[]{:S(2)}) collective-permute-start(f32[28,16,128]{2,1,0:T(8,128)S(1)} %get-tuple-element.36), channel_id=1, source_target_pairs={{0,2},{1,3},{2,0},{3,1},{4,6},{5,7},{6,4},{7,5},{8,10},{9,11},{10,... | collective-permute-start | bytes 688136 | tf_op jit(solution)/shard_map/ppermute | solution.py:514
  12.8 10.9 %collective-permute-start.7 = (f32[28,16,128]{2,1,0:T(8,128)S(1)}, f32[28,16,128]{2,1,0:T(8,128)S(1)}, u32[]{:S(2)}, u32[]{:S(2)}) collective-permute-start(f32[28,16,128]{2,1,0:T(8,128)S(1)} %get-tuple-element.37), channel_id=1, source_target_pairs={{0,3},{1,2},{2,1},{3,0},{4,7},{5,6},{6,5},{7,4},{8,11},{9,10},{10,... | collective-permute-start | bytes 688136 | tf_op jit(solution)/shard_map/ppermute | solution.py:514
  12.9 13.4 %collective-permute-start = (f32[18,16,128]{2,1,0:T(8,128)S(1)}, f32[18,16,128]{2,1,0:T(8,128)S(1)}, u32[]{:S(2)}, u32[]{:S(2)}) collective-permute-start(f32[18,16,128]{2,1,0:T(8,128)S(1)} %get-tuple-element.29), channel_id=1, source_target_pairs={{0,1},{1,0},{2,3},{3,2},{4,5},{5,4},{6,7},{7,6},{8,9},{9,8},{10,11... | collective-permute-start | bytes 442376 | tf_op jit(solution)/shard_map/ppermute | solution.py:514
  13.0 14.3 %collective-permute-start.1 = (f32[18,16,128]{2,1,0:T(8,128)S(1)}, f32[18,16,128]{2,1,0:T(8,128)S(1)}, u32[]{:S(2)}, u32[]{:S(2)}) collective-permute-start(f32[18,16,128]{2,1,0:T(8,128)S(1)} %get-tuple-element.30), channel_id=1, source_target_pairs={{0,2},{1,3},{2,0},{3,1},{4,6},{5,7},{6,4},{7,5},{8,10},{9,11},{10,... | collective-permute-start | bytes 442376 | tf_op jit(solution)/shard_map/ppermute | solution.py:514
  15.0 15.0 %collective-permute-start.2 = (f32[18,16,128]{2,1,0:T(8,128)S(1)}, f32[18,16,128]{2,1,0:T(8,128)S(1)}, u32[]{:S(2)}, u32[]{:S(2)}) collective-permute-start(f32[18,16,128]{2,1,0:T(8,128)S(1)} %get-tuple-element.31), channel_id=1, source_target_pairs={{0,3},{1,2},{2,1},{3,0},{4,7},{5,6},{6,5},{7,4},{8,11},{9,10},{10,... | collective-permute-start | bytes 442376 | tf_op jit(solution)/shard_map/ppermute | solution.py:514
  24.0 10.7 %collective-permute-start.8 = (f32[27,24,128]{2,1,0:T(8,128)S(1)}, f32[27,24,128]{2,1,0:T(8,128)S(1)}, u32[]{:S(2)}, u32[]{:S(2)}) collective-permute-start(f32[27,24,128]{2,1,0:T(8,128)S(1)} %get-tuple-element.38), channel_id=1, source_target_pairs={{0,4},{1,5},{2,6},{3,7},{4,0},{5,1},{6,2},{7,3},{8,12},{9,13},{10,... | collective-permute-start | bytes 995336 | tf_op jit(solution)/shard_map/ppermute | solution.py:522
  25.6 9.1 %collective-permute-start.9 = (f32[27,24,128]{2,1,0:T(8,128)S(1)}, f32[27,24,128]{2,1,0:T(8,128)S(1)}, u32[]{:S(2)}, u32[]{:S(2)}) collective-permute-start(f32[27,24,128]{2,1,0:T(8,128)S(1)} %get-tuple-element.39), channel_id=1, source_target_pairs={{4,8},{5,9},{6,10},{7,11},{8,4},{9,5},{10,6},{11,7},{20,24},{21,25... | collective-permute-start | bytes 995336 | tf_op jit(solution)/shard_map/ppermute | solution.py:522
  30.2 20.5 %collective-permute-start.3 = (f32[18,24,128]{2,1,0:T(8,128)S(1)}, f32[18,24,128]{2,1,0:T(8,128)S(1)}, u32[]{:S(2)}, u32[]{:S(2)}) collective-permute-start(f32[18,24,128]{2,1,0:T(8,128)S(1)} %get-tuple-element.32), channel_id=1, source_target_pairs={{0,4},{1,5},{2,6},{3,7},{4,0},{5,1},{6,2},{7,3},{8,12},{9,13},{10,... | collective-permute-start | bytes 663560 | tf_op jit(solution)/shard_map/ppermute | solution.py:522
  31.8 19.0 %collective-permute-start.4 = (f32[18,24,128]{2,1,0:T(8,128)S(1)}, f32[18,24,128]{2,1,0:T(8,128)S(1)}, u32[]{:S(2)}, u32[]{:S(2)}) collective-permute-start(f32[18,24,128]{2,1,0:T(8,128)S(1)} %get-tuple-element.33), channel_id=1, source_target_pairs={{4,8},{5,9},{6,10},{7,11},{8,4},{9,5},{10,6},{11,7},{20,24},{21,25... | collective-permute-start | bytes 663560 | tf_op jit(solution)/shard_map/ppermute | solution.py:522
  45.4 19.8 %collective-permute-start.12 = (f32[18,24,128]{2,1,0:T(8,128)S(1)}, f32[18,24,128]{2,1,0:T(8,128)S(1)}, u32[]{:S(2)}, u32[]{:S(2)}) collective-permute-start(f32[18,24,128]{2,1,0:T(8,128)S(1)} %get-tuple-element.45), channel_id=1, source_target_pairs={{0,4},{1,5},{2,6},{3,7},{4,0},{5,1},{6,2},{7,3},{8,12},{9,13},{10,... | collective-permute-start | bytes 663560 | tf_op jit(solution)/shard_map/ppermute | solution.py:522
  50.1 15.1 %collective-permute-start.13 = (f32[18,24,128]{2,1,0:T(8,128)S(1)}, f32[18,24,128]{2,1,0:T(8,128)S(1)}, u32[]{:S(2)}, u32[]{:S(2)}) collective-permute-start(f32[18,24,128]{2,1,0:T(8,128)S(1)} %get-tuple-element.46), channel_id=1, source_target_pairs={{4,8},{5,9},{6,10},{7,11},{8,4},{9,5},{10,6},{11,7},{20,24},{21,25... | collective-permute-start | bytes 663560 | tf_op jit(solution)/shard_map/ppermute | solution.py:522
  61.2 16.5 %collective-permute-start.10 = (f32[18,24,128]{2,1,0:T(8,128)S(1)}, f32[18,24,128]{2,1,0:T(8,128)S(1)}, u32[]{:S(2)}, u32[]{:S(2)}) collective-permute-start(f32[18,24,128]{2,1,0:T(8,128)S(1)} %get-tuple-element.42), channel_id=1, source_target_pairs={{0,4},{1,5},{2,6},{3,7},{4,0},{5,1},{6,2},{7,3},{8,12},{9,13},{10,... | collective-permute-start | bytes 663560 | tf_op jit(solution)/shard_map/ppermute | solution.py:522
  64.5 13.2 %collective-permute-start.11 = (f32[18,24,128]{2,1,0:T(8,128)S(1)}, f32[18,24,128]{2,1,0:T(8,128)S(1)}, u32[]{:S(2)}, u32[]{:S(2)}) collective-permute-start(f32[18,24,128]{2,1,0:T(8,128)S(1)} %get-tuple-element.43), channel_id=1, source_target_pairs={{4,8},{5,9},{6,10},{7,11},{8,4},{9,5},{10,6},{11,7},{20,24},{21,25... | collective-permute-start | bytes 663560 | tf_op jit(solution)/shard_map/ppermute | solution.py:522
  91.7 11.8 %all-to-all-start = ((f32[16,4,256]{2,1,0:T(4,128)}), f32[16,4,256]{2,1,0:T(4,128)S(1)}, u32[]{:S(2)}, u32[]{:S(2)}) async-start(f32[16,4,256]{2,1,0:T(4,128)} %get-tuple-element.53), calls=%async_computation | async-start | bytes 131072 | tf_op jit(solution)/shard_map/all_to_all | solution.py:602
  96.6 2.0 %collective-permute-start.14 = (f32[8,16,128]{2,1,0:T(8,128)S(1)}, f32[8,16,128]{2,1,0:T(8,128)S(1)}, u32[]{:S(2)}, u32[]{:S(2)}) collective-permute-start(f32[8,16,128]{2,1,0:T(8,128)S(1)} %get-tuple-element.50), channel_id=1, source_target_pairs={{0,1},{1,0},{2,3},{3,2},{4,5},{5,4},{6,7},{7,6},{8,9},{9,8},{10,11... | collective-permute-start | bytes 196616 | tf_op jit(solution)/shard_map/ppermute | solution.py:514
  97.0 4.6 %collective-permute-start.15 = (f32[8,16,128]{2,1,0:T(8,128)S(1)}, f32[8,16,128]{2,1,0:T(8,128)S(1)}, u32[]{:S(2)}, u32[]{:S(2)}) collective-permute-start(f32[8,16,128]{2,1,0:T(8,128)S(1)} %get-tuple-element.51), channel_id=1, source_target_pairs={{0,2},{1,3},{2,0},{3,1},{4,6},{5,7},{6,4},{7,5},{8,10},{9,11},{10,... | collective-permute-start | bytes 196616 | tf_op jit(solution)/shard_map/ppermute | solution.py:514
  98.7 4.4 %collective-permute-start.16 = (f32[8,16,128]{2,1,0:T(8,128)S(1)}, f32[8,16,128]{2,1,0:T(8,128)S(1)}, u32[]{:S(2)}, u32[]{:S(2)}) collective-permute-start(f32[8,16,128]{2,1,0:T(8,128)S(1)} %get-tuple-element.52), channel_id=1, source_target_pairs={{0,3},{1,2},{2,1},{3,0},{4,7},{5,6},{6,5},{7,4},{8,11},{9,10},{10,... | collective-permute-start | bytes 196616 | tf_op jit(solution)/shard_map/ppermute | solution.py:514

commit v4 on v0

v4 whole, which is shorter than its diff:
```python
import functools
import jax
import jax.numpy as jnp
from jax import lax
from jax.experimental import pallas as pl
from jax.experimental.pallas import tpu as pltpu
from jax.sharding import PartitionSpec as P

SWEEPS = 8
BLOCKS = 3
FIRST = 8

far_value = 1000000.0
land_cost = 10000.0
clip_value = 48.0
root_two = 1.41421356
root_five = 2.23606798

PLANE = 4
LANES = 128
SIDE = 64
PAD = 8
REACH = 2
VMEM_BYTES = 24 * 1024 * 1024
ANY = pl.BlockSpec(memory_space=pl.ANY)
HBM = pl.BlockSpec(memory_space=pltpu.HBM)
SMEM = pl.BlockSpec(memory_space=pltpu.SMEM)
VMEM = pl.BlockSpec(memory_space=pltpu.VMEM)


def run_copies(copies):
    def each(act):
        for copy in copies:
            if isinstance(copy, tuple):
                pl.when(copy[0])(functools.partial(act, copy[1]))
            else:
                act(copy)

    each(lambda copy: copy.start())
    each(lambda copy: copy.wait())


class Semaphores:
    def __init__(self, sem):
        self.sem, self.used = sem, 0

    def copy(self, source, target):
        self.used += 1
        return pltpu.make_async_copy(source, target, self.sem.at[self.used - 1])


def inverse(number):
    return pow(number, -1, LANES)


def gather_lanes(x, order):
    return jnp.take_along_axis(x, order, axis=1, mode="promise_in_bounds")


def here():
    index = lax.axis_index("space")
    return lax.rem(index, PLANE), lax.div(index, PLANE), index


def aligned(at):
    return pl.multiple_of(at, 8)


def pack_kernel(groups, source_hbm, slow_hbm, ocean_hbm, start_hbm, cell_hbm, owner_hbm, *rest):
    outs, (source_ref, cell_ref, owner_ref, field_ref, ocean_ref, side_ref, sem) = rest[:-7], rest[-7:]
    sources, rows, width = start_hbm.shape
    own = width // PLANE
    tiles = own // LANES
    chunk = tiles + 1
    member, _, index = here()
    sems = Semaphores(sem)
    run_copies(
        [
            sems.copy(start_hbm, field_ref.at[0:sources]),
            sems.copy(slow_hbm, field_ref.at[sources]),
            sems.copy(ocean_hbm, ocean_ref),
            sems.copy(source_hbm, source_ref),
            sems.copy(cell_hbm, cell_ref),
            sems.copy(owner_hbm, owner_ref),
        ]
    )
    lane = lax.broadcasted_iota(jnp.int32, (8, LANES), 1)
    row = lax.broadcasted_iota(jnp.int32, (8, LANES), 0)
    far = jnp.full((8, LANES), far_value, jnp.float32)

    for t in range(width // LANES):
        at = slice(t * LANES, (t + 1) * LANES)
        field_ref[sources, :, at] = jnp.where(
            ocean_ref[:, at] == 1, field_ref[sources, :, at], jnp.float32(land_cost)
        )
    for s in range(sources):
        cell = source_ref[s] - index * (rows * width)

        @pl.when((cell >= 0) & (cell < rows * width))
        def _():
            line, column = lax.div(cell, width), lax.rem(cell, width)
            spot = pl.ds(aligned(lax.div(line, 8) * 8), 8)
            at = pl.ds(pl.multiple_of(lax.div(column, LANES) * LANES, LANES), LANES)
            hit = (row == lax.rem(line, 8)) & (lane == lax.rem(column, LANES))
            field_ref[s, spot, at] = jnp.where(hit, 0.0, field_ref[s, spot, at])

    for f in range(sources + 1):
        for w in range(PLANE):
            for half in range(0, rows, 8):
                right = (w + 1) * own
                left = w * own - LANES
                value_right = field_ref[f, half : half + 8, right : right + LANES] if w < PLANE - 1 else far
                value_left = field_ref[f, half : half + 8, left : left + LANES] if w > 0 else far
                side_ref[w, f, half : half + 8] = jnp.where(lane < SIDE, value_right, value_left)

    order_of = []
    for number, group in enumerate(groups):
        order_of += [(number, k, s) for k, s in enumerate(group)]
        if number == 0:
            order_of.append((0, len(group), sources))

    def convert(j, carry):
        column = (((lane + (LANES - j)) * inverse(chunk)) & (LANES - 1)) * chunk + j
        masks = [column >= t * LANES for t in range(1, chunk)]
        order = (lane * chunk + j) & (LANES - 1)
        for shift in range(PLANE):
            window = member ^ shift
            for number, slab, f in order_of:
                out = outs[number * PLANE + shift]
                for half in range(0, rows, 8):
                    mixed = None
                    for t in range(chunk):
                        if t < tiles:
                            at = pl.multiple_of(window * own + t * LANES, LANES)
                            value = field_ref[f, half : half + 8, pl.ds(at, LANES)]
                        else:
                            value = side_ref[window, f, half : half + 8]
                        mixed = value if t == 0 else jnp.where(masks[t - 1], value, mixed)
                    out[slab * chunk + j, half : half + 8] = gather_lanes(mixed, order)
        return carry

    lax.fori_loop(0, chunk, convert, 0)

    owner = owner_ref[...].astype(jnp.float32)
    across = jnp.broadcast_to(owner, (LANES, LANES))
    down = jnp.transpose(across)
    earlier = lax.broadcasted_iota(jnp.int32, (LANES, LANES), 0) < lax.broadcasted_iota(
        jnp.int32, (LANES, LANES), 1
    )
    rank = jnp.sum(jnp.where(earlier & (across == down), 1.0, 0.0), axis=0, keepdims=True)
    cell = cell_ref[...].astype(jnp.float32)
    line = jnp.floor(cell / width)
    column = cell - line * width
    part = jnp.floor(column / own)
    column = column - part * own
    spot = jnp.floor((column + 0.5) / chunk)
    place = (part * chunk + (column - spot * chunk)) * rows + line
    filler = jnp.zeros((rows - 4, LANES), jnp.float32)
    meta = jnp.concatenate([place, spot, owner, rank, filler], axis=0)
    for shift in range(PLANE):
        outs[shift][outs[shift].shape[0] - 1] = meta


def keep_ends(dst, s, t, spot, value, tiles):
    if t < REACH:
        dst[s, tiles + REACH + t, spot] = pltpu.roll(value, LANES - 1, 1)
    if t >= tiles - REACH:
        dst[s, t - (tiles - REACH), spot] = pltpu.roll(value, 1, 1)


def relax_rows(src, dst, cost, count, tiles, start):
    spot = pl.ds(start, 8)
    order = sorted(range(tiles), key=lambda t: REACH <= t < tiles - REACH)
    for s in range(count):

        def load(t, shift):
            return src[s, t + REACH, pl.ds(start + shift, 8)]

        near = {t: load(t, 0) for t in range(-1, tiles + 1)}
        one = {t: jnp.minimum(load(t, -1), load(t, 1)) for t in range(-2, tiles + 2)}
        two = {t: jnp.minimum(load(t, -2), load(t, 2)) for t in range(-1, tiles + 1)}
        for t in order:
            m1 = jnp.minimum(one[t], jnp.minimum(near[t - 1], near[t + 1]))
            m2 = jnp.minimum(one[t - 1], one[t + 1])
            m5 = jnp.minimum(
                jnp.minimum(one[t - 2], one[t + 2]), jnp.minimum(two[t - 1], two[t + 1])
            )
            best = jnp.minimum(m1 + cost[0, t, spot], m2 + cost[1, t, spot])
            best = jnp.minimum(best, m5 + cost[2, t, spot])
            value = jnp.minimum(near[t], best)
            dst[s, t + REACH, spot] = value


def fill_rows(field, tiles, start):
    spot = pl.ds(start, 8)
    for s in range(field.shape[0]):
        for t in list(range(REACH)) + list(range(tiles - REACH, tiles)):
            keep_ends(field, s, t, spot, field[s, t + REACH, spot], tiles)


def fill_ends(field, tiles):
    def group(at, carry):
        for k in range(2):
            fill_rows(field, tiles, pl.multiple_of(PAD + at * 16 + k * 8, 8))
        return carry

    lax.fori_loop(0, (field.shape[2] - 3 * PAD) // 16, group, 0)


def scale_cost(cost):
    def group(at, carry):
        spot = pl.ds(pl.multiple_of(at * 8, 8), 8)
        for t in range(cost.shape[1]):
            value = cost[0, t, spot]
            cost[1, t, spot] = root_two * value
            cost[2, t, spot] = root_five * value
        return carry

    lax.fori_loop(0, cost.shape[2] // 8, group, 0)


def run_sweeps(first, second, cost, count, tiles, sweeps, groups):
    def sweep(src, dst, number):
        low = lax.shift_right_logical(number, 2)

        def group(at, carry):
            start = aligned(PAD + (low + 2 * at) * 8)
            fill_rows(dst, tiles, aligned(start - 8))
            relax_rows(src, dst, cost, count, tiles, start)
            fill_rows(dst, tiles, start)
            relax_rows(src, dst, cost, count, tiles, aligned(start + 8))
            return carry

        lax.fori_loop(0, groups // 2 - low, group, 0)
        fill_rows(dst, tiles, aligned(PAD + (groups - low - 1) * 8))

    def pair(at, carry):
        sweep(first, second, 2 * at + 1)
        sweep(second, first, 2 * at + 2)
        return carry

    fill_ends(first, tiles)
    lax.fori_loop(0, sweeps // 2, pair, 0)


def core(field, s, tiles):
    return field.at[s, REACH : REACH + tiles]


def fence(plane, planes, halo, total, field):
    for missing, at in ((plane == 0, PAD), (plane == planes - 1, PAD + halo + total)):

        @pl.when(missing)
        def _():
            for t in range(field.shape[0]):
                field[t, at : at + halo] = jnp.full((halo, LANES), far_value, jnp.float32)


def first_kernel(count, halo, planes, edge, has_cost, *refs):
    own, beside, rest = refs[0:4], refs[4:8], refs[8:]
    if has_cost:
        state, low_ref, high_ref, cost_out, one, two, cost, sem = rest
    else:
        cost_in, state, low_ref, high_ref, one, two, cost, sem = rest
    member, plane, _ = here()
    rows = own[0].shape[1]
    total = PLANE * rows
    tiles = cost.shape[1]
    sems = Semaphores(sem)

    def gather(slabs, field):
        copies = []
        for j in range(PLANE):
            at = aligned(PAD + halo + (member ^ j) * rows)
            copies.append(sems.copy(own[j].at[slabs], field.at[:, pl.ds(at, rows)]))
            below = sems.copy(beside[j].at[slabs], field.at[:, PAD + halo + total : PAD + total + 2 * halo])
            above = sems.copy(beside[j].at[slabs], field.at[:, PAD : PAD + halo])
            copies.append(((member == j) & (plane < planes - 1), below))
            copies.append(((member == PLANE - 1 - j) & (plane > 0), above))
        return copies

    copies = []
    for s in range(count):
        copies += gather(slice(s * tiles, (s + 1) * tiles), core(one, s, tiles))
    if has_cost:
        copies += gather(slice(count * tiles, (count + 1) * tiles), cost.at[0])
    else:
        copies.append(sems.copy(cost_in, cost))
    run_copies(copies)
    for s in range(count):
        fence(plane, planes, halo, total, core(one, s, tiles))
    if has_cost:
        fence(plane, planes, halo, total, cost.at[0])
        scale_cost(cost)
    run_sweeps(one, two, cost, count, tiles, FIRST, (total + 2 * halo) // 8)
    parity = lax.rem(plane, 2)
    top, bottom = PAD + halo, PAD + halo + total - edge
    low = aligned(parity * top + (1 - parity) * bottom)
    high = aligned((1 - parity) * top + parity * bottom)
    fields = [core(one, s, tiles) for s in range(count)] + ([cost.at[0]] if has_cost else [])
    copies = []
    for k, field in enumerate(fields):
        slabs = slice(k * tiles, (k + 1) * tiles)
        copies.append(sems.copy(field.at[:, pl.ds(low, edge)], low_ref.at[slabs]))
        copies.append(sems.copy(field.at[:, pl.ds(high, edge)], high_ref.at[slabs]))
        copies.append(sems.copy(field.at[:, PAD + halo : PAD + halo + total], state.at[slabs]))
    if has_cost:
        copies.append(sems.copy(cost, cost_out))
    run_copies(copies)


def last_kernel(count, sweeps, is_last, planes, state, even, odd, base, base_even, base_odd, *rest):
    if is_last:
        partial_ref, each_ref, r0, r1, r2, r3, one, two, cost, best, plain, sem = rest
    else:
        each_ref, best, one, two, cost, sem = rest
    member, plane, _ = here()
    total, halo = state.shape[1], even.shape[1]
    rows = total // PLANE
    tiles = cost.shape[1]
    own = tiles - 1
    sems = Semaphores(sem)
    parity = lax.rem(plane, 2)
    above, below = PAD, PAD + halo + total
    even_at = aligned(parity * above + (1 - parity) * below)
    odd_at = aligned((1 - parity) * above + parity * below)

    def gather(slabs, field, middle, from_even, from_odd):
        return [
            sems.copy(middle.at[slabs], field.at[:, PAD + halo : PAD + halo + total]),
            sems.copy(from_even.at[slabs], field.at[:, pl.ds(even_at, halo)]),
            sems.copy(from_odd.at[slabs], field.at[:, pl.ds(odd_at, halo)]),
        ]

    copies = gather(slice(count * tiles, (count + 1) * tiles), cost.at[0], base, base_even, base_odd)
    for s in range(count):
        copies += gather(slice(s * tiles, (s + 1) * tiles), core(one, s, tiles), state, even, odd)
    run_copies(copies)
    for s in range(count):
        fence(plane, planes, halo, total, core(one, s, tiles))
    fence(plane, planes, halo, total, cost.at[0])
    scale_cost(cost)
    run_sweeps(one, two, cost, count, tiles, sweeps, (total + 2 * halo) // 8)

    for t in range(tiles):
        low = None
        for s in range(count):
            each = jnp.minimum(
                one[s, REACH + t, PAD + halo : PAD + halo + total], jnp.float32(clip_value)
            )
            each = each / clip_value
            each_ref[s * tiles + t] = each
            low = each if low is None else jnp.minimum(low, each)
        best[t] = jnp.minimum(low, partial_ref[t]) if is_last else low
    if not is_last:
        return
    lane = lax.broadcasted_iota(jnp.int32, (8, LANES), 1)
    orders = [((lane + (LANES - j)) * inverse(tiles)) & (LANES - 1) for j in range(tiles)]
    chosen = [lax.rem(lane + t * LANES, tiles) for t in range(own)]

    def back(at, carry):
        spot = pl.ds(aligned(at * 8), 8)
        turned = [gather_lanes(best[j, spot], orders[j]) for j in range(tiles)]
        for t in range(own):
            value = turned[0]
            for j in range(1, tiles):
                value = jnp.where(chosen[t] == j, turned[j], value)
            plain[t, spot] = value
        return carry

    lax.fori_loop(0, total // 8, back, 0)
    run_copies(
        [
            sems.copy(plain.at[:, pl.ds(aligned((member ^ j) * rows), rows)], r)
            for j, r in enumerate((r0, r1, r2, r3))
        ]
    )


def gauge_kernel(cap, half, each_a, each_b, m0, m1, m2, m3, placed_ref, meta, sem):
    def exact(pick, value):
        found = None
        for _ in range(3):
            part = value.astype(jnp.bfloat16)
            value = value - part.astype(jnp.float32)
            term = jnp.dot(pick, part, preferred_element_type=jnp.float32)
            found = term if found is None else found + term
        return found

    member, plane, _ = here()
    sems = Semaphores(sem)
    run_copies(
        [
            sems.copy(m.at[m.shape[0] - 1], meta.at[member ^ j])
            for j, m in enumerate((m0, m1, m2, m3))
        ]
    )
    n, sources, slots = placed_ref.shape
    rows = each_a.shape[1] // PLANE
    tiles = each_a.shape[0] // half
    height = tiles * rows
    lane = lax.broadcasted_iota(jnp.int32, (LANES, LANES), 1).astype(jnp.float32)
    place = lax.broadcasted_iota(jnp.int32, (LANES, height), 1).astype(jnp.float32)
    spot = lax.broadcasted_iota(jnp.int32, (LANES, slots), 1).astype(jnp.float32)
    device = lax.broadcasted_iota(jnp.int32, (n, LANES), 0).astype(jnp.float32)
    filler = jnp.zeros((LANES - meta.shape[1], LANES), jnp.float32)
    offset = (member * height).astype(jnp.float32)
    placed_ref[...] = jnp.zeros(placed_ref.shape, jnp.float32)

    def block_of(q, carry):
        turned = jnp.transpose(jnp.concatenate([meta[q], filler], axis=0))
        pick = jnp.where(turned[:, 0:1] - offset == place, 1.0, 0.0).astype(jnp.bfloat16)
        at_lane = turned[:, 1:2] == lane
        base = ((plane * PLANE + q) * cap).astype(jnp.float32)
        at_slot = turned[:, 3:4] + base == spot
        to_owner = jnp.where(meta[q, 2:3] == device, 1.0, 0.0).astype(jnp.bfloat16)
        blocks = []
        for s in range(sources):
            each, k = (each_a, s) if s < half else (each_b, s - half)
            block = each[k * tiles : (k + 1) * tiles, pl.ds(aligned(q * rows), rows)]
            blocks.append(block.reshape(height, LANES))
        found = exact(pick, jnp.concatenate(blocks, axis=1))
        for s in range(sources):
            mine = jnp.where(at_lane, found[:, s * LANES : (s + 1) * LANES], 0.0)
            value = jnp.sum(mine, axis=1, keepdims=True)
            placed_ref[:, s] = placed_ref[:, s] + exact(to_owner, jnp.where(at_slot, value, 0.0))
        return carry

    lax.fori_loop(0, PLANE, block_of, 0)


def join_kernel(r0, r1, r2, r3, gauge_ref, out_ref, result_ref):
    member, _, _ = here()
    tiles, _, _ = r0.shape
    for j, r in enumerate((r0, r1, r2, r3)):
        base = (member ^ j) * (tiles * LANES)
        for t in range(tiles):
            out_ref[:, pl.ds(pl.multiple_of(base + t * LANES, LANES), LANES)] = r[t]
    result_ref[0] = jnp.sum(gauge_ref[...], axis=0)


def shape_of(*dims):
    return jax.ShapeDtypeStruct(dims, jnp.float32)


def on_device(slowness, ocean, start_times, source_cells, gauge_cells, gauge_owner):
    axis = "space"
    n = lax.axis_size(axis)
    rows, width = slowness.shape
    sources = start_times.shape[0]
    gauges = gauge_cells.shape[0]
    planes = n // PLANE
    later_sweeps = SWEEPS * BLOCKS - FIRST
    halo, edge = 2 * FIRST, 2 * later_sweeps
    total = rows * PLANE
    tiles = width // PLANE // LANES + 1
    assert n % (2 * PLANE) == 0 and width % (PLANE * LANES) == 0 and tiles % 2 == 1
    assert gauges == LANES and sources % 2 == 0 and rows == halo
    assert 2 * SWEEPS * BLOCKS <= SIDE and edge <= total and FIRST % 2 == later_sweeps % 2 == 0
    assert total % 16 == halo % 8 == edge % 8 == 0
    cap = max(2, 2 * gauges // n)
    half = sources // 2
    groups = (tuple(range(half)), tuple(range(half, sources)))
    size = half * tiles
    sizes = [size + tiles + 1, size]

    def call(kernel, out_shape, in_specs, out_specs, scratch, micros=2):
        return pl.pallas_call(
            kernel,
            out_shape=out_shape,
            in_specs=in_specs,
            out_specs=out_specs,
            scratch_shapes=scratch,
            compiler_params=pltpu.CompilerParams(vmem_limit_bytes=VMEM_BYTES),
            cost_estimate=pl.CostEstimate(
                flops=0, bytes_accessed=3_000_000 * micros, transcendentals=0
            ),
        )

    def vmem(*dims):
        return pltpu.VMEM(dims, jnp.float32)

    def semaphores(number):
        return pltpu.SemaphoreType.DMA((number,))

    packed = call(
        functools.partial(pack_kernel, groups),
        [shape_of(k, rows, LANES) for k in sizes for _ in range(PLANE)],
        [HBM] * 6,
        [VMEM] * (2 * PLANE),
        [
            pltpu.SMEM((sources,), jnp.int32),
            pltpu.VMEM((1, gauges), jnp.int32),
            pltpu.VMEM((1, gauges), jnp.int32),
            vmem(sources + 1, rows, width),
            pltpu.VMEM((rows, width), jnp.int32),
            vmem(PLANE, sources + 1, rows, LANES),
            semaphores(6),
        ],
    )(
        *(
            pltpu.with_memory_space_constraint(x, pltpu.HBM)
            for x in (
                source_cells,
                slowness,
                ocean,
                start_times,
                gauge_cells.reshape(1, gauges),
                gauge_owner.reshape(1, gauges),
            )
        )
    )

    def swap(x, j):
        return lax.ppermute(x, axis, [(d, d ^ j) for d in range(n)])

    def to_next_planes(x, j):
        up = [(z * PLANE, (z - 1) * PLANE + j) for z in range(1, planes)]
        down = [(z * PLANE + PLANE - 1, (z + 1) * PLANE + (PLANE - 1 - j)) for z in range(planes - 1)]
        return lax.ppermute(x, axis, up + down)

    def swap_planes(even, odd):
        pairs_even = [(d, (d // PLANE ^ 1) * PLANE + d % PLANE) for d in range(n)]
        pairs_odd = [
            (d, (((d // PLANE + 1) ^ 1) - 1) * PLANE + d % PLANE)
            for d in range(PLANE, n - PLANE)
        ]
        return lax.ppermute(even, axis, pairs_even), lax.ppermute(odd, axis, pairs_odd)

    pieces, beside = [], []
    for k in range(2):
        mine = packed[k * PLANE : (k + 1) * PLANE]
        pieces.append([mine[0]] + [swap(mine[j], j) for j in range(1, PLANE)])
        beside.append([to_next_planes(mine[j], j) for j in range(PLANE)])

    def buffers(deep):
        deep += 3 * PAD
        ends = tiles + 2 * REACH
        return [vmem(half, ends, deep, LANES), vmem(half, ends, deep, LANES), vmem(3, tiles, deep, LANES)]

    states, later, cost = [], [], None
    for k in range(2):
        slabs = size + (tiles if k == 0 else 0)
        scratch = buffers(total + 2 * halo)
        outs = call(
            functools.partial(first_kernel, half, halo, planes, edge, k == 0),
            [shape_of(slabs, total, LANES)]
            + [shape_of(slabs, edge, LANES)] * 2
            + ([shape_of(*scratch[2].shape)] if k == 0 else []),
            [ANY] * (2 * PLANE + k),
            [ANY] * (4 - k),
            scratch + [semaphores(3 * PLANE * (half + 1) + 3 * half + 4)],
            7,
        )(*pieces[k], *beside[k], *([] if k == 0 else [cost]))
        if k == 0:
            cost = outs[3]
        states.append(outs[0])
        later.append(swap_planes(outs[1], outs[2]))

    slots = n * cap
    each, partial = [], None
    for k in range(2):
        out_shape, out_specs, more = [shape_of(size, total, LANES)], [VMEM], []
        if k == 0:
            out_shape.append(shape_of(tiles, total, LANES))
            out_specs.append(VMEM)
        else:
            out_shape += [shape_of(tiles - 1, rows, LANES)] * PLANE
            out_specs += [ANY] * PLANE
            more = [vmem(tiles, total, LANES), vmem(tiles - 1, total, LANES)]
        outs = call(
            functools.partial(last_kernel, half, later_sweeps, k == 1, planes),
            out_shape,
            [ANY] * 6 + [VMEM] * k,
            out_specs,
            buffers(total + 2 * edge) + more + [semaphores(3 * (half + 1) + PLANE)],
            15,
        )(states[k], *later[k], states[0], *later[0], *([] if k == 0 else [partial]))
        each.append(outs[0])
        if k == 0:
            partial = outs[1]
        else:
            returned = outs[1:]

    back = [returned[0]] + [swap(returned[j], j) for j in range(1, PLANE)]
    gauge_call = call(
        functools.partial(gauge_kernel, cap, half),
        shape_of(n, sources, slots),
        [VMEM] * 2 + [ANY] * PLANE,
        VMEM,
        [vmem(PLANE, rows, LANES), semaphores(PLANE)],
        4,
    )
    placed = gauge_call(*each, *pieces[0])
    received = lax.all_to_all(placed, axis, split_axis=0, concat_axis=0, tiled=True)
    return call(
        join_kernel,
        (shape_of(rows, width), shape_of(1, sources, slots)),
        [VMEM] * (PLANE + 1),
        (VMEM, VMEM),
        [],
    )(*back, received)


def solution(mesh):
    return jax.shard_map(
        on_device,
        mesh=mesh,
        in_specs=(
            P(("groups", "space"), None),
            P(("groups", "space"), None),
            P("groups", "space", None),
            P("groups"),
            P(("groups", "space")),
            P(("groups", "space"), None),
        ),
        out_specs=(P(("groups", "space"), None), P(("groups", "space"), None, None)),
        check_vma=False,
    )
```

time: 373 us -> 104 us (0.28)
  starting transfers between devices: 191 us -> 38.1 us
  other arithmetic: 107 us -> 0 us
  Pallas kernels: 0 us -> 51.9 us
  local copies, waits for them, and re-layouts: 30.6 us -> 0 us
  blocking collectives: 17.9 us -> 0 us
  waiting for transfers between devices: 21.3 us -> 12.6 us
    ppermute x48 -> x21, starting transfers between devices: 191 us -> 33.6 us  [the longest x9 21.3 us: swap(): return lax.ppermute(x, axis, [(d, d ^ j) for d in range(n)])]
    min x24 -> x0, other arithmetic: 95 us -> none  [relax(): return jnp.minimum(shifted(0, 0), best)]
    pallas_call x0 -> x7, Pallas kernels: none -> 51.9 us  [the longest x2 29.3 us: on_device(): call(functools.partial(last_kernel, half, later_sweeps, k == 1, planes),...]
    all_to_all x1 -> x0, blocking collectives: 17.9 us -> none  [on_device(): lax.all_to_all(placed.reshape(sources, count, capacity), 'space', split_a...]
    div x1 -> x0, local copies, waits for them, and re-layouts: 16.2 us -> none  [on_device(): each_arrival = jnp.minimum(times, jnp.float32(clip_value)) / clip_value]
    gather x1 -> x0, local copies, waits for them, and re-layouts: 11.2 us -> none  [on_device(): values = each_arrival.reshape(sources, -1)[:, gauge_cells]]
    select_n x27 -> x0, other arithmetic: 9.4 us -> none  [the longest x24 7.45 us: fence(): return jnp.where(inside[None, :, None], field, jnp.float32(far_value))]
    ppermute x48 -> x21, waiting for transfers between devices: 21.3 us -> 12.1 us  [the longest x9 12.1 us: swap(): return lax.ppermute(x, axis, [(d, d ^ j) for d in range(n)])]
  transfers between devices with their start and end apart: 48 -> 22, of which waited for: 24 -> 6; matrix products, arithmetic and copies ran while one was open for 0% -> 0% of each run, Pallas kernels for 0% -> 28%
where the time goes in v4:
time: 104 us; the launch traced here: 103 us
  Pallas kernels  51.9 us (50%)
  starting transfers between devices  38.1 us (37%)
  waiting for transfers between devices  12.6 us (12%)
    pallas_call x2, Pallas kernels, on_device(): call(functools.partial(last_kernel, half, later_sweeps, k == 1, planes),...  29.3 us
    ppermute x9, starting transfers between devices, swap(): return lax.ppermute(x, axis, [(d, d ^ j) for d in range(n)])  21.3 us
    pallas_call x2, Pallas kernels, on_device(): call(functools.partial(first_kernel, half, halo, planes, edge, k == 0), [...  14.4 us
    ppermute x9, waiting for transfers between devices, swap(): return lax.ppermute(x, axis, [(d, d ^ j) for d in range(n)])  12.1 us
    ppermute x8, starting transfers between devices, to_next_planes(): return lax.ppermute(x, axis, up + down)  6.56 us
    all_to_all x1, starting transfers between devices, on_device(): lax.all_to_all(placed, axis, split_axis=0, concat_axis=0, tiled=True)  4.51 us
    ppermute x2, starting transfers between devices, swap_planes(): lax.ppermute(even, axis, pairs_even)  4.37 us
    pallas_call x1, Pallas kernels, on_device(): call(functools.partial(pack_kernel, groups), [shape_of(k, rows, LANES) fo...  3.83 us
  transfers between devices with their start and end apart: 22, of which 6 were waited for; matrix products, arithmetic and copies ran while one was open for 0% of the time, Pallas kernels for 28%

profile of v4, /device:TPU:0, one launch (start us, length us, event | category | flops | bytes accessed | tf_op | source)
XLA Modules:
  0.0 103.5 jit_solution(3909305416098532822)
XLA Ops:
  0.6 3.8 %shard_map.77 = (f32[28,16,128]{2,1,0:T(8,128)S(1)}, f32[28,16,128]{2,1,0:T(8,128)S(1)}, f32[28,16,128]{2,1,0:T(8,128)S(1)}, f32[28,16,128]{2,1,0:T(8,128)S(1)},...) custom-call(s32[4]{0:T(128)} %source_hbm.1, ...), custom_call_target="tpu_custom_call" | custom-call | bytes 6000000 | tf_op jit(solution)/shard_map/pallas_call | solution.py:486
  4.5 0.7 collective-permute-start.11
  5.2 1.2 %collective-permute-start.7 = (f32[28,16,128]{2,1,0:T(8,128)S(1)}, f32[28,16,128]{2,1,0:T(8,128)S(1)}, u32[]{:S(2)}, u32[]{:S(2)}) collective-permute-start(f32[28,16,128]{2,1,0:T(8,128)S(1)} %get-tuple-element.29), channel_id=1, source_target_pairs={{0,1},{1,0},{2,3},{3,2},{4,5},{5,4},{6,7},{7,6},{8,9},{9,8},{10,11... | collective-permute-start | bytes 688136 | tf_op jit(solution)/shard_map/ppermute | solution.py:515
  6.3 0.7 collective-permute-start.12
  7.0 5.5 %collective-permute-start.8 = (f32[28,16,128]{2,1,0:T(8,128)S(1)}, f32[28,16,128]{2,1,0:T(8,128)S(1)}, u32[]{:S(2)}, u32[]{:S(2)}) collective-permute-start(f32[28,16,128]{2,1,0:T(8,128)S(1)} %get-tuple-element.30), channel_id=1, source_target_pairs={{0,2},{1,3},{2,0},{3,1},{4,6},{5,7},{6,4},{7,5},{8,10},{9,11},{10,... | collective-permute-start | bytes 688136 | tf_op jit(solution)/shard_map/ppermute | solution.py:515
  12.5 0.7 collective-permute-start.13
  13.2 4.6 %collective-permute-start.9 = (f32[28,16,128]{2,1,0:T(8,128)S(1)}, f32[28,16,128]{2,1,0:T(8,128)S(1)}, u32[]{:S(2)}, u32[]{:S(2)}) collective-permute-start(f32[28,16,128]{2,1,0:T(8,128)S(1)} %get-tuple-element.31), channel_id=1, source_target_pairs={{0,3},{1,2},{2,1},{3,0},{4,7},{5,6},{6,5},{7,4},{8,11},{9,10},{10,... | collective-permute-start | bytes 688136 | tf_op jit(solution)/shard_map/ppermute | solution.py:515
  17.8 1.3 %collective-permute-start.10 = (f32[28,16,128]{2,1,0:T(8,128)S(1)}, f32[28,16,128]{2,1,0:T(8,128)S(1)}, u32[]{:S(2)}, u32[]{:S(2)}) collective-permute-start(f32[28,16,128]{2,1,0:T(8,128)S(1)} %get-tuple-element.28.refs_0_.m0), channel_id=1, source_target_pairs={{4,0},{8,4},{12,8},{3,7},{7,11},{11,15},{20,16},{24,20},{28,24},{1... | collective-permute-start | bytes 688136 | tf_op jit(solution)/shard_map/ppermute | solution.py:520
  19.1 1.3 %collective-permute-start.3 = (f32[18,16,128]{2,1,0:T(8,128)S(1)}, f32[18,16,128]{2,1,0:T(8,128)S(1)}, u32[]{:S(2)}, u32[]{:S(2)}) collective-permute-start(f32[18,16,128]{2,1,0:T(8,128)S(1)} %get-tuple-element.24.refs_0_), channel_id=1, source_target_pairs={{4,0},{8,4},{12,8},{3,7},{7,11},{11,15},{20,16},{24,20},{28,24},{1... | collective-permute-start | bytes 442376 | tf_op jit(solution)/shard_map/ppermute | solution.py:520
  20.4 3.0 %collective-permute-done.8.refs_2_.m2 = f32[28,16,128]{2,1,0:T(8,128)S(1)} collective-permute-done((f32[28,16,128]{2,1,0:T(8,128)S(1)}, f32[28,16,128]{2,1,0:T(8,128)S(1)}, u32[]{:S(2)}, u32[]{:S(2)}) %collective-permute-start.8) | collective-permute-done | bytes 229408 | tf_op jit(solution)/shard_map/ppermute | solution.py:515
  23.4 0.7 collective-permute-start.4
  24.2 3.3 %collective-permute-done.9.refs_3_.m3 = f32[28,16,128]{2,1,0:T(8,128)S(1)} collective-permute-done((f32[28,16,128]{2,1,0:T(8,128)S(1)}, f32[28,16,128]{2,1,0:T(8,128)S(1)}, u32[]{:S(2)}, u32[]{:S(2)}) %collective-permute-start.9) | collective-permute-done | bytes 229408 | tf_op jit(solution)/shard_map/ppermute | solution.py:515
  27.4 0.7 collective-permute-start.5
  28.1 3.3 %collective-permute-start.1 = (f32[18,16,128]{2,1,0:T(8,128)S(1)}, f32[18,16,128]{2,1,0:T(8,128)S(1)}, u32[]{:S(2)}, u32[]{:S(2)}) collective-permute-start(f32[18,16,128]{2,1,0:T(8,128)S(1)} %get-tuple-element.26), channel_id=1, source_target_pairs={{0,2},{1,3},{2,0},{3,1},{4,6},{5,7},{6,4},{7,5},{8,10},{9,11},{10,... | collective-permute-start | bytes 442376 | tf_op jit(solution)/shard_map/ppermute | solution.py:515
  31.4 7.4 %shard_map.78 = (f32[27,64,128]{2,1,0:T(8,128)S(1)}, f32[27,32,128]{2,1,0:T(8,128)S(1)}, f32[27,32,128]{2,1,0:T(8,128)S(1)}, f32[3,9,120,128]{3,2,1,0:T(8,128)S(1)}) custom-call(f32[28,16,128]{2,1,0:T(8,128)S(1)} %get-tuple-element.28.refs_0_.m0, f32[28,16,128]{2,1,0:T(8,128)S(1)} %collective-permute-done.7.refs_1_.m1, ...), custom_call_target="tpu_custom_call" | custom-call | bytes 21000000 | tf_op jit(solution)/shard_map/pallas_call | solution.py:545
  38.8 0.7 collective-permute-start.6
  39.5 4.6 %collective-permute-start.2 = (f32[18,16,128]{2,1,0:T(8,128)S(1)}, f32[18,16,128]{2,1,0:T(8,128)S(1)}, u32[]{:S(2)}, u32[]{:S(2)}) collective-permute-start(f32[18,16,128]{2,1,0:T(8,128)S(1)} %get-tuple-element.27), channel_id=1, source_target_pairs={{0,3},{1,2},{2,1},{3,0},{4,7},{5,6},{6,5},{7,4},{8,11},{9,10},{10,... | collective-permute-start | bytes 442376 | tf_op jit(solution)/shard_map/ppermute | solution.py:515
  44.2 1.6 %collective-permute-start.16 = (f32[27,32,128]{2,1,0:T(8,128)S(1)}, f32[27,32,128]{2,1,0:T(8,128)S(1)}, u32[]{:S(2)}, u32[]{:S(2)}) collective-permute-start(f32[27,32,128]{2,1,0:T(8,128)S(1)} %get-tuple-element.37), channel_id=1, source_target_pairs={{0,4},{1,5},{2,6},{3,7},{4,0},{5,1},{6,2},{7,3},{8,12},{9,13},{10,... | collective-permute-start | bytes 1327112 | tf_op jit(solution)/shard_map/ppermute | solution.py:528
  45.7 0.7 collective-permute-start.17
  46.5 1.4 %collective-permute-done.2.refs_3_ = f32[18,16,128]{2,1,0:T(8,128)S(1)} collective-permute-done((f32[18,16,128]{2,1,0:T(8,128)S(1)}, f32[18,16,128]{2,1,0:T(8,128)S(1)}, u32[]{:S(2)}, u32[]{:S(2)}) %collective-permute-start.2) | collective-permute-done | bytes 147488 | tf_op jit(solution)/shard_map/ppermute | solution.py:515
  47.9 7.0 %shard_map.79 = (f32[18,64,128]{2,1,0:T(8,128)S(1)}, f32[18,32,128]{2,1,0:T(8,128)S(1)}, f32[18,32,128]{2,1,0:T(8,128)S(1)}) custom-call(f32[18,16,128]{2,1,0:T(8,128)S(1)} %get-tuple-element.24.refs_0_, f32[18,16,128]{2,1,0:T(8,128)S(1)} %collective-permute-done.refs_1_, f32[18,16,128]{2,1,0:T(8,128)S(1)} %collective-permute-done.1.refs_2_, ...), custom_call_target="tpu_custom_call" | custom-call | bytes 21000000 | tf_op jit(solution)/shard_map/pallas_call | solution.py:545
  54.9 2.8 %collective-permute-start.14 = (f32[18,32,128]{2,1,0:T(8,128)S(1)}, f32[18,32,128]{2,1,0:T(8,128)S(1)}, u32[]{:S(2)}, u32[]{:S(2)}) collective-permute-start(f32[18,32,128]{2,1,0:T(8,128)S(1)} %get-tuple-element.34), channel_id=1, source_target_pairs={{0,4},{1,5},{2,6},{3,7},{4,0},{5,1},{6,2},{7,3},{8,12},{9,13},{10,... | collective-permute-start | bytes 884744 | tf_op jit(solution)/shard_map/ppermute | solution.py:528
  57.7 0.7 collective-permute-start.15
  58.4 14.2 %shard_map.80 = (f32[18,64,128]{2,1,0:T(8,128)S(1)}, f32[9,64,128]{2,1,0:T(8,128)S(1)}) custom-call(f32[27,64,128]{2,1,0:T(8,128)S(1)} %get-tuple-element.36.state.base, f32[27,32,128]{2,1,0:T(8,128)S(1)} %collective-permute-done.16.even.base_even, f32[27,32,128]{2,1,0:T(8,128)S(1)} %collective-permute-done.17.odd.base_odd, ...), custom_call_target="tpu_custom_call" | custom-call | bytes 45000000 | tf_op jit(solution)/shard_map/pallas_call | solution.py:571
  72.7 15.1 %shard_map.81 = (f32[18,64,128]{2,1,0:T(8,128)S(1)}, f32[8,16,128]{2,1,0:T(8,128)S(1)}, f32[8,16,128]{2,1,0:T(8,128)S(1)}, f32[8,16,128]{2,1,0:T(8,128)S(1)}, f32[8,16,128]{2,1,0:T(8,128)S(1)}) custom-call(f32[18,64,128]{2,1,0:T(8,128)S(1)} %get-tuple-element.33.state, f32[18,32,128]{2,1,0:T(8,128)S(1)} %collective-permute-done.14.even, ...), custom_call_target="tpu_custom_call" | custom-call | bytes 45000000 | tf_op jit(solution)/shard_map/pallas_call | solution.py:571
  87.8 3.6 %shard_map.82 = f32[16,4,256]{2,1,0:T(4,128)} custom-call(f32[18,64,128]{2,1,0:T(8,128)S(1)} %get-tuple-element.44.each_a, f32[18,64,128]{2,1,0:T(8,128)S(1)} %get-tuple-element.45.each_b, f32[28,16,128]{2,1,0:T(8,128)S(1)} %get-tuple-element.28.refs_0_.m0, f32[28,16,128]{2,1,0:T(8,128)S(1)} %collective-permute-done.7.refs_1_.m1, ...), custom_call_target="tpu_custom_call" | custom-call | bytes 12000000 | tf_op jit(solution)/shard_map/pallas_call | solution.py:594
  91.3 4.5 %all-to-all-start = ((f32[16,4,256]{2,1,0:T(4,128)}), f32[16,4,256]{2,1,0:T(4,128)S(1)}, u32[]{:S(2)}, u32[]{:S(2)}) async-start(f32[16,4,256]{2,1,0:T(4,128)} %shard_map.82), calls=%async_computation | async-start | bytes 131072 | tf_op jit(solution)/shard_map/all_to_all | solution.py:595
  96.3 1.6 %collective-permute-start.19 = (f32[8,16,128]{2,1,0:T(8,128)S(1)}, f32[8,16,128]{2,1,0:T(8,128)S(1)}, u32[]{:S(2)}, u32[]{:S(2)}) collective-permute-start(f32[8,16,128]{2,1,0:T(8,128)S(1)} %get-tuple-element.42), channel_id=1, source_target_pairs={{0,2},{1,3},{2,0},{3,1},{4,6},{5,7},{6,4},{7,5},{8,10},{9,11},{10,... | collective-permute-start | bytes 196616 | tf_op jit(solution)/shard_map/ppermute | solution.py:515
  97.9 2.9 %collective-permute-done.19.r2 = f32[8,16,128]{2,1,0:T(8,128)S(1)} collective-permute-done((f32[8,16,128]{2,1,0:T(8,128)S(1)}, f32[8,16,128]{2,1,0:T(8,128)S(1)}, u32[]{:S(2)}, u32[]{:S(2)}) %collective-permute-start.19) | collective-permute-done | bytes 65568 | tf_op jit(solution)/shard_map/ppermute | solution.py:515
  100.9 1.4 %collective-permute-done.20.r3 = f32[8,16,128]{2,1,0:T(8,128)S(1)} collective-permute-done((f32[8,16,128]{2,1,0:T(8,128)S(1)}, f32[8,16,128]{2,1,0:T(8,128)S(1)}, u32[]{:S(2)}, u32[]{:S(2)}) %collective-permute-start.20) | collective-permute-done | bytes 65568 | tf_op jit(solution)/shard_map/ppermute | solution.py:515
  102.3 0.5 all-to-all-done.gauge_ref
  102.8 0.7 shard_map.83
  (19 shorter events, 0.5 us)
Async XLA Ops:
  4.5 8.7 %collective-permute-start.11 = (f32[28,16,128]{2,1,0:T(8,128)S(1)}, f32[28,16,128]{2,1,0:T(8,128)S(1)}, u32[]{:S(2)}, u32[]{:S(2)}) collective-permute-start(f32[28,16,128]{2,1,0:T(8,128)S(1)} %get-tuple-element.29), channel_id=1, source_target_pairs={{4,1},{8,5},{12,9},{3,6},{7,10},{11,14},{20,17},{24,21},{28,25},{1... | collective-permute-start | bytes 688136 | tf_op jit(solution)/shard_map/ppermute | solution.py:520
  5.2 12.6 %collective-permute-start.7 = (f32[28,16,128]{2,1,0:T(8,128)S(1)}, f32[28,16,128]{2,1,0:T(8,128)S(1)}, u32[]{:S(2)}, u32[]{:S(2)}) collective-permute-start(f32[28,16,128]{2,1,0:T(8,128)S(1)} %get-tuple-element.29), channel_id=1, source_target_pairs={{0,1},{1,0},{2,3},{3,2},{4,5},{5,4},{6,7},{7,6},{8,9},{9,8},{10,11... | collective-permute-start | bytes 688136 | tf_op jit(solution)/shard_map/ppermute | solution.py:515
  6.3 12.7 %collective-permute-start.12 = (f32[28,16,128]{2,1,0:T(8,128)S(1)}, f32[28,16,128]{2,1,0:T(8,128)S(1)}, u32[]{:S(2)}, u32[]{:S(2)}) collective-permute-start(f32[28,16,128]{2,1,0:T(8,128)S(1)} %get-tuple-element.30), channel_id=1, source_target_pairs={{4,2},{8,6},{12,10},{3,5},{7,9},{11,13},{20,18},{24,22},{28,26},{1... | collective-permute-start | bytes 688136 | tf_op jit(solution)/shard_map/ppermute | solution.py:520
  7.0 16.4 %collective-permute-start.8 = (f32[28,16,128]{2,1,0:T(8,128)S(1)}, f32[28,16,128]{2,1,0:T(8,128)S(1)}, u32[]{:S(2)}, u32[]{:S(2)}) collective-permute-start(f32[28,16,128]{2,1,0:T(8,128)S(1)} %get-tuple-element.30), channel_id=1, source_target_pairs={{0,2},{1,3},{2,0},{3,1},{4,6},{5,7},{6,4},{7,5},{8,10},{9,11},{10,... | collective-permute-start | bytes 688136 | tf_op jit(solution)/shard_map/ppermute | solution.py:515
  12.5 11.6 %collective-permute-start.13 = (f32[28,16,128]{2,1,0:T(8,128)S(1)}, f32[28,16,128]{2,1,0:T(8,128)S(1)}, u32[]{:S(2)}, u32[]{:S(2)}) collective-permute-start(f32[28,16,128]{2,1,0:T(8,128)S(1)} %get-tuple-element.31), channel_id=1, source_target_pairs={{4,3},{8,7},{12,11},{3,4},{7,8},{11,12},{20,19},{24,23},{28,27},{1... | collective-permute-start | bytes 688136 | tf_op jit(solution)/shard_map/ppermute | solution.py:520
  13.2 14.2 %collective-permute-start.9 = (f32[28,16,128]{2,1,0:T(8,128)S(1)}, f32[28,16,128]{2,1,0:T(8,128)S(1)}, u32[]{:S(2)}, u32[]{:S(2)}) collective-permute-start(f32[28,16,128]{2,1,0:T(8,128)S(1)} %get-tuple-element.31), channel_id=1, source_target_pairs={{0,3},{1,2},{2,1},{3,0},{4,7},{5,6},{6,5},{7,4},{8,11},{9,10},{10,... | collective-permute-start | bytes 688136 | tf_op jit(solution)/shard_map/ppermute | solution.py:515
  17.8 10.3 %collective-permute-start.10 = (f32[28,16,128]{2,1,0:T(8,128)S(1)}, f32[28,16,128]{2,1,0:T(8,128)S(1)}, u32[]{:S(2)}, u32[]{:S(2)}) collective-permute-start(f32[28,16,128]{2,1,0:T(8,128)S(1)} %get-tuple-element.28.refs_0_.m0), channel_id=1, source_target_pairs={{4,0},{8,4},{12,8},{3,7},{7,11},{11,15},{20,16},{24,20},{28,24},{1... | collective-permute-start | bytes 688136 | tf_op jit(solution)/shard_map/ppermute | solution.py:520
  19.1 19.8 %collective-permute-start.3 = (f32[18,16,128]{2,1,0:T(8,128)S(1)}, f32[18,16,128]{2,1,0:T(8,128)S(1)}, u32[]{:S(2)}, u32[]{:S(2)}) collective-permute-start(f32[18,16,128]{2,1,0:T(8,128)S(1)} %get-tuple-element.24.refs_0_), channel_id=1, source_target_pairs={{4,0},{8,4},{12,8},{3,7},{7,11},{11,15},{20,16},{24,20},{28,24},{1... | collective-permute-start | bytes 442376 | tf_op jit(solution)/shard_map/ppermute | solution.py:520
  23.4 16.1 %collective-permute-start.4 = (f32[18,16,128]{2,1,0:T(8,128)S(1)}, f32[18,16,128]{2,1,0:T(8,128)S(1)}, u32[]{:S(2)}, u32[]{:S(2)}) collective-permute-start(f32[18,16,128]{2,1,0:T(8,128)S(1)} %get-tuple-element.25), channel_id=1, source_target_pairs={{4,1},{8,5},{12,9},{3,6},{7,10},{11,14},{20,17},{24,21},{28,25},{1... | collective-permute-start | bytes 442376 | tf_op jit(solution)/shard_map/ppermute | solution.py:520
  24.1 20.1 %collective-permute-start = (f32[18,16,128]{2,1,0:T(8,128)S(1)}, f32[18,16,128]{2,1,0:T(8,128)S(1)}, u32[]{:S(2)}, u32[]{:S(2)}) collective-permute-start(f32[18,16,128]{2,1,0:T(8,128)S(1)} %get-tuple-element.25), channel_id=1, source_target_pairs={{0,1},{1,0},{2,3},{3,2},{4,5},{5,4},{6,7},{7,6},{8,9},{9,8},{10,11... | collective-permute-start | bytes 442376 | tf_op jit(solution)/shard_map/ppermute | solution.py:515
  27.4 18.3 %collective-permute-start.5 = (f32[18,16,128]{2,1,0:T(8,128)S(1)}, f32[18,16,128]{2,1,0:T(8,128)S(1)}, u32[]{:S(2)}, u32[]{:S(2)}) collective-permute-start(f32[18,16,128]{2,1,0:T(8,128)S(1)} %get-tuple-element.26), channel_id=1, source_target_pairs={{4,2},{8,6},{12,10},{3,5},{7,9},{11,13},{20,18},{24,22},{28,26},{1... | collective-permute-start | bytes 442376 | tf_op jit(solution)/shard_map/ppermute | solution.py:520
  28.1 18.3 %collective-permute-start.1 = (f32[18,16,128]{2,1,0:T(8,128)S(1)}, f32[18,16,128]{2,1,0:T(8,128)S(1)}, u32[]{:S(2)}, u32[]{:S(2)}) collective-permute-start(f32[18,16,128]{2,1,0:T(8,128)S(1)} %get-tuple-element.26), channel_id=1, source_target_pairs={{0,2},{1,3},{2,0},{3,1},{4,6},{5,7},{6,4},{7,5},{8,10},{9,11},{10,... | collective-permute-start | bytes 442376 | tf_op jit(solution)/shard_map/ppermute | solution.py:515
  38.8 7.6 %collective-permute-start.6 = (f32[18,16,128]{2,1,0:T(8,128)S(1)}, f32[18,16,128]{2,1,0:T(8,128)S(1)}, u32[]{:S(2)}, u32[]{:S(2)}) collective-permute-start(f32[18,16,128]{2,1,0:T(8,128)S(1)} %get-tuple-element.27), channel_id=1, source_target_pairs={{4,3},{8,7},{12,11},{3,4},{7,8},{11,12},{20,19},{24,23},{28,27},{1... | collective-permute-start | bytes 442376 | tf_op jit(solution)/shard_map/ppermute | solution.py:520
  39.5 8.4 %collective-permute-start.2 = (f32[18,16,128]{2,1,0:T(8,128)S(1)}, f32[18,16,128]{2,1,0:T(8,128)S(1)}, u32[]{:S(2)}, u32[]{:S(2)}) collective-permute-start(f32[18,16,128]{2,1,0:T(8,128)S(1)} %get-tuple-element.27), channel_id=1, source_target_pairs={{0,3},{1,2},{2,1},{3,0},{4,7},{5,6},{6,5},{7,4},{8,11},{9,10},{10,... | collective-permute-start | bytes 442376 | tf_op jit(solution)/shard_map/ppermute | solution.py:515
  44.2 14.2 %collective-permute-start.16 = (f32[27,32,128]{2,1,0:T(8,128)S(1)}, f32[27,32,128]{2,1,0:T(8,128)S(1)}, u32[]{:S(2)}, u32[]{:S(2)}) collective-permute-start(f32[27,32,128]{2,1,0:T(8,128)S(1)} %get-tuple-element.37), channel_id=1, source_target_pairs={{0,4},{1,5},{2,6},{3,7},{4,0},{5,1},{6,2},{7,3},{8,12},{9,13},{10,... | collective-permute-start | bytes 1327112 | tf_op jit(solution)/shard_map/ppermute | solution.py:528
  45.7 12.7 %collective-permute-start.17 = (f32[27,32,128]{2,1,0:T(8,128)S(1)}, f32[27,32,128]{2,1,0:T(8,128)S(1)}, u32[]{:S(2)}, u32[]{:S(2)}) collective-permute-start(f32[27,32,128]{2,1,0:T(8,128)S(1)} %get-tuple-element.38), channel_id=1, source_target_pairs={{4,8},{5,9},{6,10},{7,11},{8,4},{9,5},{10,6},{11,7},{20,24},{21,25... | collective-permute-start | bytes 1327112 | tf_op jit(solution)/shard_map/ppermute | solution.py:528
  54.9 17.7 %collective-permute-start.14 = (f32[18,32,128]{2,1,0:T(8,128)S(1)}, f32[18,32,128]{2,1,0:T(8,128)S(1)}, u32[]{:S(2)}, u32[]{:S(2)}) collective-permute-start(f32[18,32,128]{2,1,0:T(8,128)S(1)} %get-tuple-element.34), channel_id=1, source_target_pairs={{0,4},{1,5},{2,6},{3,7},{4,0},{5,1},{6,2},{7,3},{8,12},{9,13},{10,... | collective-permute-start | bytes 884744 | tf_op jit(solution)/shard_map/ppermute | solution.py:528
  57.7 15.0 %collective-permute-start.15 = (f32[18,32,128]{2,1,0:T(8,128)S(1)}, f32[18,32,128]{2,1,0:T(8,128)S(1)}, u32[]{:S(2)}, u32[]{:S(2)}) collective-permute-start(f32[18,32,128]{2,1,0:T(8,128)S(1)} %get-tuple-element.35), channel_id=1, source_target_pairs={{4,8},{5,9},{6,10},{7,11},{8,4},{9,5},{10,6},{11,7},{20,24},{21,25... | collective-permute-start | bytes 884744 | tf_op jit(solution)/shard_map/ppermute | solution.py:528
  91.3 11.4 %all-to-all-start = ((f32[16,4,256]{2,1,0:T(4,128)}), f32[16,4,256]{2,1,0:T(4,128)S(1)}, u32[]{:S(2)}, u32[]{:S(2)}) async-start(f32[16,4,256]{2,1,0:T(4,128)} %shard_map.82), calls=%async_computation | async-start | bytes 131072 | tf_op jit(solution)/shard_map/all_to_all | solution.py:595
  95.9 2.0 %collective-permute-start.18 = (f32[8,16,128]{2,1,0:T(8,128)S(1)}, f32[8,16,128]{2,1,0:T(8,128)S(1)}, u32[]{:S(2)}, u32[]{:S(2)}) collective-permute-start(f32[8,16,128]{2,1,0:T(8,128)S(1)} %get-tuple-element.41), channel_id=1, source_target_pairs={{0,1},{1,0},{2,3},{3,2},{4,5},{5,4},{6,7},{7,6},{8,9},{9,8},{10,11... | collective-permute-start | bytes 196616 | tf_op jit(solution)/shard_map/ppermute | solution.py:515
  96.3 4.6 %collective-permute-start.19 = (f32[8,16,128]{2,1,0:T(8,128)S(1)}, f32[8,16,128]{2,1,0:T(8,128)S(1)}, u32[]{:S(2)}, u32[]{:S(2)}) collective-permute-start(f32[8,16,128]{2,1,0:T(8,128)S(1)} %get-tuple-element.42), channel_id=1, source_target_pairs={{0,2},{1,3},{2,0},{3,1},{4,6},{5,7},{6,4},{7,5},{8,10},{9,11},{10,... | collective-permute-start | bytes 196616 | tf_op jit(solution)/shard_map/ppermute | solution.py:515
  97.9 4.4 %collective-permute-start.20 = (f32[8,16,128]{2,1,0:T(8,128)S(1)}, f32[8,16,128]{2,1,0:T(8,128)S(1)}, u32[]{:S(2)}, u32[]{:S(2)}) collective-permute-start(f32[8,16,128]{2,1,0:T(8,128)S(1)} %get-tuple-element.43), channel_id=1, source_target_pairs={{0,3},{1,2},{2,1},{3,0},{4,7},{5,6},{6,5},{7,4},{8,11},{9,10},{10,... | collective-permute-start | bytes 196616 | tf_op jit(solution)/shard_map/ppermute | solution.py:515

commit v5 on v4

--- a/solution.py
+++ b/solution.py
@@ -66,35 +66,44 @@
     return pl.multiple_of(at, 8)
 
 
-def pack_kernel(groups, source_hbm, slow_hbm, ocean_hbm, start_hbm, cell_hbm, owner_hbm, *rest):
-    outs, (source_ref, cell_ref, owner_ref, field_ref, ocean_ref, side_ref, sem) = rest[:-7], rest[-7:]
-    sources, rows, width = start_hbm.shape
+def pack_kernel(group, has_cost, source_hbm, start_hbm, *rest):
+    if has_cost:
+        slow_hbm, ocean_hbm, cell_hbm, owner_hbm, *outs = rest[:-7]
+        source_ref, cell_ref, owner_ref, field_ref, ocean_ref, side_ref, sem = rest[-7:]
+    else:
+        outs = rest[:-4]
+        source_ref, field_ref, side_ref, sem = rest[-4:]
+    _, rows, width = start_hbm.shape
+    sources = len(group)
+    fields = field_ref.shape[0]
     own = width // PLANE
     tiles = own // LANES
     chunk = tiles + 1
     member, _, index = here()
     sems = Semaphores(sem)
-    run_copies(
-        [
-            sems.copy(start_hbm, field_ref.at[0:sources]),
+    copies = [
+        sems.copy(start_hbm.at[group[0] : group[-1] + 1], field_ref.at[0:sources]),
+        sems.copy(source_hbm, source_ref),
+    ]
+    if has_cost:
+        copies += [
             sems.copy(slow_hbm, field_ref.at[sources]),
             sems.copy(ocean_hbm, ocean_ref),
-            sems.copy(source_hbm, source_ref),
             sems.copy(cell_hbm, cell_ref),
             sems.copy(owner_hbm, owner_ref),
         ]
-    )
+    run_copies(copies)
     lane = lax.broadcasted_iota(jnp.int32, (8, LANES), 1)
     row = lax.broadcasted_iota(jnp.int32, (8, LANES), 0)
     far = jnp.full((8, LANES), far_value, jnp.float32)
 
-    for t in range(width // LANES):
+    for t in range(width // LANES if has_cost else 0):
         at = slice(t * LANES, (t + 1) * LANES)
         field_ref[sources, :, at] = jnp.where(
             ocean_ref[:, at] == 1, field_ref[sources, :, at], jnp.float32(land_cost)
         )
     for s in range(sources):
-        cell = source_ref[s] - index * (rows * width)
+        cell = source_ref[group[s]] - index * (rows * width)
 
         @pl.when((cell >= 0) & (cell < rows * width))
         def _():
@@ -104,7 +113,7 @@
             hit = (row == lax.rem(line, 8)) & (lane == lax.rem(column, LANES))
             field_ref[s, spot, at] = jnp.where(hit, 0.0, field_ref[s, spot, at])
 
-    for f in range(sources + 1):
+    for f in range(fields):
         for w in range(PLANE):
             for half in range(0, rows, 8):
                 right = (w + 1) * own
@@ -113,20 +122,14 @@
                 value_left = field_ref[f, half : half + 8, left : left + LANES] if w > 0 else far
                 side_ref[w, f, half : half + 8] = jnp.where(lane < SIDE, value_right, value_left)
 
-    order_of = []
-    for number, group in enumerate(groups):
-        order_of += [(number, k, s) for k, s in enumerate(group)]
-        if number == 0:
-            order_of.append((0, len(group), sources))
-
     def convert(j, carry):
         column = (((lane + (LANES - j)) * inverse(chunk)) & (LANES - 1)) * chunk + j
         masks = [column >= t * LANES for t in range(1, chunk)]
         order = (lane * chunk + j) & (LANES - 1)
         for shift in range(PLANE):
             window = member ^ shift
-            for number, slab, f in order_of:
-                out = outs[number * PLANE + shift]
+            out = outs[shift]
+            for f in range(fields):
                 for half in range(0, rows, 8):
                     mixed = None
                     for t in range(chunk):
@@ -136,10 +139,12 @@
                         else:
                             value = side_ref[window, f, half : half + 8]
                         mixed = value if t == 0 else jnp.where(masks[t - 1], value, mixed)
-                    out[slab * chunk + j, half : half + 8] = gather_lanes(mixed, order)
+                    out[f * chunk + j, half : half + 8] = gather_lanes(mixed, order)
         return carry
 
     lax.fori_loop(0, chunk, convert, 0)
+    if not has_cost:
+        return
 
     owner = owner_ref[...].astype(jnp.float32)
     across = jnp.broadcast_to(owner, (LANES, LANES))
@@ -256,8 +261,31 @@
                 field[t, at : at + halo] = jnp.full((halo, LANES), far_value, jnp.float32)
 
 
+def edge_kernel(slabs, p0, p1, p2, p3, even_ref, odd_ref, sem):
+    member, plane, _ = here()
+    parity = lax.rem(plane, 2)
+    sems = Semaphores(sem)
+    copies = []
+    for j, p in enumerate((p0, p1, p2, p3)):
+        first, last = member == j, member == PLANE - 1 - j
+        even = ((parity == 0) & last) | ((parity == 1) & first)
+        odd = ((parity == 0) & first) | ((parity == 1) & last)
+        copies.append((even, sems.copy(p.at[0:slabs], even_ref)))
+        copies.append((odd, sems.copy(p.at[0:slabs], odd_ref)))
+    run_copies(copies)
+
+
+def sides(plane, halo, total):
+    parity = lax.rem(plane, 2)
+    above, below = PAD, PAD + halo + total
+    return (
+        aligned(parity * above + (1 - parity) * below),
+        aligned((1 - parity) * above + parity * below),
+    )
+
+
 def first_kernel(count, halo, planes, edge, has_cost, *refs):
-    own, beside, rest = refs[0:4], refs[4:8], refs[8:]
+    own, (even, odd), rest = refs[0:4], refs[4:6], refs[6:]
     if has_cost:
         state, low_ref, high_ref, cost_out, one, two, cost, sem = rest
     else:
@@ -267,16 +295,15 @@
     total = PLANE * rows
     tiles = cost.shape[1]
     sems = Semaphores(sem)
+    even_at, odd_at = sides(plane, halo, total)
 
     def gather(slabs, field):
         copies = []
         for j in range(PLANE):
             at = aligned(PAD + halo + (member ^ j) * rows)
             copies.append(sems.copy(own[j].at[slabs], field.at[:, pl.ds(at, rows)]))
-            below = sems.copy(beside[j].at[slabs], field.at[:, PAD + halo + total : PAD + total + 2 * halo])
-            above = sems.copy(beside[j].at[slabs], field.at[:, PAD : PAD + halo])
-            copies.append(((member == j) & (plane < planes - 1), below))
-            copies.append(((member == PLANE - 1 - j) & (plane > 0), above))
+        for partner, at in ((even, even_at), (odd, odd_at)):
+            copies.append(sems.copy(partner.at[slabs], field.at[:, pl.ds(at, halo)]))
         return copies
 
     copies = []
@@ -320,10 +347,7 @@
     tiles = cost.shape[1]
     own = tiles - 1
     sems = Semaphores(sem)
-    parity = lax.rem(plane, 2)
-    above, below = PAD, PAD + halo + total
-    even_at = aligned(parity * above + (1 - parity) * below)
-    odd_at = aligned((1 - parity) * above + parity * below)
+    even_at, odd_at = sides(plane, halo, total)
 
     def gather(slabs, field, middle, from_even, from_odd):
         return [
@@ -378,12 +402,13 @@
 
 
 def gauge_kernel(cap, half, each_a, each_b, m0, m1, m2, m3, placed_ref, meta, sem):
-    def exact(pick, value):
-        found = None
+    def exact(left, pick, right):
+        value, found = right if left is None else left, None
         for _ in range(3):
             part = value.astype(jnp.bfloat16)
             value = value - part.astype(jnp.float32)
-            term = jnp.dot(pick, part, preferred_element_type=jnp.float32)
+            pair = (pick, part) if left is None else (part, pick)
+            term = jnp.dot(*pair, preferred_element_type=jnp.float32)
             found = term if found is None else found + term
         return found
 
@@ -413,17 +438,23 @@
         at_lane = turned[:, 1:2] == lane
         base = ((plane * PLANE + q) * cap).astype(jnp.float32)
         at_slot = turned[:, 3:4] + base == spot
-        to_owner = jnp.where(meta[q, 2:3] == device, 1.0, 0.0).astype(jnp.bfloat16)
+        at_slot = jnp.where(at_slot, 1.0, 0.0).astype(jnp.bfloat16)
         blocks = []
         for s in range(sources):
             each, k = (each_a, s) if s < half else (each_b, s - half)
             block = each[k * tiles : (k + 1) * tiles, pl.ds(aligned(q * rows), rows)]
             blocks.append(block.reshape(height, LANES))
-        found = exact(pick, jnp.concatenate(blocks, axis=1))
+        found = exact(None, pick, jnp.concatenate(blocks, axis=1))
+        values = jnp.zeros((LANES, LANES), jnp.float32)
         for s in range(sources):
             mine = jnp.where(at_lane, found[:, s * LANES : (s + 1) * LANES], 0.0)
-            value = jnp.sum(mine, axis=1, keepdims=True)
-            placed_ref[:, s] = placed_ref[:, s] + exact(to_owner, jnp.where(at_slot, value, 0.0))
+            values = jnp.where(lane == s, jnp.sum(mine, axis=1, keepdims=True), values)
+        values = jnp.transpose(values)
+        to_owner = meta[q, 2:3] == device
+        sent = [jnp.where(to_owner, values[s : s + 1], 0.0) for s in range(sources)]
+        added = exact(jnp.concatenate(sent, axis=0), at_slot, None)
+        for s in range(sources):
+            placed_ref[:, s] = placed_ref[:, s] + added[s * n : (s + 1) * n]
         return carry
 
     lax.fori_loop(0, PLANE, block_of, 0)
@@ -483,41 +514,25 @@
     def semaphores(number):
         return pltpu.SemaphoreType.DMA((number,))
 
-    packed = call(
-        functools.partial(pack_kernel, groups),
-        [shape_of(k, rows, LANES) for k in sizes for _ in range(PLANE)],
-        [HBM] * 6,
-        [VMEM] * (2 * PLANE),
-        [
-            pltpu.SMEM((sources,), jnp.int32),
-            pltpu.VMEM((1, gauges), jnp.int32),
-            pltpu.VMEM((1, gauges), jnp.int32),
-            vmem(sources + 1, rows, width),
-            pltpu.VMEM((rows, width), jnp.int32),
-            vmem(PLANE, sources + 1, rows, LANES),
-            semaphores(6),
-        ],
-    )(
-        *(
-            pltpu.with_memory_space_constraint(x, pltpu.HBM)
-            for x in (
-                source_cells,
-                slowness,
-                ocean,
-                start_times,
-                gauge_cells.reshape(1, gauges),
-                gauge_owner.reshape(1, gauges),
-            )
-        )
-    )
+    def pack(k):
+        fields = half + (k == 0)
+        more = [slowness, ocean, gauge_cells.reshape(1, gauges), gauge_owner.reshape(1, gauges)]
+        inputs = [source_cells, start_times] + (more if k == 0 else [])
+        line = pltpu.VMEM((1, gauges), jnp.int32)
+        return call(
+            functools.partial(pack_kernel, groups[k], k == 0),
+            [shape_of(sizes[k], rows, LANES)] * PLANE,
+            [HBM] * len(inputs),
+            [VMEM] * PLANE,
+            [pltpu.SMEM((sources,), jnp.int32)]
+            + ([line, line] if k == 0 else [])
+            + [vmem(fields, rows, width)]
+            + ([pltpu.VMEM((rows, width), jnp.int32)] if k == 0 else [])
+            + [vmem(PLANE, fields, rows, LANES), semaphores(6)],
+        )(*(pltpu.with_memory_space_constraint(x, pltpu.HBM) for x in inputs))
 
     def swap(x, j):
         return lax.ppermute(x, axis, [(d, d ^ j) for d in range(n)])
-
-    def to_next_planes(x, j):
-        up = [(z * PLANE, (z - 1) * PLANE + j) for z in range(1, planes)]
-        down = [(z * PLANE + PLANE - 1, (z + 1) * PLANE + (PLANE - 1 - j)) for z in range(planes - 1)]
-        return lax.ppermute(x, axis, up + down)
 
     def swap_planes(even, odd):
         pairs_even = [(d, (d // PLANE ^ 1) * PLANE + d % PLANE) for d in range(n)]
@@ -529,9 +544,20 @@
 
     pieces, beside = [], []
     for k in range(2):
-        mine = packed[k * PLANE : (k + 1) * PLANE]
+        mine = pack(k)
         pieces.append([mine[0]] + [swap(mine[j], j) for j in range(1, PLANE)])
-        beside.append([to_next_planes(mine[j], j) for j in range(PLANE)])
+    for k in range(2):
+        slabs = size + (tiles if k == 0 else 0)
+        edge_call = call(
+            functools.partial(edge_kernel, slabs),
+            [shape_of(slabs, rows, LANES)] * 2,
+            [ANY] * PLANE,
+            [ANY] * 2,
+            [semaphores(2 * PLANE)],
+            1,
+        )
+        edges = edge_call(*pieces[k])
+        beside.append(swap_planes(*edges))
 
     def buffers(deep):
         deep += 3 * PAD
@@ -547,9 +573,9 @@
             [shape_of(slabs, total, LANES)]
             + [shape_of(slabs, edge, LANES)] * 2
             + ([shape_of(*scratch[2].shape)] if k == 0 else []),
-            [ANY] * (2 * PLANE + k),
+            [ANY] * (PLANE + 2 + k),
             [ANY] * (4 - k),
-            scratch + [semaphores(3 * PLANE * (half + 1) + 3 * half + 4)],
+            scratch + [semaphores((PLANE + 2) * (half + 1) + 3 * half + 4)],
             7,
         )(*pieces[k], *beside[k], *([] if k == 0 else [cost]))
         if k == 0:

time: 104 us -> 105 us (level)
  starting transfers between devices: 38.1 us -> 27.2 us
  waiting for transfers between devices: 12.6 us -> 22.7 us
  Pallas kernels: 51.9 us -> 54.4 us
    ppermute x9, starting transfers between devices: 21.3 us -> 7.14 us  [swap(): return lax.ppermute(x, axis, [(d, d ^ j) for d in range(n)])]
    ppermute x9, waiting for transfers between devices: 12.1 us -> 22.2 us  [swap(): return lax.ppermute(x, axis, [(d, d ^ j) for d in range(n)])]
    ppermute x8 -> x0, starting transfers between devices: 6.56 us -> none  [to_next_planes(): return lax.ppermute(x, axis, up + down)]
    ppermute x2 -> x4, starting transfers between devices: 4.37 us -> 10.7 us  [swap_planes(): lax.ppermute(even, axis, pairs_even)]
    pallas_call x1 -> x4, Pallas kernels: 3.83 us -> 6.52 us  [the longest x2 5.44 us: pack(): call(functools.partial(pack_kernel, groups[k], k == 0), [shape_of(sizes[k...]
    all_to_all x1, starting transfers between devices: 4.51 us -> 6.71 us  [on_device(): lax.all_to_all(placed, axis, split_axis=0, concat_axis=0, tiled=True)]
    ppermute x2 -> x4, starting transfers between devices: 1.35 us -> 2.66 us  [swap_planes(): lax.ppermute(odd, axis, pairs_odd)]
  transfers between devices with their start and end apart: 22 -> 18, of which waited for: 6 -> 7; matrix products, arithmetic and copies ran while one was open for 0% -> 0% of each run, Pallas kernels for 28% -> 30%
where the time goes in v5:
time: 105 us
  Pallas kernels  54.4 us (52%)
  starting transfers between devices  27.2 us (26%)
  waiting for transfers between devices  22.7 us (22%)
    pallas_call x2, Pallas kernels, on_device(): call(functools.partial(last_kernel, half, later_sweeps, k == 1, planes),...  29.3 us
    ppermute x9, waiting for transfers between devices, swap(): return lax.ppermute(x, axis, [(d, d ^ j) for d in range(n)])  22.2 us
    pallas_call x2, Pallas kernels, on_device(): call(functools.partial(first_kernel, half, halo, planes, edge, k == 0), [...  14 us
    ppermute x4, starting transfers between devices, swap_planes(): lax.ppermute(even, axis, pairs_even)  10.7 us
    ppermute x9, starting transfers between devices, swap(): return lax.ppermute(x, axis, [(d, d ^ j) for d in range(n)])  7.14 us
    all_to_all x1, starting transfers between devices, on_device(): lax.all_to_all(placed, axis, split_axis=0, concat_axis=0, tiled=True)  6.71 us
    pallas_call x2, Pallas kernels, pack(): call(functools.partial(pack_kernel, groups[k], k == 0), [shape_of(sizes[k...  5.44 us
    pallas_call x1, Pallas kernels, on_device(): placed = gauge_call(*each, *pieces[0])  3.81 us
  transfers between devices with their start and end apart: 18, of which 7 were waited for; matrix products, arithmetic and copies ran while one was open for 0% of the time, Pallas kernels for 30%

profile of v5, /device:TPU:0, one launch (start us, length us, event | category | flops | bytes accessed | tf_op | source)
XLA Modules:
  0.0 105.1 jit_solution(5960066303826861905)
XLA Ops:
  0.6 3.0 %shard_map.79 = (f32[28,16,128]{2,1,0:T(8,128)S(1)}, f32[28,16,128]{2,1,0:T(8,128)S(1)}, f32[28,16,128]{2,1,0:T(8,128)S(1)}, f32[28,16,128]{2,1,0:T(8,128)S(1)}) custom-call(s32[4]{0:T(128)} %source_hbm.3, f32[4,16,4096]{2,1,0:T(8,128)} %start_hbm.3, f32[16,4096]{1,0:T(8,128)} %rest_0_.1, s32[16,4096]{1,0:T(8,128)} %rest_1_.1, s32[1,128]{1,0:T(1,128)} %bitcast.2, ...), custom_call_target="tpu_custom_call" | custom-call | bytes 6000000 | tf_op jit(solution)/shard_map/pallas_call | solution.py:522
  3.6 0.5 collective-permute-start.5
  4.2 2.6 %collective-permute-start.6 = (f32[28,16,128]{2,1,0:T(8,128)S(1)}, f32[28,16,128]{2,1,0:T(8,128)S(1)}, u32[]{:S(2)}, u32[]{:S(2)}) collective-permute-start(f32[28,16,128]{2,1,0:T(8,128)S(1)} %get-tuple-element.36), channel_id=1, source_target_pairs={{0,2},{1,3},{2,0},{3,1},{4,6},{5,7},{6,4},{7,5},{8,10},{9,11},{10,... | collective-permute-start | bytes 688136 | tf_op jit(solution)/shard_map/ppermute | solution.py:535
  6.8 6.4 %collective-permute-done.6.p2.refs_2_.m2 = f32[28,16,128]{2,1,0:T(8,128)S(1)} collective-permute-done((f32[28,16,128]{2,1,0:T(8,128)S(1)}, f32[28,16,128]{2,1,0:T(8,128)S(1)}, u32[]{:S(2)}, u32[]{:S(2)}) %collective-permute-start.6) | collective-permute-done | bytes 229408 | tf_op jit(solution)/shard_map/ppermute | solution.py:535
  13.2 4.4 %collective-permute-done.7.p3.refs_3_.m3 = f32[28,16,128]{2,1,0:T(8,128)S(1)} collective-permute-done((f32[28,16,128]{2,1,0:T(8,128)S(1)}, f32[28,16,128]{2,1,0:T(8,128)S(1)}, u32[]{:S(2)}, u32[]{:S(2)}) %collective-permute-start.7) | collective-permute-done | bytes 229408 | tf_op jit(solution)/shard_map/ppermute | solution.py:535
  17.6 0.6 shard_map.80
  18.3 1.6 %collective-permute-start.8 = (f32[27,16,128]{2,1,0:T(8,128)S(1)}, f32[27,16,128]{2,1,0:T(8,128)S(1)}, u32[]{:S(2)}, u32[]{:S(2)}) collective-permute-start(f32[27,16,128]{2,1,0:T(8,128)S(1)} %get-tuple-element.38), channel_id=1, source_target_pairs={{0,4},{1,5},{2,6},{3,7},{4,0},{5,1},{6,2},{7,3},{8,12},{9,13},{10,... | collective-permute-start | bytes 663560 | tf_op jit(solution)/shard_map/ppermute | solution.py:543
  19.8 0.7 collective-permute-start.9
  20.5 2.4 %shard_map.77 = (f32[18,16,128]{2,1,0:T(8,128)S(1)}, f32[18,16,128]{2,1,0:T(8,128)S(1)}, f32[18,16,128]{2,1,0:T(8,128)S(1)}, f32[18,16,128]{2,1,0:T(8,128)S(1)}) custom-call(s32[4]{0:T(128)} %source_hbm.3, f32[4,16,4096]{2,1,0:T(8,128)} %start_hbm.3), custom_call_target="tpu_custom_call" | custom-call | bytes 6000000 | tf_op jit(solution)/shard_map/pallas_call | solution.py:522
  23.1 1.5 %collective-permute-start.1 = (f32[18,16,128]{2,1,0:T(8,128)S(1)}, f32[18,16,128]{2,1,0:T(8,128)S(1)}, u32[]{:S(2)}, u32[]{:S(2)}) collective-permute-start(f32[18,16,128]{2,1,0:T(8,128)S(1)} %get-tuple-element.30), channel_id=1, source_target_pairs={{0,2},{1,3},{2,0},{3,1},{4,6},{5,7},{6,4},{7,5},{8,10},{9,11},{10,... | collective-permute-start | bytes 442376 | tf_op jit(solution)/shard_map/ppermute | solution.py:535
  24.6 0.3 collective-permute-start.2
  24.9 4.9 %collective-permute-done.1.p2.refs_2_ = f32[18,16,128]{2,1,0:T(8,128)S(1)} collective-permute-done((f32[18,16,128]{2,1,0:T(8,128)S(1)}, f32[18,16,128]{2,1,0:T(8,128)S(1)}, u32[]{:S(2)}, u32[]{:S(2)}) %collective-permute-start.1) | collective-permute-done | bytes 147488 | tf_op jit(solution)/shard_map/ppermute | solution.py:535
  29.8 2.1 %collective-permute-done.2.p3.refs_3_ = f32[18,16,128]{2,1,0:T(8,128)S(1)} collective-permute-done((f32[18,16,128]{2,1,0:T(8,128)S(1)}, f32[18,16,128]{2,1,0:T(8,128)S(1)}, u32[]{:S(2)}, u32[]{:S(2)}) %collective-permute-start.2) | collective-permute-done | bytes 147488 | tf_op jit(solution)/shard_map/ppermute | solution.py:535
  31.9 0.4 shard_map.78
  32.4 4.4 %collective-permute-start.3 = (f32[18,16,128]{2,1,0:T(8,128)S(1)}, f32[18,16,128]{2,1,0:T(8,128)S(1)}, u32[]{:S(2)}, u32[]{:S(2)}) collective-permute-start(f32[18,16,128]{2,1,0:T(8,128)S(1)} %get-tuple-element.32), channel_id=1, source_target_pairs={{0,4},{1,5},{2,6},{3,7},{4,0},{5,1},{6,2},{7,3},{8,12},{9,13},{10,... | collective-permute-start | bytes 442376 | tf_op jit(solution)/shard_map/ppermute | solution.py:543
  36.8 0.7 collective-permute-start.4
  37.5 7.2 %shard_map.81 = (f32[27,64,128]{2,1,0:T(8,128)S(1)}, f32[27,32,128]{2,1,0:T(8,128)S(1)}, f32[27,32,128]{2,1,0:T(8,128)S(1)}, f32[3,9,120,128]{3,2,1,0:T(8,128)S(1)}) custom-call(f32[28,16,128]{2,1,0:T(8,128)S(1)} %get-tuple-element.34.p0.refs_0_.m0, f32[28,16,128]{2,1,0:T(8,128)S(1)} %collective-permute-done.5.p1.refs_1_.m1, ...), custom_call_target="tpu_custom_call" | custom-call | bytes 21000000 | tf_op jit(solution)/shard_map/pallas_call | solution.py:571
  44.7 1.3 %collective-permute-start.12 = (f32[27,32,128]{2,1,0:T(8,128)S(1)}, f32[27,32,128]{2,1,0:T(8,128)S(1)}, u32[]{:S(2)}, u32[]{:S(2)}) collective-permute-start(f32[27,32,128]{2,1,0:T(8,128)S(1)} %get-tuple-element.45), channel_id=1, source_target_pairs={{0,4},{1,5},{2,6},{3,7},{4,0},{5,1},{6,2},{7,3},{8,12},{9,13},{10,... | collective-permute-start | bytes 1327112 | tf_op jit(solution)/shard_map/ppermute | solution.py:543
  46.0 0.7 collective-permute-start.13
  46.7 6.8 %shard_map.82 = (f32[18,64,128]{2,1,0:T(8,128)S(1)}, f32[18,32,128]{2,1,0:T(8,128)S(1)}, f32[18,32,128]{2,1,0:T(8,128)S(1)}) custom-call(f32[18,16,128]{2,1,0:T(8,128)S(1)} %get-tuple-element.28.p0.refs_0_, f32[18,16,128]{2,1,0:T(8,128)S(1)} %collective-permute-done.p1.refs_1_, f32[18,16,128]{2,1,0:T(8,128)S(1)} %collective-permute-done.1.p2.refs_2_, ...), custom_call_target="tpu_custom_call" | custom-call | bytes 21000000 | tf_op jit(solution)/shard_map/pallas_call | solution.py:571
  53.5 3.3 %collective-permute-start.10 = (f32[18,32,128]{2,1,0:T(8,128)S(1)}, f32[18,32,128]{2,1,0:T(8,128)S(1)}, u32[]{:S(2)}, u32[]{:S(2)}) collective-permute-start(f32[18,32,128]{2,1,0:T(8,128)S(1)} %get-tuple-element.42), channel_id=1, source_target_pairs={{0,4},{1,5},{2,6},{3,7},{4,0},{5,1},{6,2},{7,3},{8,12},{9,13},{10,... | collective-permute-start | bytes 884744 | tf_op jit(solution)/shard_map/ppermute | solution.py:543
  56.9 0.7 collective-permute-start.11
  57.6 14.2 %shard_map.83 = (f32[18,64,128]{2,1,0:T(8,128)S(1)}, f32[9,64,128]{2,1,0:T(8,128)S(1)}) custom-call(f32[27,64,128]{2,1,0:T(8,128)S(1)} %get-tuple-element.44.state.base, f32[27,32,128]{2,1,0:T(8,128)S(1)} %collective-permute-done.12.even.base_even, f32[27,32,128]{2,1,0:T(8,128)S(1)} %collective-permute-done.13.odd.base_odd, ...), custom_call_target="tpu_custom_call" | custom-call | bytes 45000000 | tf_op jit(solution)/shard_map/pallas_call | solution.py:597
  71.8 15.1 %shard_map.84 = (f32[18,64,128]{2,1,0:T(8,128)S(1)}, f32[8,16,128]{2,1,0:T(8,128)S(1)}, f32[8,16,128]{2,1,0:T(8,128)S(1)}, f32[8,16,128]{2,1,0:T(8,128)S(1)}, f32[8,16,128]{2,1,0:T(8,128)S(1)}) custom-call(f32[18,64,128]{2,1,0:T(8,128)S(1)} %get-tuple-element.41.state, f32[18,32,128]{2,1,0:T(8,128)S(1)} %collective-permute-done.10.even, ...), custom_call_target="tpu_custom_call" | custom-call | bytes 45000000 | tf_op jit(solution)/shard_map/pallas_call | solution.py:597
  86.9 3.8 %shard_map.85 = f32[16,4,256]{2,1,0:T(4,128)} custom-call(f32[18,64,128]{2,1,0:T(8,128)S(1)} %get-tuple-element.52.each_a, f32[18,64,128]{2,1,0:T(8,128)S(1)} %get-tuple-element.53.each_b, f32[28,16,128]{2,1,0:T(8,128)S(1)} %get-tuple-element.34.p0.refs_0_.m0, f32[28,16,128]{2,1,0:T(8,128)S(1)} %collective-permute-done.5.p1.refs_1_.m1, ...), custom_call_target="tpu_custom_call" | custom-call | bytes 12000000 | tf_op jit(solution)/shard_map/pallas_call | solution.py:620
  90.7 6.7 %all-to-all-start = ((f32[16,4,256]{2,1,0:T(4,128)}), f32[16,4,256]{2,1,0:T(4,128)S(1)}, u32[]{:S(2)}, u32[]{:S(2)}) async-start(f32[16,4,256]{2,1,0:T(4,128)} %shard_map.85), calls=%async_computation | async-start | bytes 131072 | tf_op jit(solution)/shard_map/all_to_all | solution.py:621
  97.4 0.4 collective-permute-start.14
  97.8 1.6 %collective-permute-start.15 = (f32[8,16,128]{2,1,0:T(8,128)S(1)}, f32[8,16,128]{2,1,0:T(8,128)S(1)}, u32[]{:S(2)}, u32[]{:S(2)}) collective-permute-start(f32[8,16,128]{2,1,0:T(8,128)S(1)} %get-tuple-element.50), channel_id=1, source_target_pairs={{0,2},{1,3},{2,0},{3,1},{4,6},{5,7},{6,4},{7,5},{8,10},{9,11},{10,... | collective-permute-start | bytes 196616 | tf_op jit(solution)/shard_map/ppermute | solution.py:535
  99.5 2.9 %collective-permute-done.15.r2 = f32[8,16,128]{2,1,0:T(8,128)S(1)} collective-permute-done((f32[8,16,128]{2,1,0:T(8,128)S(1)}, f32[8,16,128]{2,1,0:T(8,128)S(1)}, u32[]{:S(2)}, u32[]{:S(2)}) %collective-permute-start.15) | collective-permute-done | bytes 65568 | tf_op jit(solution)/shard_map/ppermute | solution.py:535
  102.4 1.4 %collective-permute-done.16.r3 = f32[8,16,128]{2,1,0:T(8,128)S(1)} collective-permute-done((f32[8,16,128]{2,1,0:T(8,128)S(1)}, f32[8,16,128]{2,1,0:T(8,128)S(1)}, u32[]{:S(2)}, u32[]{:S(2)}) %collective-permute-start.16) | collective-permute-done | bytes 65568 | tf_op jit(solution)/shard_map/ppermute | solution.py:535
  103.8 0.5 all-to-all-done.gauge_ref
  104.3 0.7 shard_map.86
  (14 shorter events, 0.2 us)
Async XLA Ops:
  3.6 3.2 %collective-permute-start.5 = (f32[28,16,128]{2,1,0:T(8,128)S(1)}, f32[28,16,128]{2,1,0:T(8,128)S(1)}, u32[]{:S(2)}, u32[]{:S(2)}) collective-permute-start(f32[28,16,128]{2,1,0:T(8,128)S(1)} %get-tuple-element.35), channel_id=1, source_target_pairs={{0,1},{1,0},{2,3},{3,2},{4,5},{5,4},{6,7},{7,6},{8,9},{9,8},{10,11... | collective-permute-start | bytes 688136 | tf_op jit(solution)/shard_map/ppermute | solution.py:535
  4.2 9.0 %collective-permute-start.6 = (f32[28,16,128]{2,1,0:T(8,128)S(1)}, f32[28,16,128]{2,1,0:T(8,128)S(1)}, u32[]{:S(2)}, u32[]{:S(2)}) collective-permute-start(f32[28,16,128]{2,1,0:T(8,128)S(1)} %get-tuple-element.36), channel_id=1, source_target_pairs={{0,2},{1,3},{2,0},{3,1},{4,6},{5,7},{6,4},{7,5},{8,10},{9,11},{10,... | collective-permute-start | bytes 688136 | tf_op jit(solution)/shard_map/ppermute | solution.py:535
  6.8 10.8 %collective-permute-start.7 = (f32[28,16,128]{2,1,0:T(8,128)S(1)}, f32[28,16,128]{2,1,0:T(8,128)S(1)}, u32[]{:S(2)}, u32[]{:S(2)}) collective-permute-start(f32[28,16,128]{2,1,0:T(8,128)S(1)} %get-tuple-element.37), channel_id=1, source_target_pairs={{0,3},{1,2},{2,1},{3,0},{4,7},{5,6},{6,5},{7,4},{8,11},{9,10},{10,... | collective-permute-start | bytes 688136 | tf_op jit(solution)/shard_map/ppermute | solution.py:535
  18.3 19.2 %collective-permute-start.8 = (f32[27,16,128]{2,1,0:T(8,128)S(1)}, f32[27,16,128]{2,1,0:T(8,128)S(1)}, u32[]{:S(2)}, u32[]{:S(2)}) collective-permute-start(f32[27,16,128]{2,1,0:T(8,128)S(1)} %get-tuple-element.38), channel_id=1, source_target_pairs={{0,4},{1,5},{2,6},{3,7},{4,0},{5,1},{6,2},{7,3},{8,12},{9,13},{10,... | collective-permute-start | bytes 663560 | tf_op jit(solution)/shard_map/ppermute | solution.py:543
  19.8 17.6 %collective-permute-start.9 = (f32[27,16,128]{2,1,0:T(8,128)S(1)}, f32[27,16,128]{2,1,0:T(8,128)S(1)}, u32[]{:S(2)}, u32[]{:S(2)}) collective-permute-start(f32[27,16,128]{2,1,0:T(8,128)S(1)} %get-tuple-element.39), channel_id=1, source_target_pairs={{4,8},{5,9},{6,10},{7,11},{8,4},{9,5},{10,6},{11,7},{20,24},{21,25... | collective-permute-start | bytes 663560 | tf_op jit(solution)/shard_map/ppermute | solution.py:543
  23.0 1.9 %collective-permute-start = (f32[18,16,128]{2,1,0:T(8,128)S(1)}, f32[18,16,128]{2,1,0:T(8,128)S(1)}, u32[]{:S(2)}, u32[]{:S(2)}) collective-permute-start(f32[18,16,128]{2,1,0:T(8,128)S(1)} %get-tuple-element.29), channel_id=1, source_target_pairs={{0,1},{1,0},{2,3},{3,2},{4,5},{5,4},{6,7},{7,6},{8,9},{9,8},{10,11... | collective-permute-start | bytes 442376 | tf_op jit(solution)/shard_map/ppermute | solution.py:535
  23.1 6.7 %collective-permute-start.1 = (f32[18,16,128]{2,1,0:T(8,128)S(1)}, f32[18,16,128]{2,1,0:T(8,128)S(1)}, u32[]{:S(2)}, u32[]{:S(2)}) collective-permute-start(f32[18,16,128]{2,1,0:T(8,128)S(1)} %get-tuple-element.30), channel_id=1, source_target_pairs={{0,2},{1,3},{2,0},{3,1},{4,6},{5,7},{6,4},{7,5},{8,10},{9,11},{10,... | collective-permute-start | bytes 442376 | tf_op jit(solution)/shard_map/ppermute | solution.py:535
  24.6 7.3 %collective-permute-start.2 = (f32[18,16,128]{2,1,0:T(8,128)S(1)}, f32[18,16,128]{2,1,0:T(8,128)S(1)}, u32[]{:S(2)}, u32[]{:S(2)}) collective-permute-start(f32[18,16,128]{2,1,0:T(8,128)S(1)} %get-tuple-element.31), channel_id=1, source_target_pairs={{0,3},{1,2},{2,1},{3,0},{4,7},{5,6},{6,5},{7,4},{8,11},{9,10},{10,... | collective-permute-start | bytes 442376 | tf_op jit(solution)/shard_map/ppermute | solution.py:535
  32.4 14.3 %collective-permute-start.3 = (f32[18,16,128]{2,1,0:T(8,128)S(1)}, f32[18,16,128]{2,1,0:T(8,128)S(1)}, u32[]{:S(2)}, u32[]{:S(2)}) collective-permute-start(f32[18,16,128]{2,1,0:T(8,128)S(1)} %get-tuple-element.32), channel_id=1, source_target_pairs={{0,4},{1,5},{2,6},{3,7},{4,0},{5,1},{6,2},{7,3},{8,12},{9,13},{10,... | collective-permute-start | bytes 442376 | tf_op jit(solution)/shard_map/ppermute | solution.py:543
  36.8 9.9 %collective-permute-start.4 = (f32[18,16,128]{2,1,0:T(8,128)S(1)}, f32[18,16,128]{2,1,0:T(8,128)S(1)}, u32[]{:S(2)}, u32[]{:S(2)}) collective-permute-start(f32[18,16,128]{2,1,0:T(8,128)S(1)} %get-tuple-element.33), channel_id=1, source_target_pairs={{4,8},{5,9},{6,10},{7,11},{8,4},{9,5},{10,6},{11,7},{20,24},{21,25... | collective-permute-start | bytes 442376 | tf_op jit(solution)/shard_map/ppermute | solution.py:543
  44.7 12.8 %collective-permute-start.12 = (f32[27,32,128]{2,1,0:T(8,128)S(1)}, f32[27,32,128]{2,1,0:T(8,128)S(1)}, u32[]{:S(2)}, u32[]{:S(2)}) collective-permute-start(f32[27,32,128]{2,1,0:T(8,128)S(1)} %get-tuple-element.45), channel_id=1, source_target_pairs={{0,4},{1,5},{2,6},{3,7},{4,0},{5,1},{6,2},{7,3},{8,12},{9,13},{10,... | collective-permute-start | bytes 1327112 | tf_op jit(solution)/shard_map/ppermute | solution.py:543
  46.0 11.5 %collective-permute-start.13 = (f32[27,32,128]{2,1,0:T(8,128)S(1)}, f32[27,32,128]{2,1,0:T(8,128)S(1)}, u32[]{:S(2)}, u32[]{:S(2)}) collective-permute-start(f32[27,32,128]{2,1,0:T(8,128)S(1)} %get-tuple-element.46), channel_id=1, source_target_pairs={{4,8},{5,9},{6,10},{7,11},{8,4},{9,5},{10,6},{11,7},{20,24},{21,25... | collective-permute-start | bytes 1327112 | tf_op jit(solution)/shard_map/ppermute | solution.py:543
  53.5 18.3 %collective-permute-start.10 = (f32[18,32,128]{2,1,0:T(8,128)S(1)}, f32[18,32,128]{2,1,0:T(8,128)S(1)}, u32[]{:S(2)}, u32[]{:S(2)}) collective-permute-start(f32[18,32,128]{2,1,0:T(8,128)S(1)} %get-tuple-element.42), channel_id=1, source_target_pairs={{0,4},{1,5},{2,6},{3,7},{4,0},{5,1},{6,2},{7,3},{8,12},{9,13},{10,... | collective-permute-start | bytes 884744 | tf_op jit(solution)/shard_map/ppermute | solution.py:543
  56.9 15.0 %collective-permute-start.11 = (f32[18,32,128]{2,1,0:T(8,128)S(1)}, f32[18,32,128]{2,1,0:T(8,128)S(1)}, u32[]{:S(2)}, u32[]{:S(2)}) collective-permute-start(f32[18,32,128]{2,1,0:T(8,128)S(1)} %get-tuple-element.43), channel_id=1, source_target_pairs={{4,8},{5,9},{6,10},{7,11},{8,4},{9,5},{10,6},{11,7},{20,24},{21,25... | collective-permute-start | bytes 884744 | tf_op jit(solution)/shard_map/ppermute | solution.py:543
  90.7 13.6 %all-to-all-start = ((f32[16,4,256]{2,1,0:T(4,128)}), f32[16,4,256]{2,1,0:T(4,128)S(1)}, u32[]{:S(2)}, u32[]{:S(2)}) async-start(f32[16,4,256]{2,1,0:T(4,128)} %shard_map.85), calls=%async_computation | async-start | bytes 131072 | tf_op jit(solution)/shard_map/all_to_all | solution.py:621
  97.4 2.0 %collective-permute-start.14 = (f32[8,16,128]{2,1,0:T(8,128)S(1)}, f32[8,16,128]{2,1,0:T(8,128)S(1)}, u32[]{:S(2)}, u32[]{:S(2)}) collective-permute-start(f32[8,16,128]{2,1,0:T(8,128)S(1)} %get-tuple-element.49), channel_id=1, source_target_pairs={{0,1},{1,0},{2,3},{3,2},{4,5},{5,4},{6,7},{7,6},{8,9},{9,8},{10,11... | collective-permute-start | bytes 196616 | tf_op jit(solution)/shard_map/ppermute | solution.py:535
  97.8 4.6 %collective-permute-start.15 = (f32[8,16,128]{2,1,0:T(8,128)S(1)}, f32[8,16,128]{2,1,0:T(8,128)S(1)}, u32[]{:S(2)}, u32[]{:S(2)}) collective-permute-start(f32[8,16,128]{2,1,0:T(8,128)S(1)} %get-tuple-element.50), channel_id=1, source_target_pairs={{0,2},{1,3},{2,0},{3,1},{4,6},{5,7},{6,4},{7,5},{8,10},{9,11},{10,... | collective-permute-start | bytes 196616 | tf_op jit(solution)/shard_map/ppermute | solution.py:535
  99.5 4.4 %collective-permute-start.16 = (f32[8,16,128]{2,1,0:T(8,128)S(1)}, f32[8,16,128]{2,1,0:T(8,128)S(1)}, u32[]{:S(2)}, u32[]{:S(2)}) collective-permute-start(f32[8,16,128]{2,1,0:T(8,128)S(1)} %get-tuple-element.51), channel_id=1, source_target_pairs={{0,3},{1,2},{2,1},{3,0},{4,7},{5,6},{6,5},{7,4},{8,11},{9,10},{10,... | collective-permute-start | bytes 196616 | tf_op jit(solution)/shard_map/ppermute | solution.py:535

commit v6 on v5

--- a/solution.py
+++ b/solution.py
@@ -228,16 +228,14 @@
     def sweep(src, dst, number):
         low = lax.shift_right_logical(number, 2)
 
-        def group(at, carry):
-            start = aligned(PAD + (low + 2 * at) * 8)
-            fill_rows(dst, tiles, aligned(start - 8))
-            relax_rows(src, dst, cost, count, tiles, start)
-            fill_rows(dst, tiles, start)
-            relax_rows(src, dst, cost, count, tiles, aligned(start + 8))
-            return carry
-
-        lax.fori_loop(0, groups // 2 - low, group, 0)
-        fill_rows(dst, tiles, aligned(PAD + (groups - low - 1) * 8))
+        for step in range(sweeps // 4 + 1):
+
+            @pl.when(low == step)
+            def _():
+                for at in range(step, groups - step):
+                    fill_rows(dst, tiles, PAD + 8 * at - 8)
+                    relax_rows(src, dst, cost, count, tiles, PAD + 8 * at)
+                fill_rows(dst, tiles, PAD + 8 * (groups - step - 1))
 
     def pair(at, carry):
         sweep(first, second, 2 * at + 1)
@@ -430,9 +428,8 @@
     device = lax.broadcasted_iota(jnp.int32, (n, LANES), 0).astype(jnp.float32)
     filler = jnp.zeros((LANES - meta.shape[1], LANES), jnp.float32)
     offset = (member * height).astype(jnp.float32)
-    placed_ref[...] = jnp.zeros(placed_ref.shape, jnp.float32)
-
-    def block_of(q, carry):
+    totals = [None] * sources
+    for q in range(PLANE):
         turned = jnp.transpose(jnp.concatenate([meta[q], filler], axis=0))
         pick = jnp.where(turned[:, 0:1] - offset == place, 1.0, 0.0).astype(jnp.bfloat16)
         at_lane = turned[:, 1:2] == lane
@@ -442,7 +439,7 @@
         blocks = []
         for s in range(sources):
             each, k = (each_a, s) if s < half else (each_b, s - half)
-            block = each[k * tiles : (k + 1) * tiles, pl.ds(aligned(q * rows), rows)]
+            block = each[k * tiles : (k + 1) * tiles, q * rows : (q + 1) * rows]
             blocks.append(block.reshape(height, LANES))
         found = exact(None, pick, jnp.concatenate(blocks, axis=1))
         values = jnp.zeros((LANES, LANES), jnp.float32)
@@ -454,10 +451,10 @@
         sent = [jnp.where(to_owner, values[s : s + 1], 0.0) for s in range(sources)]
         added = exact(jnp.concatenate(sent, axis=0), at_slot, None)
         for s in range(sources):
-            placed_ref[:, s] = placed_ref[:, s] + added[s * n : (s + 1) * n]
-        return carry
-
-    lax.fori_loop(0, PLANE, block_of, 0)
+            term = added[s * n : (s + 1) * n]
+            totals[s] = term if q == 0 else totals[s] + term
+    for s in range(sources):
+        placed_ref[:, s] = totals[s]
 
 
 def join_kernel(r0, r1, r2, r3, gauge_ref, out_ref, result_ref):
@@ -568,7 +565,7 @@
     for k in range(2):
         slabs = size + (tiles if k == 0 else 0)
         scratch = buffers(total + 2 * halo)
-        outs = call(
+        first_call = call(
             functools.partial(first_kernel, half, halo, planes, edge, k == 0),
             [shape_of(slabs, total, LANES)]
             + [shape_of(slabs, edge, LANES)] * 2
@@ -577,7 +574,8 @@
             [ANY] * (4 - k),
             scratch + [semaphores((PLANE + 2) * (half + 1) + 3 * half + 4)],
             7,
-        )(*pieces[k], *beside[k], *([] if k == 0 else [cost]))
+        )
+        outs = first_call(*pieces[k], *beside[k], *([] if k == 0 else [cost]))
         if k == 0:
             cost = outs[3]
         states.append(outs[0])

time: 105 us -> 93.7 us (0.89)
  Pallas kernels: 54.4 us -> 40.3 us
  waiting for transfers between devices: 22.7 us -> 24.9 us
    pallas_call x2, Pallas kernels: 29.3 us -> 20.4 us  [on_device(): call(functools.partial(last_kernel, half, later_sweeps, k == 1, planes),...]
    pallas_call x2, Pallas kernels: 14 us -> 10.1 us  [on_device(): outs = first_call(*pieces[k], *beside[k], *([] if k == 0 else [cost]))]
    ppermute x4, waiting for transfers between devices: 0.01 us -> 2.18 us  [swap_planes(): lax.ppermute(even, axis, pairs_even)]
    pallas_call x1, Pallas kernels: 3.81 us -> 2.53 us  [on_device(): placed = gauge_call(*each, *pieces[0])]
  transfers between devices with their start and end apart: 18 -> 18, of which waited for: 7 -> 8; matrix products, arithmetic and copies ran while one was open for 0% -> 0% of each run, Pallas kernels for 30% -> 25%
where the time goes in v6:
time: 93.7 us; the launch traced here: 93.4 us
  Pallas kernels  40.3 us (43%)
  starting transfers between devices  27.4 us (29%)
  waiting for transfers between devices  24.9 us (27%)
    ppermute x9, waiting for transfers between devices, swap(): return lax.ppermute(x, axis, [(d, d ^ j) for d in range(n)])  22.2 us
    pallas_call x2, Pallas kernels, on_device(): call(functools.partial(last_kernel, half, later_sweeps, k == 1, planes),...  20.4 us
    ppermute x4, starting transfers between devices, swap_planes(): lax.ppermute(even, axis, pairs_even)  10.7 us
    pallas_call x2, Pallas kernels, on_device(): outs = first_call(*pieces[k], *beside[k], *([] if k == 0 else [cost]))  10.1 us
    ppermute x9, starting transfers between devices, swap(): return lax.ppermute(x, axis, [(d, d ^ j) for d in range(n)])  7.14 us
    all_to_all x1, starting transfers between devices, on_device(): lax.all_to_all(placed, axis, split_axis=0, concat_axis=0, tiled=True)  6.91 us
    pallas_call x2, Pallas kernels, pack(): call(functools.partial(pack_kernel, groups[k], k == 0), [shape_of(sizes[k...  5.44 us
    ppermute x4, starting transfers between devices, swap_planes(): lax.ppermute(odd, axis, pairs_odd)  2.66 us
  transfers between devices with their start and end apart: 18, of which 8 were waited for; matrix products, arithmetic and copies ran while one was open for 0% of the time, Pallas kernels for 25%

profile of v6, /device:TPU:0, one launch (start us, length us, event | category | flops | bytes accessed | tf_op | source)
XLA Modules:
  0.0 93.4 jit_solution(6560155037966950849)
XLA Ops:
  0.6 3.0 %shard_map.79 = (f32[28,16,128]{2,1,0:T(8,128)S(1)}, f32[28,16,128]{2,1,0:T(8,128)S(1)}, f32[28,16,128]{2,1,0:T(8,128)S(1)}, f32[28,16,128]{2,1,0:T(8,128)S(1)}) custom-call(s32[4]{0:T(128)} %source_hbm.3, f32[4,16,4096]{2,1,0:T(8,128)} %start_hbm.3, f32[16,4096]{1,0:T(8,128)} %rest_0_.1, s32[16,4096]{1,0:T(8,128)} %rest_1_.1, s32[1,128]{1,0:T(1,128)} %bitcast.2, ...), custom_call_target="tpu_custom_call" | custom-call | bytes 6000000 | tf_op jit(solution)/shard_map/pallas_call | solution.py:519
  3.6 0.5 collective-permute-start.5
  4.2 2.6 %collective-permute-start.6 = (f32[28,16,128]{2,1,0:T(8,128)S(1)}, f32[28,16,128]{2,1,0:T(8,128)S(1)}, u32[]{:S(2)}, u32[]{:S(2)}) collective-permute-start(f32[28,16,128]{2,1,0:T(8,128)S(1)} %get-tuple-element.36), channel_id=1, source_target_pairs={{0,2},{1,3},{2,0},{3,1},{4,6},{5,7},{6,4},{7,5},{8,10},{9,11},{10,... | collective-permute-start | bytes 688136 | tf_op jit(solution)/shard_map/ppermute | solution.py:532
  6.8 6.4 %collective-permute-done.6.p2.refs_2_.m2 = f32[28,16,128]{2,1,0:T(8,128)S(1)} collective-permute-done((f32[28,16,128]{2,1,0:T(8,128)S(1)}, f32[28,16,128]{2,1,0:T(8,128)S(1)}, u32[]{:S(2)}, u32[]{:S(2)}) %collective-permute-start.6) | collective-permute-done | bytes 229408 | tf_op jit(solution)/shard_map/ppermute | solution.py:532
  13.2 4.4 %collective-permute-done.7.p3.refs_3_.m3 = f32[28,16,128]{2,1,0:T(8,128)S(1)} collective-permute-done((f32[28,16,128]{2,1,0:T(8,128)S(1)}, f32[28,16,128]{2,1,0:T(8,128)S(1)}, u32[]{:S(2)}, u32[]{:S(2)}) %collective-permute-start.7) | collective-permute-done | bytes 229408 | tf_op jit(solution)/shard_map/ppermute | solution.py:532
  17.6 0.6 shard_map.80
  18.3 1.6 %collective-permute-start.8 = (f32[27,16,128]{2,1,0:T(8,128)S(1)}, f32[27,16,128]{2,1,0:T(8,128)S(1)}, u32[]{:S(2)}, u32[]{:S(2)}) collective-permute-start(f32[27,16,128]{2,1,0:T(8,128)S(1)} %get-tuple-element.38), channel_id=1, source_target_pairs={{0,4},{1,5},{2,6},{3,7},{4,0},{5,1},{6,2},{7,3},{8,12},{9,13},{10,... | collective-permute-start | bytes 663560 | tf_op jit(solution)/shard_map/ppermute | solution.py:540
  19.8 0.7 collective-permute-start.9
  20.5 2.4 %shard_map.77 = (f32[18,16,128]{2,1,0:T(8,128)S(1)}, f32[18,16,128]{2,1,0:T(8,128)S(1)}, f32[18,16,128]{2,1,0:T(8,128)S(1)}, f32[18,16,128]{2,1,0:T(8,128)S(1)}) custom-call(s32[4]{0:T(128)} %source_hbm.3, f32[4,16,4096]{2,1,0:T(8,128)} %start_hbm.3), custom_call_target="tpu_custom_call" | custom-call | bytes 6000000 | tf_op jit(solution)/shard_map/pallas_call | solution.py:519
  23.1 1.5 %collective-permute-start.1 = (f32[18,16,128]{2,1,0:T(8,128)S(1)}, f32[18,16,128]{2,1,0:T(8,128)S(1)}, u32[]{:S(2)}, u32[]{:S(2)}) collective-permute-start(f32[18,16,128]{2,1,0:T(8,128)S(1)} %get-tuple-element.30), channel_id=1, source_target_pairs={{0,2},{1,3},{2,0},{3,1},{4,6},{5,7},{6,4},{7,5},{8,10},{9,11},{10,... | collective-permute-start | bytes 442376 | tf_op jit(solution)/shard_map/ppermute | solution.py:532
  24.9 4.9 %collective-permute-done.1.p2.refs_2_ = f32[18,16,128]{2,1,0:T(8,128)S(1)} collective-permute-done((f32[18,16,128]{2,1,0:T(8,128)S(1)}, f32[18,16,128]{2,1,0:T(8,128)S(1)}, u32[]{:S(2)}, u32[]{:S(2)}) %collective-permute-start.1) | collective-permute-done | bytes 147488 | tf_op jit(solution)/shard_map/ppermute | solution.py:532
  29.8 2.1 %collective-permute-done.2.p3.refs_3_ = f32[18,16,128]{2,1,0:T(8,128)S(1)} collective-permute-done((f32[18,16,128]{2,1,0:T(8,128)S(1)}, f32[18,16,128]{2,1,0:T(8,128)S(1)}, u32[]{:S(2)}, u32[]{:S(2)}) %collective-permute-start.2) | collective-permute-done | bytes 147488 | tf_op jit(solution)/shard_map/ppermute | solution.py:532
  31.9 0.4 shard_map.78
  32.4 4.4 %collective-permute-start.3 = (f32[18,16,128]{2,1,0:T(8,128)S(1)}, f32[18,16,128]{2,1,0:T(8,128)S(1)}, u32[]{:S(2)}, u32[]{:S(2)}) collective-permute-start(f32[18,16,128]{2,1,0:T(8,128)S(1)} %get-tuple-element.32), channel_id=1, source_target_pairs={{0,4},{1,5},{2,6},{3,7},{4,0},{5,1},{6,2},{7,3},{8,12},{9,13},{10,... | collective-permute-start | bytes 442376 | tf_op jit(solution)/shard_map/ppermute | solution.py:540
  36.8 0.7 collective-permute-start.4
  37.5 5.3 %shard_map.81 = (f32[27,64,128]{2,1,0:T(8,128)S(1)}, f32[27,32,128]{2,1,0:T(8,128)S(1)}, f32[27,32,128]{2,1,0:T(8,128)S(1)}, f32[3,9,120,128]{3,2,1,0:T(8,128)S(1)}) custom-call(f32[28,16,128]{2,1,0:T(8,128)S(1)} %get-tuple-element.34.p0.refs_0_.m0, f32[28,16,128]{2,1,0:T(8,128)S(1)} %collective-permute-done.5.p1.refs_1_.m1, ...), custom_call_target="tpu_custom_call" | custom-call | bytes 21000000 | tf_op jit(solution)/shard_map/pallas_call | solution.py:578
  42.8 1.3 %collective-permute-start.12 = (f32[27,32,128]{2,1,0:T(8,128)S(1)}, f32[27,32,128]{2,1,0:T(8,128)S(1)}, u32[]{:S(2)}, u32[]{:S(2)}) collective-permute-start(f32[27,32,128]{2,1,0:T(8,128)S(1)} %get-tuple-element.45), channel_id=1, source_target_pairs={{0,4},{1,5},{2,6},{3,7},{4,0},{5,1},{6,2},{7,3},{8,12},{9,13},{10,... | collective-permute-start | bytes 1327112 | tf_op jit(solution)/shard_map/ppermute | solution.py:540
  44.1 0.7 collective-permute-start.13
  44.8 4.9 %shard_map.82 = (f32[18,64,128]{2,1,0:T(8,128)S(1)}, f32[18,32,128]{2,1,0:T(8,128)S(1)}, f32[18,32,128]{2,1,0:T(8,128)S(1)}) custom-call(f32[18,16,128]{2,1,0:T(8,128)S(1)} %get-tuple-element.28.p0.refs_0_, f32[18,16,128]{2,1,0:T(8,128)S(1)} %collective-permute-done.p1.refs_1_, f32[18,16,128]{2,1,0:T(8,128)S(1)} %collective-permute-done.1.p2.refs_2_, ...), custom_call_target="tpu_custom_call" | custom-call | bytes 21000000 | tf_op jit(solution)/shard_map/pallas_call | solution.py:578
  49.7 3.3 %collective-permute-start.10 = (f32[18,32,128]{2,1,0:T(8,128)S(1)}, f32[18,32,128]{2,1,0:T(8,128)S(1)}, u32[]{:S(2)}, u32[]{:S(2)}) collective-permute-start(f32[18,32,128]{2,1,0:T(8,128)S(1)} %get-tuple-element.42), channel_id=1, source_target_pairs={{0,4},{1,5},{2,6},{3,7},{4,0},{5,1},{6,2},{7,3},{8,12},{9,13},{10,... | collective-permute-start | bytes 884744 | tf_op jit(solution)/shard_map/ppermute | solution.py:540
  53.0 0.7 collective-permute-start.11
  53.7 2.2 %collective-permute-done.12.even.base_even = f32[27,32,128]{2,1,0:T(8,128)S(1)} collective-permute-done((f32[27,32,128]{2,1,0:T(8,128)S(1)}, f32[27,32,128]{2,1,0:T(8,128)S(1)}, u32[]{:S(2)}, u32[]{:S(2)}) %collective-permute-start.12) | collective-permute-done | bytes 442400 | tf_op jit(solution)/shard_map/ppermute | solution.py:540
  55.9 9.9 %shard_map.83 = (f32[18,64,128]{2,1,0:T(8,128)S(1)}, f32[9,64,128]{2,1,0:T(8,128)S(1)}) custom-call(f32[27,64,128]{2,1,0:T(8,128)S(1)} %get-tuple-element.44.state.base, f32[27,32,128]{2,1,0:T(8,128)S(1)} %collective-permute-done.12.even.base_even, f32[27,32,128]{2,1,0:T(8,128)S(1)} %collective-permute-done.13.odd.base_odd, ...), custom_call_target="tpu_custom_call" | custom-call | bytes 45000000 | tf_op jit(solution)/shard_map/pallas_call | solution.py:595
  65.8 10.5 %shard_map.84 = (f32[18,64,128]{2,1,0:T(8,128)S(1)}, f32[8,16,128]{2,1,0:T(8,128)S(1)}, f32[8,16,128]{2,1,0:T(8,128)S(1)}, f32[8,16,128]{2,1,0:T(8,128)S(1)}, f32[8,16,128]{2,1,0:T(8,128)S(1)}) custom-call(f32[18,64,128]{2,1,0:T(8,128)S(1)} %get-tuple-element.41.state, f32[18,32,128]{2,1,0:T(8,128)S(1)} %collective-permute-done.10.even, ...), custom_call_target="tpu_custom_call" | custom-call | bytes 45000000 | tf_op jit(solution)/shard_map/pallas_call | solution.py:595
  76.3 2.5 %shard_map.85 = f32[16,4,256]{2,1,0:T(4,128)} custom-call(f32[18,64,128]{2,1,0:T(8,128)S(1)} %get-tuple-element.52.each_a, f32[18,64,128]{2,1,0:T(8,128)S(1)} %get-tuple-element.53.each_b, f32[28,16,128]{2,1,0:T(8,128)S(1)} %get-tuple-element.34.p0.refs_0_.m0, f32[28,16,128]{2,1,0:T(8,128)S(1)} %collective-permute-done.5.p1.refs_1_.m1, ...), custom_call_target="tpu_custom_call" | custom-call | bytes 12000000 | tf_op jit(solution)/shard_map/pallas_call | solution.py:618
  78.8 6.9 %all-to-all-start = ((f32[16,4,256]{2,1,0:T(4,128)}), f32[16,4,256]{2,1,0:T(4,128)S(1)}, u32[]{:S(2)}, u32[]{:S(2)}) async-start(f32[16,4,256]{2,1,0:T(4,128)} %shard_map.85), calls=%async_computation | async-start | bytes 131072 | tf_op jit(solution)/shard_map/all_to_all | solution.py:619
  85.7 0.4 collective-permute-start.14
  86.1 1.6 %collective-permute-start.15 = (f32[8,16,128]{2,1,0:T(8,128)S(1)}, f32[8,16,128]{2,1,0:T(8,128)S(1)}, u32[]{:S(2)}, u32[]{:S(2)}) collective-permute-start(f32[8,16,128]{2,1,0:T(8,128)S(1)} %get-tuple-element.50), channel_id=1, source_target_pairs={{0,2},{1,3},{2,0},{3,1},{4,6},{5,7},{6,4},{7,5},{8,10},{9,11},{10,... | collective-permute-start | bytes 196616 | tf_op jit(solution)/shard_map/ppermute | solution.py:532
  87.8 2.9 %collective-permute-done.15.r2 = f32[8,16,128]{2,1,0:T(8,128)S(1)} collective-permute-done((f32[8,16,128]{2,1,0:T(8,128)S(1)}, f32[8,16,128]{2,1,0:T(8,128)S(1)}, u32[]{:S(2)}, u32[]{:S(2)}) %collective-permute-start.15) | collective-permute-done | bytes 65568 | tf_op jit(solution)/shard_map/ppermute | solution.py:532
  90.7 1.4 %collective-permute-done.16.r3 = f32[8,16,128]{2,1,0:T(8,128)S(1)} collective-permute-done((f32[8,16,128]{2,1,0:T(8,128)S(1)}, f32[8,16,128]{2,1,0:T(8,128)S(1)}, u32[]{:S(2)}, u32[]{:S(2)}) %collective-permute-start.16) | collective-permute-done | bytes 65568 | tf_op jit(solution)/shard_map/ppermute | solution.py:532
  92.1 0.5 all-to-all-done.gauge_ref
  92.6 0.7 shard_map.86
  (14 shorter events, 0.5 us)
Async XLA Ops:
  3.6 3.2 %collective-permute-start.5 = (f32[28,16,128]{2,1,0:T(8,128)S(1)}, f32[28,16,128]{2,1,0:T(8,128)S(1)}, u32[]{:S(2)}, u32[]{:S(2)}) collective-permute-start(f32[28,16,128]{2,1,0:T(8,128)S(1)} %get-tuple-element.35), channel_id=1, source_target_pairs={{0,1},{1,0},{2,3},{3,2},{4,5},{5,4},{6,7},{7,6},{8,9},{9,8},{10,11... | collective-permute-start | bytes 688136 | tf_op jit(solution)/shard_map/ppermute | solution.py:532
  4.2 9.0 %collective-permute-start.6 = (f32[28,16,128]{2,1,0:T(8,128)S(1)}, f32[28,16,128]{2,1,0:T(8,128)S(1)}, u32[]{:S(2)}, u32[]{:S(2)}) collective-permute-start(f32[28,16,128]{2,1,0:T(8,128)S(1)} %get-tuple-element.36), channel_id=1, source_target_pairs={{0,2},{1,3},{2,0},{3,1},{4,6},{5,7},{6,4},{7,5},{8,10},{9,11},{10,... | collective-permute-start | bytes 688136 | tf_op jit(solution)/shard_map/ppermute | solution.py:532
  6.8 10.8 %collective-permute-start.7 = (f32[28,16,128]{2,1,0:T(8,128)S(1)}, f32[28,16,128]{2,1,0:T(8,128)S(1)}, u32[]{:S(2)}, u32[]{:S(2)}) collective-permute-start(f32[28,16,128]{2,1,0:T(8,128)S(1)} %get-tuple-element.37), channel_id=1, source_target_pairs={{0,3},{1,2},{2,1},{3,0},{4,7},{5,6},{6,5},{7,4},{8,11},{9,10},{10,... | collective-permute-start | bytes 688136 | tf_op jit(solution)/shard_map/ppermute | solution.py:532
  18.3 19.2 %collective-permute-start.8 = (f32[27,16,128]{2,1,0:T(8,128)S(1)}, f32[27,16,128]{2,1,0:T(8,128)S(1)}, u32[]{:S(2)}, u32[]{:S(2)}) collective-permute-start(f32[27,16,128]{2,1,0:T(8,128)S(1)} %get-tuple-element.38), channel_id=1, source_target_pairs={{0,4},{1,5},{2,6},{3,7},{4,0},{5,1},{6,2},{7,3},{8,12},{9,13},{10,... | collective-permute-start | bytes 663560 | tf_op jit(solution)/shard_map/ppermute | solution.py:540
  19.8 17.6 %collective-permute-start.9 = (f32[27,16,128]{2,1,0:T(8,128)S(1)}, f32[27,16,128]{2,1,0:T(8,128)S(1)}, u32[]{:S(2)}, u32[]{:S(2)}) collective-permute-start(f32[27,16,128]{2,1,0:T(8,128)S(1)} %get-tuple-element.39), channel_id=1, source_target_pairs={{4,8},{5,9},{6,10},{7,11},{8,4},{9,5},{10,6},{11,7},{20,24},{21,25... | collective-permute-start | bytes 663560 | tf_op jit(solution)/shard_map/ppermute | solution.py:540
  23.0 1.9 %collective-permute-start = (f32[18,16,128]{2,1,0:T(8,128)S(1)}, f32[18,16,128]{2,1,0:T(8,128)S(1)}, u32[]{:S(2)}, u32[]{:S(2)}) collective-permute-start(f32[18,16,128]{2,1,0:T(8,128)S(1)} %get-tuple-element.29), channel_id=1, source_target_pairs={{0,1},{1,0},{2,3},{3,2},{4,5},{5,4},{6,7},{7,6},{8,9},{9,8},{10,11... | collective-permute-start | bytes 442376 | tf_op jit(solution)/shard_map/ppermute | solution.py:532
  23.1 6.7 %collective-permute-start.1 = (f32[18,16,128]{2,1,0:T(8,128)S(1)}, f32[18,16,128]{2,1,0:T(8,128)S(1)}, u32[]{:S(2)}, u32[]{:S(2)}) collective-permute-start(f32[18,16,128]{2,1,0:T(8,128)S(1)} %get-tuple-element.30), channel_id=1, source_target_pairs={{0,2},{1,3},{2,0},{3,1},{4,6},{5,7},{6,4},{7,5},{8,10},{9,11},{10,... | collective-permute-start | bytes 442376 | tf_op jit(solution)/shard_map/ppermute | solution.py:532
  24.6 7.3 %collective-permute-start.2 = (f32[18,16,128]{2,1,0:T(8,128)S(1)}, f32[18,16,128]{2,1,0:T(8,128)S(1)}, u32[]{:S(2)}, u32[]{:S(2)}) collective-permute-start(f32[18,16,128]{2,1,0:T(8,128)S(1)} %get-tuple-element.31), channel_id=1, source_target_pairs={{0,3},{1,2},{2,1},{3,0},{4,7},{5,6},{6,5},{7,4},{8,11},{9,10},{10,... | collective-permute-start | bytes 442376 | tf_op jit(solution)/shard_map/ppermute | solution.py:532
  32.4 12.4 %collective-permute-start.3 = (f32[18,16,128]{2,1,0:T(8,128)S(1)}, f32[18,16,128]{2,1,0:T(8,128)S(1)}, u32[]{:S(2)}, u32[]{:S(2)}) collective-permute-start(f32[18,16,128]{2,1,0:T(8,128)S(1)} %get-tuple-element.32), channel_id=1, source_target_pairs={{0,4},{1,5},{2,6},{3,7},{4,0},{5,1},{6,2},{7,3},{8,12},{9,13},{10,... | collective-permute-start | bytes 442376 | tf_op jit(solution)/shard_map/ppermute | solution.py:540
  36.8 8.0 %collective-permute-start.4 = (f32[18,16,128]{2,1,0:T(8,128)S(1)}, f32[18,16,128]{2,1,0:T(8,128)S(1)}, u32[]{:S(2)}, u32[]{:S(2)}) collective-permute-start(f32[18,16,128]{2,1,0:T(8,128)S(1)} %get-tuple-element.33), channel_id=1, source_target_pairs={{4,8},{5,9},{6,10},{7,11},{8,4},{9,5},{10,6},{11,7},{20,24},{21,25... | collective-permute-start | bytes 442376 | tf_op jit(solution)/shard_map/ppermute | solution.py:540
  42.8 13.1 %collective-permute-start.12 = (f32[27,32,128]{2,1,0:T(8,128)S(1)}, f32[27,32,128]{2,1,0:T(8,128)S(1)}, u32[]{:S(2)}, u32[]{:S(2)}) collective-permute-start(f32[27,32,128]{2,1,0:T(8,128)S(1)} %get-tuple-element.45), channel_id=1, source_target_pairs={{0,4},{1,5},{2,6},{3,7},{4,0},{5,1},{6,2},{7,3},{8,12},{9,13},{10,... | collective-permute-start | bytes 1327112 | tf_op jit(solution)/shard_map/ppermute | solution.py:540
  44.1 11.8 %collective-permute-start.13 = (f32[27,32,128]{2,1,0:T(8,128)S(1)}, f32[27,32,128]{2,1,0:T(8,128)S(1)}, u32[]{:S(2)}, u32[]{:S(2)}) collective-permute-start(f32[27,32,128]{2,1,0:T(8,128)S(1)} %get-tuple-element.46), channel_id=1, source_target_pairs={{4,8},{5,9},{6,10},{7,11},{8,4},{9,5},{10,6},{11,7},{20,24},{21,25... | collective-permute-start | bytes 1327112 | tf_op jit(solution)/shard_map/ppermute | solution.py:540
  49.7 16.0 %collective-permute-start.10 = (f32[18,32,128]{2,1,0:T(8,128)S(1)}, f32[18,32,128]{2,1,0:T(8,128)S(1)}, u32[]{:S(2)}, u32[]{:S(2)}) collective-permute-start(f32[18,32,128]{2,1,0:T(8,128)S(1)} %get-tuple-element.42), channel_id=1, source_target_pairs={{0,4},{1,5},{2,6},{3,7},{4,0},{5,1},{6,2},{7,3},{8,12},{9,13},{10,... | collective-permute-start | bytes 884744 | tf_op jit(solution)/shard_map/ppermute | solution.py:540
  53.0 12.7 %collective-permute-start.11 = (f32[18,32,128]{2,1,0:T(8,128)S(1)}, f32[18,32,128]{2,1,0:T(8,128)S(1)}, u32[]{:S(2)}, u32[]{:S(2)}) collective-permute-start(f32[18,32,128]{2,1,0:T(8,128)S(1)} %get-tuple-element.43), channel_id=1, source_target_pairs={{4,8},{5,9},{6,10},{7,11},{8,4},{9,5},{10,6},{11,7},{20,24},{21,25... | collective-permute-start | bytes 884744 | tf_op jit(solution)/shard_map/ppermute | solution.py:540
  78.8 13.8 %all-to-all-start = ((f32[16,4,256]{2,1,0:T(4,128)}), f32[16,4,256]{2,1,0:T(4,128)S(1)}, u32[]{:S(2)}, u32[]{:S(2)}) async-start(f32[16,4,256]{2,1,0:T(4,128)} %shard_map.85), calls=%async_computation | async-start | bytes 131072 | tf_op jit(solution)/shard_map/all_to_all | solution.py:619
  85.7 2.0 %collective-permute-start.14 = (f32[8,16,128]{2,1,0:T(8,128)S(1)}, f32[8,16,128]{2,1,0:T(8,128)S(1)}, u32[]{:S(2)}, u32[]{:S(2)}) collective-permute-start(f32[8,16,128]{2,1,0:T(8,128)S(1)} %get-tuple-element.49), channel_id=1, source_target_pairs={{0,1},{1,0},{2,3},{3,2},{4,5},{5,4},{6,7},{7,6},{8,9},{9,8},{10,11... | collective-permute-start | bytes 196616 | tf_op jit(solution)/shard_map/ppermute | solution.py:532
  86.1 4.6 %collective-permute-start.15 = (f32[8,16,128]{2,1,0:T(8,128)S(1)}, f32[8,16,128]{2,1,0:T(8,128)S(1)}, u32[]{:S(2)}, u32[]{:S(2)}) collective-permute-start(f32[8,16,128]{2,1,0:T(8,128)S(1)} %get-tuple-element.50), channel_id=1, source_target_pairs={{0,2},{1,3},{2,0},{3,1},{4,6},{5,7},{6,4},{7,5},{8,10},{9,11},{10,... | collective-permute-start | bytes 196616 | tf_op jit(solution)/shard_map/ppermute | solution.py:532
  87.8 4.4 %collective-permute-start.16 = (f32[8,16,128]{2,1,0:T(8,128)S(1)}, f32[8,16,128]{2,1,0:T(8,128)S(1)}, u32[]{:S(2)}, u32[]{:S(2)}) collective-permute-start(f32[8,16,128]{2,1,0:T(8,128)S(1)} %get-tuple-element.51), channel_id=1, source_target_pairs={{0,3},{1,2},{2,1},{3,0},{4,7},{5,6},{6,5},{7,4},{8,11},{9,10},{10,... | collective-permute-start | bytes 196616 | tf_op jit(solution)/shard_map/ppermute | solution.py:532
